TPU v7x, 256 devices: a whole 4x4x8 slice. The times are simulated.
256 devices in a mesh: ctx: 32 (over y, x, core), tp: 8 (over z).
Axes of the slice: x: 4, y: 4, z: 8, core: 2. Of those that a mesh axis runs over, the one named last changes fastest.
Arguments:
- tokens: bfloat16 [8192, 8192], P('ctx', 'tp'), may hold values from -6 to 6
- frozen: bfloat16 [8192, 3, 8192], P('ctx', None, 'tp'), may hold values from -3 to 3
- cotangent: bfloat16 [8192, 8192], P('ctx', 'tp'), may hold values from -0.119628906 to 0.119628906
- adapter_down_weight: bfloat16 [16, 8192], P(None, 'tp'), may hold values from -0.0625 to 0.0625
- adapter_up_weight: bfloat16 [16, 3, 8192], P(None, None, 'tp'), may hold values from -0.75 to 0.75
- short_depthwise_filter: bfloat16 [3, 3, 8192], P(None, None, 'tp'), may hold values from -3.5 to 3.5
- long_group_filter: bfloat16 [512, 128], P('tp'), may hold values from -8 to 8
- skip_direct_scale: float32 [8192], P('tp'), may hold values from -3 to 3
- document_lengths: int32 [64], replicated, may hold values from 1 to 1024, 8192 in all
- window_row_position: int32 [8192], P('ctx'), may hold values from 0 to 8191, as said below
Outputs:
- mixer_out: bfloat16 [8192, 8192], P('ctx', 'tp')
- grad_down: float32 [16, 8192], P(None, 'tp')
- up_gradient: float32 [16, 3, 8192], P(None, None, 'tp')
- grad_short: float32 [3, 3, 8192], P(None, None, 'tp')
- grad_long: float32 [512, 128], P('tp')
- grad_skip: float32 [8192], P('tp')
Inputs may be any that keep to these rules, and one draw needn't show every extreme that they name: `window_row_position`: a permutation of the window's positions; the rows of one loader device (one index of ctx) go to each context shard (places j * 256 to (j + 1) * 256 - 1) in a count of 0, 8 or 16, and in a count of 16 to at least one shard. `document_lengths`: the documents lie end to end in the window in this order; the lengths sum to 8192.
All inputs are finite; a program needn't handle non-finite values.
Results may differ from a plain program's by a relative error of at most 0.0055.
The roundings to bfloat16 on the way count: a program that leaves them out, or rounds other values in their place, can miss the bound.
Values may be sent and summed in bfloat16 or wider, within the bound.
No kernel may reach another device: no remote copies, remote signals or barrier semaphores. Data moves between devices by JAX's collectives and lax.ppermute only.
A program may use at most 128 MiB of HBM per device.

v0:
```python
import jax
import jax.numpy as jnp
from jax import lax
from jax.experimental import pallas as pl
from jax.experimental.pallas import tpu as pltpu
from jax.sharding import PartitionSpec as P

BF = jnp.bfloat16
F32 = jnp.float32
I32 = jnp.int32


def whole(kernel, outs, scratch=(), flops=0, nbytes=0):
    def call(*args):
        return pl.pallas_call(
            kernel,
            out_shape=tuple(jax.ShapeDtypeStruct(s, d) for s, d in outs),
            in_specs=[pl.BlockSpec(memory_space=pltpu.VMEM)] * len(args),
            out_specs=tuple(pl.BlockSpec(memory_space=pltpu.VMEM) for _ in outs),
            scratch_shapes=list(scratch),
            compiler_params=pltpu.CompilerParams(vmem_limit_bytes=40 << 20),
            cost_estimate=pl.CostEstimate(flops=flops, bytes_accessed=nbytes, transcendentals=0),
        )(*args)

    return call


def dot(a, b, ca=1, cb=0):
    return lax.dot_general(a, b, (((ca,), (cb,)), ((), ())), preferred_element_type=F32)


def iota(shape, dim):
    return lax.broadcasted_iota(I32, shape, dim)


def send_kernel(pos_ref, tok_ref, frozen_ref, down_ref, out_ref, sel_ref):
    rows = pos_ref.shape[1]
    slots = sel_ref.shape[0]
    shards, cap, _ = out_ref.shape
    pos = pos_ref[...]
    dest = (pos // rows).astype(F32)
    within = (pos % rows).astype(F32)
    dest_row = jnp.broadcast_to(dest, (rows, rows))
    dest_col = dest_row.T
    earlier = (dest_row == dest_col) & (iota((rows, rows), 0) < iota((rows, rows), 1))
    rank = jnp.sum(jnp.where(earlier, 1.0, 0.0), axis=0, keepdims=True)
    slot = dest * cap + rank
    sel = jnp.where(
        iota((slots, rows), 0).astype(F32) == jnp.broadcast_to(slot, (slots, rows)), 1.0, 0.0
    ).astype(BF)
    sel_ref[...] = sel
    down = down_ref[...]
    rank_dim = down.shape[0]
    down3 = jnp.concatenate([down, down, down, jnp.zeros((128 - 3 * rank_dim, down.shape[1]), BF)])
    low = dot(tok_ref[...], down3, 1, 1)
    high = low.astype(BF).astype(F32)
    rest = low - high
    mid = rest.astype(BF).astype(F32)
    tail = rest - mid
    lane = iota((rows, 128), 1)
    within_col = jnp.broadcast_to(within, (128, rows)).T
    extra = jnp.where(
        lane < rank_dim,
        high,
        jnp.where(
            lane < 2 * rank_dim,
            mid,
            jnp.where(
                lane < 3 * rank_dim,
                tail,
                jnp.where(lane == 48, within_col, jnp.where(lane == 49, 1.0, 0.0)),
            ),
        ),
    )
    parts, _, chans = frozen_ref.shape
    out_ref[:, :, parts * chans :] = (
        dot(sel, extra.astype(BF)).astype(BF).reshape(shards, cap, 128)
    )
    for a in range(parts):
        for c in range(0, chans, 256):
            out_ref[:, :, a * chans + c : a * chans + c + 256] = (
                dot(sel, frozen_ref[a, :, c : c + 256]).astype(BF).reshape(shards, cap, 256)
            )


def send_tokens_kernel(sel_ref, tok_ref, out_ref):
    shards, cap, chans = out_ref.shape
    for c in range(0, chans, 256):
        out_ref[:, :, c : c + 256] = (
            dot(sel_ref[...], tok_ref[:, c : c + 256]).astype(BF).reshape(shards, cap, 256)
        )


def place_kernel(got_ref, place_ref, low_ref):
    shards, cap, width = got_ref.shape
    slots = shards * cap
    copies, rank_dim, rows = low_ref.shape
    extra = got_ref[:, :, width - 128 :].reshape(slots, 128)
    target = jnp.where(extra[:, 49:50].astype(F32) > 0.5, extra[:, 48:49].astype(F32), -1.0)
    place_t = jnp.where(
        jnp.broadcast_to(target, (slots, rows)) == iota((slots, rows), 1).astype(F32), 1.0, 0.0
    )
    place = place_t.T.astype(BF)
    place_ref[...] = place
    split = dot(place, extra)
    split_t = split.T
    low = split_t[:rank_dim] + split_t[rank_dim : 2 * rank_dim] + split_t[2 * rank_dim : 3 * rank_dim]
    for t in range(copies):
        low_ref[t] = low


def pack_kernel(got_ref, place_ref, out_ref):
    shards, cap, width = got_ref.shape
    parts, rows, chans = out_ref.shape
    place = place_ref[...]
    for a in range(parts):
        for c in range(0, chans, 256):
            block = got_ref[:, :, a * chans + c : a * chans + c + 256].reshape(shards * cap, 256)
            out_ref[a, :, c : c + 256] = dot(place, block).astype(BF)


def pre_kernel(packed_ref, lows_ref, up_ref, pre_ref, edge_ref, low_ref):
    parts, rows, chans = packed_ref.shape
    total = lows_ref[0]
    for t in range(1, lows_ref.shape[0]):
        total = total + lows_ref[t]
    low = total.astype(BF)
    low_ref[...] = low
    low_t = total.T.astype(BF)
    edge_ref[...] = jnp.zeros_like(edge_ref)
    for a in range(parts):
        for c in range(0, chans, 256):
            cols = slice(c, c + 256)
            value = packed_ref[a, :, cols].astype(F32) + dot(low_t, up_ref[a, :, cols])
            pre_ref[a, :, cols] = value.astype(BF)
            edge_ref[2 * a : 2 * a + 2, cols] = value[rows - 2 :]


def shifted_down(value, edge0, edge1):
    row = iota(value.shape, 0)
    one = jnp.where(row == 0, edge1, pltpu.roll(value, 1, 0))
    two = jnp.where(row == 0, edge0, jnp.where(row == 1, edge1, pltpu.roll(value, 2, 0)))
    return one, two


def post_kernel(pre_ref, edge_ref, taps_ref, off_ref, cot_ref, post_ref, x_ref, b_ref, xe_ref, be_ref):
    parts, rows, chans = pre_ref.shape
    mask1 = jnp.where(off_ref[:rows] >= 1.0, 1.0, 0.0)
    mask2 = jnp.where(off_ref[:rows] >= 2.0, 1.0, 0.0)

    def chunk(i, carry):
        cols = pl.ds(pl.multiple_of(i * 128, 128), 128)
        made = []
        for a in range(parts):
            value = pre_ref[a, :, cols].astype(F32)
            one, two = shifted_down(
                value, edge_ref[2 * a : 2 * a + 1, cols], edge_ref[2 * a + 1 : 2 * a + 2, cols]
            )
            total = (
                taps_ref[a : a + 1, cols] * value
                + taps_ref[parts + a : parts + a + 1, cols] * one * mask1
                + taps_ref[2 * parts + a : 2 * parts + a + 1, cols] * two * mask2
            ).astype(BF)
            post_ref[a, :, cols] = total
            made.append(total.astype(F32))
        product = (made[1] * made[2]).astype(BF)
        back = (cot_ref[:, cols].astype(F32) * made[0]).astype(BF)
        x_ref[:, cols] = product
        b_ref[:, cols] = back
        xe_ref[:, cols] = product[rows - 128 :]
        be_ref[:, cols] = back[:128]
        return carry

    lax.fori_loop(0, chans // 128, chunk, 0)


def conv_kernel(
    x_ref, xh_ref, b_ref, bh_ref, post_ref, cot_ref, skip_ref, filt_ref, offc_ref, offr_ref,
    mixer_ref, backpost_ref, edge_ref, long_ref, gskip_ref,
    mfwd_ref, madj_ref, mpair_ref, frow_ref, grow_ref, fwd_ref, adj_ref, lhs_ref, bm_ref, rf_ref, ra_ref, rp_ref,
):
    rows, chans = x_ref.shape
    blocks = rows // 128
    sub, lane = iota((128, 128), 0), iota((128, 128), 1)
    turn = jnp.where(sub + lane == 127, 1.0, 0.0).astype(BF)
    for b in range(blocks):
        first = 128 * b
        begin_col = (first + sub).astype(F32) - offc_ref[first : first + 128]
        own = (lane <= sub) & ((first + lane).astype(F32) >= begin_col)
        prev = (lane > sub) & ((first - 128 + lane).astype(F32) >= begin_col)
        prev, own = jnp.where(prev, 1.0, 0.0), jnp.where(own, 1.0, 0.0)
        mfwd_ref[b, :, :128] = prev.astype(BF)
        mfwd_ref[b, :, 128:] = own.astype(BF)
        mpair_ref[b, :, :128] = dot(turn, prev.astype(BF))
        mpair_ref[b, :, 128:] = dot(turn, own.astype(BF))
        row0 = jnp.broadcast_to(offr_ref[:, first : first + 128], (128, 128))
        row1 = jnp.broadcast_to(offr_ref[:, first + 128 : first + 256], (128, 128))
        begin0 = (first + lane).astype(F32) - row0
        begin1 = (first + 128 + lane).astype(F32) - row1
        at = (first + sub).astype(F32)
        same = (sub <= lane) & (at >= begin0)
        after = (lane < sub) & (at >= begin1)
        madj_ref[b, :, :128] = jnp.where(same, 1.0, 0.0).astype(BF)
        madj_ref[b, :, 128:] = jnp.where(after, 1.0, 0.0).astype(BF)
    filt = filt_ref[...]
    flip = jnp.where((sub + lane) % 128 == 0, 1.0, 0.0).astype(BF)
    frow_ref[...] = filt.astype(F32)
    grow_ref[...] = dot(filt, flip)

    def chunk(i, carry):
        cols = pl.ds(pl.multiple_of(i * 128, 128), 128)
        for g in range(8):
            f_row = jnp.broadcast_to(frow_ref[pl.ds(i * 8 + g, 1), :], (128, 128))
            g_row = jnp.broadcast_to(grow_ref[pl.ds(i * 8 + g, 1), :], (128, 128))
            circ = pltpu.roll(f_row, 0, 1, stride=1, stride_axis=0).astype(BF)
            circ_t = pltpu.roll(g_row, 0, 1, stride=1, stride_axis=0).astype(BF)
            two, two_t = jnp.concatenate([circ, circ], 1), jnp.concatenate([circ_t, circ_t], 1)
            for b in range(blocks):
                fwd_ref[b, 128 * g : 128 * g + 128] = two_t * mfwd_ref[b]
                adj_ref[b, 128 * g : 128 * g + 128] = two * madj_ref[b]
        x_win = jnp.concatenate([xh_ref[:, cols], x_ref[:, cols]])
        b_win = jnp.concatenate([b_ref[:, cols], bh_ref[:, cols]])
        lane_group = lane // 16
        for b in range(blocks):
            xw = x_win[128 * b : 128 * b + 256]
            rf_ref[b] = dot(fwd_ref[b], xw)
            ra_ref[b] = dot(adj_ref[b], b_win[128 * b : 128 * b + 256])
            back = dot(turn, b_win[128 * b : 128 * b + 128])
            for g in range(8):
                lhs_ref[128 * g : 128 * g + 128] = jnp.where(lane_group == g, back, 0.0).astype(BF)
            rp_ref[b] = dot(lhs_ref[...], xw, 1, 1)
        for g in range(8):
            part = jnp.zeros((128, 128), F32)
            for b in range(blocks):
                pair = rp_ref[b, 128 * g : 128 * g + 128] * mpair_ref[b]
                part = part + pair[:, :128] + pair[:, 128:]
            part = pltpu.roll(part, 0, 1, stride=1, stride_axis=0)
            long_ref[pl.ds(i * 8 + g, 1), :] = jnp.sum(part, axis=0, keepdims=True)
        skip = skip_ref[:, cols]
        gsum = jnp.zeros((1, 128), F32)
        for b in range(blocks):
            conv = jnp.zeros((128, 128), F32)
            adj = jnp.zeros((128, 128), F32)
            for g in range(8):
                conv = jnp.where(lane_group == g, rf_ref[b, 128 * g : 128 * g + 128], conv)
                adj = jnp.where(lane_group == g, ra_ref[b, 128 * g : 128 * g + 128], adj)
            at = slice(128 * b, 128 * b + 128)
            query, key, value = (post_ref[a, at, cols].astype(F32) for a in range(3))
            product = x_ref[at, cols].astype(F32)
            grad = cot_ref[at, cols].astype(F32)
            direct = conv + skip * product
            mixer_ref[at, cols] = (query * direct).astype(BF)
            gated = grad * query
            back = adj + skip * gated
            gsum = gsum + jnp.sum(gated * product, axis=0, keepdims=True)
            for a, post in enumerate((grad * direct, back * value, back * key)):
                post = post.astype(BF)
                backpost_ref[a, at, cols] = post
                if b == 0:
                    edge_ref[2 * a : 2 * a + 2, cols] = post[:2].astype(F32)
        gskip_ref[:, cols] = gsum
        return carry

    edge_ref[...] = jnp.zeros_like(edge_ref)
    lax.fori_loop(0, chans // 128, chunk, 0)


def back_kernel(
    backpost_ref, nedge_ref, pre_ref, pedge_ref, taps_ref, off_ref, low_ref, up_ref,
    upgrad_ref, short_ref, backlow_ref,
):
    parts, rows, chans = pre_ref.shape
    rank_dim = low_ref.shape[0]
    mask1 = jnp.where(off_ref[:rows] >= 1.0, 1.0, 0.0)
    mask2 = jnp.where(off_ref[:rows] >= 2.0, 1.0, 0.0)
    next1 = jnp.where(off_ref[rows : rows + 8] >= 1.0, 1.0, 0.0)
    next2 = jnp.where(off_ref[rows : rows + 8] >= 2.0, 1.0, 0.0)
    low = low_ref[...]
    row = iota((rows, 128), 0)

    def chunk(i, total):
        cols = pl.ds(pl.multiple_of(i * 128, 128), 128)
        for a in range(parts):
            post = backpost_ref[a, :, cols].astype(F32)
            edge0 = nedge_ref[2 * a : 2 * a + 1, cols]
            edge1 = nedge_ref[2 * a + 1 : 2 * a + 2, cols]
            post1, post2 = post * mask1, post * mask2
            up1 = jnp.where(row == rows - 1, edge0 * next1[0:1], pltpu.roll(post1, rows - 1, 0))
            up2 = jnp.where(
                row == rows - 2,
                edge0 * next2[0:1],
                jnp.where(row == rows - 1, edge1 * next2[1:2], pltpu.roll(post2, rows - 2, 0)),
            )
            back_pre = (
                taps_ref[a : a + 1, cols] * post
                + taps_ref[parts + a : parts + a + 1, cols] * up1
                + taps_ref[2 * parts + a : 2 * parts + a + 1, cols] * up2
            ).astype(BF)
            pre = pre_ref[a, :, cols].astype(F32)
            one, two = shifted_down(
                pre, pedge_ref[2 * a : 2 * a + 1, cols], pedge_ref[2 * a + 1 : 2 * a + 2, cols]
            )
            short_ref[a : a + 1, cols] = jnp.sum(post * pre, axis=0, keepdims=True)
            short_ref[parts + a : parts + a + 1, cols] = jnp.sum(post1 * one, axis=0, keepdims=True)
            short_ref[2 * parts + a : 2 * parts + a + 1, cols] = jnp.sum(
                post2 * two, axis=0, keepdims=True
            )
            upgrad_ref[a, :, cols] = dot(low, back_pre)
            total = total + dot(up_ref[a, :, cols], back_pre, 1, 1)
        return total

    short_ref[...] = jnp.zeros_like(short_ref)
    total = lax.fori_loop(0, chans // 128, chunk, jnp.zeros((rank_dim, rows), F32))
    for t in range(backlow_ref.shape[0]):
        backlow_ref[t] = total


def gather_kernel(lows_ref, got_ref, place_ref, upgrad_ref, short_ref, gskip_ref, long_ref, out_ref):
    shards, cap, chans = got_ref.shape
    total = lows_ref[0]
    for t in range(1, lows_ref.shape[0]):
        total = total + lows_ref[t]
    low = total.astype(BF)
    placed = dot(low, place_ref[...]).astype(BF)
    tiles = chans // 128
    for i in range(tiles):
        cols = slice(128 * i, 128 * i + 128)
        down = dot(placed, got_ref[:, :, cols].reshape(shards * cap, 128))
        up = [upgrad_ref[a, :, cols] for a in range(3)]
        out_ref[i, :16] = down
        out_ref[i, 16:24] = up[0][:8]
        out_ref[tiles + i, :8] = up[0][8:]
        out_ref[tiles + i, 8:24] = up[1]
        out_ref[2 * tiles + i, :16] = up[2]
        out_ref[2 * tiles + i, 16:24] = short_ref[:8, cols]
        out_ref[3 * tiles + i, :8] = jnp.where(
            iota((8, 128), 0) == 0,
            jnp.broadcast_to(short_ref[8:9, cols], (8, 128)),
            jnp.broadcast_to(gskip_ref[:, cols], (8, 128)),
        )
        out_ref[3 * tiles + i, 8:16] = long_ref[8 * i : 8 * i + 8]
        out_ref[3 * tiles + i, 16:24] = jnp.zeros((8, 128), F32)


def sum_kernel(in_ref, out_ref):
    total = in_ref[0]
    for t in range(1, in_ref.shape[0]):
        total = total + in_ref[t]
    for t in range(out_ref.shape[0]):
        out_ref[t] = total


def spread_kernel(in_ref, down_ref, up_ref, short_ref, long_ref, gskip_ref):
    tiles = down_ref.shape[1] // 128
    flip = jnp.where(iota((128, 128), 0) + iota((128, 128), 1) == 127, 1.0, 0.0)
    for i in range(tiles):
        cols = slice(128 * i, 128 * i + 128)
        down_ref[:, cols] = in_ref[i, :16]
        up_ref[0, :8, cols] = in_ref[i, 16:24]
        up_ref[0, 8:, cols] = in_ref[tiles + i, :8]
        up_ref[1, :, cols] = in_ref[tiles + i, 8:24]
        up_ref[2, :, cols] = in_ref[2 * tiles + i, :16]
        short_ref[:8, cols] = in_ref[2 * tiles + i, 16:24]
        short_ref[8:9, cols] = in_ref[3 * tiles + i, 0:1]
        gskip_ref[:, cols] = in_ref[3 * tiles + i, 1:2]
        long_ref[8 * i : 8 * i + 8] = lax.dot_general(
            in_ref[3 * tiles + i, 8:16],
            flip,
            (((1,), (0,)), ((), ())),
            precision=lax.Precision.HIGHEST,
            preferred_element_type=F32,
        )


def swap(value, axis):
    return lax.all_to_all(value, axis, split_axis=0, concat_axis=0, tiled=True)


def neighbour(value, steps):
    count = lax.axis_size("ctx")
    pairs = [(i, i + steps) for i in range(count) if 0 <= i + steps < count]
    return lax.ppermute(value, "ctx", pairs)


def doc_offsets(positions, lengths):
    index = jnp.arange(lengths.shape[0], dtype=I32)
    starts = jnp.sum(jnp.where(index[None, :] < index[:, None], lengths[None, :], 0), axis=1)
    begins = jnp.max(jnp.where(starts[None, :] <= positions[:, None], starts[None, :], 0), axis=1)
    return positions - begins


def on_device(
    tokens,
    frozen,
    cotangent,
    adapter_down_weight,
    adapter_up_weight,
    short_depthwise_filter,
    long_group_filter,
    skip_direct_scale,
    document_lengths,
    window_row_position,
):
    rows, chans = tokens.shape
    parts = frozen.shape[1]
    rank_dim = adapter_down_weight.shape[0]
    taps = short_depthwise_filter.shape[0]
    groups = long_group_filter.shape[0]
    shards = lax.axis_size("ctx")
    columns = lax.axis_size("tp")
    cap = 2 * rows // shards
    slots = shards * cap
    frozen = frozen.transpose(1, 0, 2)
    up = adapter_up_weight.transpose(1, 0, 2)
    send, sel = whole(
        send_kernel,
        [((shards, cap, parts * chans + 128), BF), ((slots, rows), BF)],
        flops=2 * slots * rows * parts * chans,
        nbytes=5 << 20,
    )(window_row_position.reshape(1, rows), tokens, frozen, adapter_down_weight)
    got = swap(send, "ctx")

    send, sel, document_lengths, short_depthwise_filter = lax.optimization_barrier(
        (send, sel, document_lengths, short_depthwise_filter)
    )
    (send_tok,) = whole(
        send_tokens_kernel, [((shards, cap, chans), BF)], flops=2 * slots * rows * chans, nbytes=2 << 20
    )(sel, tokens)
    first = lax.axis_index("ctx") * rows
    offsets = doc_offsets(first + jnp.arange(rows + 128, dtype=I32), document_lengths).astype(F32)
    off_row = offsets.reshape(1, rows + 128)
    off_col = jnp.broadcast_to(offsets[:, None], (rows + 128, 128))
    tap_rows = short_depthwise_filter.reshape(taps * parts, chans).astype(F32)
    tap_rows = jnp.pad(tap_rows, ((0, 16 - taps * parts), (0, 0)))
    skip_row = skip_direct_scale.reshape(1, chans)

    place, low_part = whole(
        place_kernel, [((rows, slots), BF), ((columns, rank_dim, rows), F32)], flops=1 << 26, nbytes=1 << 20
    )(got)
    lows = swap(low_part, "tp")
    (packed,) = whole(
        pack_kernel, [((parts, rows, chans), BF)], flops=2 * slots * rows * parts * chans, nbytes=5 << 20
    )(got, place)
    pre, pre_edge, low = whole(
        pre_kernel,
        [((parts, rows, chans), BF), ((8, chans), F32), ((rank_dim, rows), BF)],
        flops=1 << 27,
        nbytes=4 << 20,
    )(packed, lows, up)
    send_tok, low = lax.optimization_barrier((send_tok, low))
    edge_in = neighbour(pre_edge, 1)
    post, x, back, x_tail, b_head = whole(
        post_kernel,
        [
            ((parts, rows, chans), BF),
            ((rows, chans), BF),
            ((rows, chans), BF),
            ((128, chans), BF),
            ((128, chans), BF),
        ],
        flops=1 << 25,
        nbytes=6 << 20,
    )(pre, edge_in, tap_rows, off_col, cotangent)
    got_tok = swap(send_tok, "ctx")
    x_halo = neighbour(x_tail, 1)
    b_halo = neighbour(b_head, -1)
    blocks = rows // 128
    mixer, back_post, post_edge, long_part, skip_part = whole(
        conv_kernel,
        [
            ((rows, chans), BF),
            ((parts, rows, chans), BF),
            ((8, chans), F32),
            ((groups, 128), F32),
            ((1, chans), F32),
        ],
        scratch=[
            pltpu.VMEM((blocks, 128, 256), BF),
            pltpu.VMEM((blocks, 128, 256), BF),
            pltpu.VMEM((blocks, 128, 256), F32),
            pltpu.VMEM((groups, 128), F32),
            pltpu.VMEM((groups, 128), F32),
            pltpu.VMEM((blocks, 1024, 256), BF),
            pltpu.VMEM((blocks, 1024, 256), BF),
            pltpu.VMEM((1024, 128), BF),
            pltpu.VMEM((8, 128), F32),
            pltpu.VMEM((blocks, 1024, 128), F32),
            pltpu.VMEM((blocks, 1024, 128), F32),
            pltpu.VMEM((blocks, 1024, 256), F32),
        ],
        flops=10 << 30,
        nbytes=8 << 20,
    )(x, x_halo, back, b_halo, post, cotangent, skip_row, long_group_filter, off_col, off_row)
    got_tok, post_edge = lax.optimization_barrier((got_tok, post_edge))
    edge_next = neighbour(post_edge, -1)
    up_part, short_part, back_low_part = whole(
        back_kernel,
        [
            ((parts, rank_dim, chans), F32),
            ((16, chans), F32),
            ((columns, rank_dim, rows), F32),
        ],
        flops=1 << 27,
        nbytes=6 << 20,
    )(back_post, edge_next, pre, edge_in, tap_rows, off_col, low, up)
    back_lows = swap(back_low_part, "tp")
    (pieces,) = whole(
        gather_kernel, [((shards, 24, 128), F32)], flops=1 << 26, nbytes=2 << 20
    )(back_lows, got_tok, place, up_part, short_part, skip_part, long_part)
    pieces = swap(pieces, "ctx")
    (pieces,) = whole(sum_kernel, [((shards, 24, 128), F32)], flops=1 << 20, nbytes=1 << 20)(pieces)
    pieces = swap(pieces, "ctx")
    grad_down, up_gradient, grad_short, grad_long, grad_skip = whole(
        spread_kernel,
        [
            ((rank_dim, chans), F32),
            ((parts, rank_dim, chans), F32),
            ((taps * parts, chans), F32),
            ((groups, 128), F32),
            ((1, chans), F32),
        ],
        flops=1 << 20,
        nbytes=1 << 20,
    )(pieces)
    return (
        mixer,
        grad_down,
        up_gradient.transpose(1, 0, 2),
        grad_short.reshape(taps, parts, chans),
        grad_long,
        grad_skip.reshape(chans),
    )


def solution(mesh):
    placed = (
        P("ctx", "tp"),
        P("ctx", None, "tp"),
        P("ctx", "tp"),
        P(None, "tp"),
        P(None, None, "tp"),
        P(None, None, "tp"),
        P("tp", None),
        P("tp"),
        P(),
        P("ctx"),
    )
    return jax.shard_map(
        on_device,
        mesh=mesh,
        in_specs=placed,
        out_specs=(
            P("ctx", "tp"),
            P(None, "tp"),
            P(None, None, "tp"),
            P(None, None, "tp"),
            P("tp", None),
            P("tp"),
        ),
        check_vma=False,
    )
```

profile of v0, /device:TPU:1, one launch (start us, length us, event | category | flops | bytes accessed | tf_op | source)
XLA Modules:
  0.0 179.8 jit_solution(2695465775970838299)
XLA Ops:
  0.6 1.0 copy-done.5
  1.7 1.4 copy-done.14
  3.1 0.8 copy-done.21
  3.8 0.7 copy-done.24
  4.5 1.4 shard_map.145
  6.0 1.6 copy-done.2
  7.6 0.7 copy-done.11
  8.3 8.7 %all-to-all-start = ((bf16[32,16,3200]{2,1,0:T(8,128)(2,1)}), bf16[32,16,3200]{2,1,0:T(8,128)(2,1)S(1)}, u32[]{:S(2)}, u32[]{:S(2)}) async-start(bf16[32,16,3200]{2,1,0:T(8,128)(2,1)} %copy-done.2), calls=%async_computation | async-start | bytes 6553600 | tf_op jit(solution)/shard_map/all_to_all | solution.py:376
  17.0 0.6 convert_element_type.22
  17.7 0.1 select_reduce_fusion.1
  17.8 0.1 select_reduce_fusion
  17.9 40.3 %all-to-all-done.got_ref = bf16[32,16,3200]{2,1,0:T(8,128)(2,1)S(1)} async-done(((bf16[32,16,3200]{2,1,0:T(8,128)(2,1)}), bf16[32,16,3200]{2,1,0:T(8,128)(2,1)S(1)}, u32[]{:S(2)}, u32[]{:S(2)}) %all-to-all-start) | async-done | bytes 3276832 | tf_op jit(solution)/shard_map/all_to_all | solution.py:376
  58.2 0.5 shard_map.146
  58.7 0.0 copy-start.13
  58.7 0.7 copy-done.13
  59.3 8.2 %all-to-all-start.1 = ((f32[8,16,256]{2,1,0:T(8,128)}), f32[8,16,256]{2,1,0:T(8,128)}, u32[]{:S(2)}, u32[]{:S(2)}) async-start(f32[8,16,256]{2,1,0:T(8,128)} %copy-done.13), calls=%async_computation.1 | async-start | bytes 262144 | tf_op jit(solution)/shard_map/all_to_all | solution.py:376
  67.5 1.0 shard_map.147.packed_ref
  68.5 1.2 copy-done
  69.7 5.9 %all-to-all-done.1.lows_ref = f32[8,16,256]{2,1,0:T(8,128)} async-done(((f32[8,16,256]{2,1,0:T(8,128)}), f32[8,16,256]{2,1,0:T(8,128)}, u32[]{:S(2)}, u32[]{:S(2)}) %all-to-all-start.1) | async-done | bytes 131104 | tf_op jit(solution)/shard_map/all_to_all | solution.py:376
  75.6 1.4 copy-done.1
  77.0 0.9 copy-done.9
  77.9 1.6 shard_map.148
  79.5 5.3 %collective-permute-start = (f32[8,1024]{1,0:T(8,128)S(1)}, f32[8,1024]{1,0:T(8,128)S(1)}, u32[]{:S(2)}, u32[]{:S(2)}) collective-permute-start(f32[8,1024]{1,0:T(8,128)S(1)} %get-tuple-element.42), channel_id=1, source_target_pairs={{0,8},{8,16},{16,24},{24,32},{32,40},{40,48},{48,56},{56,64},{64,7... | collective-permute-start | bytes 98312 | tf_op jit(solution)/shard_map/ppermute | solution.py:382
  84.8 1.0 collective-permute-done.edge_ref.pedge_ref
  85.8 0.1 broadcast_in_dim.37.off_ref.offc_ref
  85.9 2.8 %shard_map.149 = (bf16[3,256,1024]{2,1,0:T(8,128)(2,1)S(1)}, bf16[256,1024]{1,0:T(8,128)(2,1)S(1)}, bf16[256,1024]{1,0:T(8,128)(2,1)S(1)}, bf16[128,1024]{1,0:T(8,128)(2,1)}, bf16[128,1024]{1,0:T(8,128)(2,1)}) custom-call(bf16[3,256,1024]{2,1,0:T(8,128)(2,1)S(1)} %get-tuple-element.41.pre_ref, f32[8,1024]{1,0:T(8,128)S(1)} %collective-permute-done.edge_ref.pedge_ref, ...), custom_call_target="tpu_custom_call" | custom-call | flops 33554432 | bytes 6291456 | tf_op jit(solution)/shard_map/pallas_call | solution.py:15
  88.6 1.2 copy-done.15
  89.8 4.2 %collective-permute-start.1 = (bf16[128,1024]{1,0:T(8,128)(2,1)}, bf16[128,1024]{1,0:T(8,128)(2,1)}, u32[]{:S(2)}, u32[]{:S(2)}) collective-permute-start(bf16[128,1024]{1,0:T(8,128)(2,1)} %get-tuple-element.47), channel_id=1, source_target_pairs={{0,8},{8,16},{16,24},{24,32},{32,40},{40,48},{48,56},{56,64},{64,7... | collective-permute-start | bytes 786440 | tf_op jit(solution)/shard_map/ppermute | solution.py:382
  94.1 1.9 %collective-permute-start.2 = (bf16[128,1024]{1,0:T(8,128)(2,1)}, bf16[128,1024]{1,0:T(8,128)(2,1)}, u32[]{:S(2)}, u32[]{:S(2)}) collective-permute-start(bf16[128,1024]{1,0:T(8,128)(2,1)} %get-tuple-element.49), channel_id=1, source_target_pairs={{8,0},{16,8},{24,16},{32,24},{40,32},{48,40},{56,48},{64,56},{72,6... | collective-permute-start | bytes 786440 | tf_op jit(solution)/shard_map/ppermute | solution.py:382
  96.0 1.4 shard_map.151
  97.4 9.1 %all-to-all-start.2 = ((bf16[32,16,1024]{2,1,0:T(8,128)(2,1)}), bf16[32,16,1024]{2,1,0:T(8,128)(2,1)S(1)}, u32[]{:S(2)}, u32[]{:S(2)}) async-start(bf16[32,16,1024]{2,1,0:T(8,128)(2,1)} %shard_map.151), calls=%async_computation.2 | async-start | bytes 2097152 | tf_op jit(solution)/shard_map/all_to_all | solution.py:376
  106.6 1.0 copy-done.8
  107.6 1.4 copy-done.16
  109.1 1.0 copy-done.18
  110.1 1.0 copy-done.20
  111.1 12.0 %shard_map.150 = (bf16[256,1024]{1,0:T(8,128)(2,1)}, bf16[3,256,1024]{2,1,0:T(8,128)(2,1)S(1)}, f32[8,1024]{1,0:T(8,128)S(1)}, f32[64,128]{1,0:T(8,128)S(1)}, f32[1,1024]{1,0:T(1,128)S(1)}) custom-call(bf16[256,1024]{1,0:T(8,128)(2,1)S(1)} %copy-done.18, bf16[128,1024]{1,0:T(8,128)(2,1)} %collective-permute-done.1.xh_ref, bf16[256,1024]{1,0:T(8,128)(2,1)S(1)} %copy-done.20, ...), custom_call_target="tpu_custom_call" | custom-call | flops 10737418240 | bytes 8388608 | tf_op jit(solution)/shard_map/pallas_call | solution.py:15
  123.2 1.2 copy-done.3
  124.3 2.1 %collective-permute-start.3 = (f32[8,1024]{1,0:T(8,128)S(1)}, f32[8,1024]{1,0:T(8,128)S(1)}, u32[]{:S(2)}, u32[]{:S(2)}) collective-permute-start(f32[8,1024]{1,0:T(8,128)S(1)} %get-tuple-element.57), channel_id=1, source_target_pairs={{8,0},{16,8},{24,16},{32,24},{40,32},{48,40},{56,48},{64,56},{72,6... | collective-permute-start | bytes 98312 | tf_op jit(solution)/shard_map/ppermute | solution.py:382
  126.5 3.1 %collective-permute-done.3.nedge_ref = f32[8,1024]{1,0:T(8,128)S(1)} collective-permute-done((f32[8,1024]{1,0:T(8,128)S(1)}, f32[8,1024]{1,0:T(8,128)S(1)}, u32[]{:S(2)}, u32[]{:S(2)}) %collective-permute-start.3) | collective-permute-done | bytes 32800 | tf_op jit(solution)/shard_map/ppermute | solution.py:382
  129.6 1.4 copy-done.4
  131.0 3.7 %shard_map.152 = (f32[3,16,1024]{2,1,0:T(8,128)S(1)}, f32[16,1024]{1,0:T(8,128)S(1)}, f32[8,16,256]{2,1,0:T(8,128)S(1)}) custom-call(bf16[3,256,1024]{2,1,0:T(8,128)(2,1)S(1)} %copy-done.4, f32[8,1024]{1,0:T(8,128)S(1)} %collective-permute-done.3.nedge_ref, bf16[3,256,1024]{2,1,0:T(8,128)(2,1)S(1)} %get-tuple-element.41.pre_ref, ...), custom_call_target="tpu_custom_call" | custom-call | flops 134217728 | bytes 6291456 | tf_op jit(solution)/shard_map/pallas_call | solution.py:15
  134.7 10.3 %all_to_all.30.lows_ref = f32[8,16,256]{2,1,0:T(8,128)S(1)} all-to-all(f32[8,16,256]{2,1,0:T(8,128)S(1)} %get-tuple-element.59), channel_id=1, replica_groups=mesh['ctx'=32,'tp'=8] {'tp'}, dimensions={0} | all-to-all | bytes 262144 | tf_op jit(solution)/shard_map/all_to_all | solution.py:376
  145.0 0.4 shard_map.153
  145.4 18.9 %all_to_all.31.in_ref = f32[32,24,128]{2,1,0:T(8,128)S(1)} all-to-all(f32[32,24,128]{2,1,0:T(8,128)S(1)} %shard_map.153), channel_id=1, replica_groups=mesh['ctx'=32,'tp'=8] {'ctx'}, dimensions={0} | all-to-all | bytes 786432 | tf_op jit(solution)/shard_map/all_to_all | solution.py:376
  164.3 0.1 shard_map.154
  164.3 13.7 %all_to_all.32.in_ref = f32[32,24,128]{2,1,0:T(8,128)S(1)} all-to-all(f32[32,24,128]{2,1,0:T(8,128)S(1)} %shard_map.154), channel_id=1, replica_groups=mesh['ctx'=32,'tp'=8] {'ctx'}, dimensions={0} | all-to-all | bytes 786432 | tf_op jit(solution)/shard_map/all_to_all | solution.py:376
  178.0 1.1 shard_map.155
  179.1 0.6 reshape.59
  (45 shorter events, 0.1 us)
Async XLA Ops:
  0.6 1.0 copy-start.5
  1.7 1.4 copy-start.14
  3.1 0.8 copy-start.21
  3.8 0.7 copy-start.24
  6.0 1.7 copy-start.2
  7.6 0.7 copy-start.11
  8.3 8.7 %copy-start.26 = (bf16[3,3,1024]{2,1,0:T(4,128)(2,1)S(1)}, bf16[3,3,1024]{2,1,0:T(4,128)(2,1)}, u32[]{:S(2)}) copy-start(bf16[3,3,1024]{2,1,0:T(4,128)(2,1)} %param.15) | copy-start | bytes 55300
  8.3 9.4 %copy-start.27 = (s32[64]{0:T(128)S(1)}, s32[64]{0:T(128)}, u32[]{:S(2)}) copy-start(s32[64]{0:T(128)} %param.18) | copy-start | bytes 772
  8.3 49.9 %all-to-all-start = ((bf16[32,16,3200]{2,1,0:T(8,128)(2,1)}), bf16[32,16,3200]{2,1,0:T(8,128)(2,1)S(1)}, u32[]{:S(2)}, u32[]{:S(2)}) async-start(bf16[32,16,3200]{2,1,0:T(8,128)(2,1)} %copy-done.2), calls=%async_computation | async-start | bytes 6553600 | tf_op jit(solution)/shard_map/all_to_all | solution.py:376
  58.7 0.7 copy-start.13
  59.3 16.2 %all-to-all-start.1 = ((f32[8,16,256]{2,1,0:T(8,128)}), f32[8,16,256]{2,1,0:T(8,128)}, u32[]{:S(2)}, u32[]{:S(2)}) async-start(f32[8,16,256]{2,1,0:T(8,128)} %copy-done.13), calls=%async_computation.1 | async-start | bytes 262144 | tf_op jit(solution)/shard_map/all_to_all | solution.py:376
  68.5 1.2 copy-start
  75.6 1.4 copy-start.1
  77.0 0.9 copy-start.9
  77.9 6.9 %copy-start.25 = (bf16[9,1024]{1,0:T(8,128)(2,1)S(1)}, bf16[9,1024]{1,0:T(8,128)(2,1)}, u32[]{:S(2)}) copy-start(bf16[9,1024]{1,0:T(8,128)(2,1)} %convert_element_type.22) | copy-start | bytes 55300
  77.9 8.0 %copy-start.7 = (bf16[256,1024]{1,0:T(8,128)(2,1)S(1)}, bf16[256,1024]{1,0:T(8,128)(2,1)}, u32[]{:S(2)}) copy-start(bf16[256,1024]{1,0:T(8,128)(2,1)} %cot_ref.3) | copy-start | bytes 1572868
  79.5 16.5 %copy-start.6 = (bf16[256,1024]{1,0:T(8,128)(2,1)S(1)}, bf16[256,1024]{1,0:T(8,128)(2,1)}, u32[]{:S(2)}) copy-start(bf16[256,1024]{1,0:T(8,128)(2,1)} %tok_ref.3) | copy-start | bytes 1572868
  79.5 16.5 %copy-start.12 = (bf16[512,256]{1,0:T(8,128)(2,1)S(1)}, bf16[512,256]{1,0:T(8,128)(2,1)}, u32[]{:S(2)}) copy-start(bf16[512,256]{1,0:T(8,128)(2,1)} %copy-done.11) | copy-start | bytes 786436
  79.5 6.3 %collective-permute-start = (f32[8,1024]{1,0:T(8,128)S(1)}, f32[8,1024]{1,0:T(8,128)S(1)}, u32[]{:S(2)}, u32[]{:S(2)}) collective-permute-start(f32[8,1024]{1,0:T(8,128)S(1)} %get-tuple-element.42), channel_id=1, source_target_pairs={{0,8},{8,16},{16,24},{24,32},{32,40},{40,48},{48,56},{56,64},{64,7... | collective-permute-start | bytes 98312 | tf_op jit(solution)/shard_map/ppermute | solution.py:382
  88.6 1.2 copy-start.15
  89.8 7.6 %copy-start.17 = (bf16[256,1024]{1,0:T(8,128)(2,1)}, bf16[256,1024]{1,0:T(8,128)(2,1)S(1)}, u32[]{:S(2)}) copy-start(bf16[256,1024]{1,0:T(8,128)(2,1)S(1)} %get-tuple-element.46.x_ref) | copy-start | bytes 1572868
  89.8 7.6 %copy-start.19 = (bf16[256,1024]{1,0:T(8,128)(2,1)}, bf16[256,1024]{1,0:T(8,128)(2,1)S(1)}, u32[]{:S(2)}) copy-start(bf16[256,1024]{1,0:T(8,128)(2,1)S(1)} %get-tuple-element.48.b_ref) | copy-start | bytes 1572868
  89.8 16.7 %collective-permute-start.1 = (bf16[128,1024]{1,0:T(8,128)(2,1)}, bf16[128,1024]{1,0:T(8,128)(2,1)}, u32[]{:S(2)}, u32[]{:S(2)}) collective-permute-start(bf16[128,1024]{1,0:T(8,128)(2,1)} %get-tuple-element.47), channel_id=1, source_target_pairs={{0,8},{8,16},{16,24},{24,32},{32,40},{40,48},{48,56},{56,64},{64,7... | collective-permute-start | bytes 786440 | tf_op jit(solution)/shard_map/ppermute | solution.py:382
  94.0 12.5 %copy-start.22 = (bf16[64,128]{1,0:T(8,128)(2,1)S(1)}, bf16[64,128]{1,0:T(8,128)(2,1)}, u32[]{:S(2)}) copy-start(bf16[64,128]{1,0:T(8,128)(2,1)} %filt_ref.1) | copy-start | bytes 49156
  94.0 12.5 %copy-start.23 = (f32[1024]{0:T(1024)S(1)}, f32[1024]{0:T(1024)}, u32[]{:S(2)}) copy-start(f32[1024]{0:T(1024)} %param.17) | copy-start | bytes 12292
  94.1 12.5 %collective-permute-start.2 = (bf16[128,1024]{1,0:T(8,128)(2,1)}, bf16[128,1024]{1,0:T(8,128)(2,1)}, u32[]{:S(2)}, u32[]{:S(2)}) collective-permute-start(bf16[128,1024]{1,0:T(8,128)(2,1)} %get-tuple-element.49), channel_id=1, source_target_pairs={{8,0},{16,8},{24,16},{32,24},{40,32},{48,40},{56,48},{64,56},{72,6... | collective-permute-start | bytes 786440 | tf_op jit(solution)/shard_map/ppermute | solution.py:382
  97.4 26.9 %all-to-all-start.2 = ((bf16[32,16,1024]{2,1,0:T(8,128)(2,1)}), bf16[32,16,1024]{2,1,0:T(8,128)(2,1)S(1)}, u32[]{:S(2)}, u32[]{:S(2)}) async-start(bf16[32,16,1024]{2,1,0:T(8,128)(2,1)} %shard_map.151), calls=%async_computation.2 | async-start | bytes 2097152 | tf_op jit(solution)/shard_map/all_to_all | solution.py:376
  106.6 1.0 copy-start.8
  107.6 1.4 copy-start.16
  109.0 1.0 copy-start.18
  110.1 1.0 copy-start.20
  111.1 18.4 %copy-start.10 = (bf16[16,3,1024]{2,0,1:T(8,128)(2,1)S(1)}, bf16[16,3,1024]{2,0,1:T(8,128)(2,1)}, u32[]{:S(2)}) copy-start(bf16[16,3,1024]{2,0,1:T(8,128)(2,1)} %param.14) | copy-start | bytes 294916
  123.2 1.2 copy-start.3
  124.3 5.2 %collective-permute-start.3 = (f32[8,1024]{1,0:T(8,128)S(1)}, f32[8,1024]{1,0:T(8,128)S(1)}, u32[]{:S(2)}, u32[]{:S(2)}) collective-permute-start(f32[8,1024]{1,0:T(8,128)S(1)} %get-tuple-element.57), channel_id=1, source_target_pairs={{8,0},{16,8},{24,16},{32,24},{40,32},{48,40},{56,48},{64,56},{72,6... | collective-permute-start | bytes 98312 | tf_op jit(solution)/shard_map/ppermute | solution.py:382
  129.6 1.4 copy-start.4
where the time goes:
time: 181 us; the launch traced here: 180 us
  waiting for transfers between devices  50.2 us (28%)
  blocking collectives  42.9 us (24%)
  starting transfers between devices  39.5 us (22%)
  Pallas kernels  26 us (14%)
  local copies, waits for them, and re-layouts  20.1 us (11%)
    all_to_all x3, waiting for transfers between devices, swap(): return lax.all_to_all(value, axis, split_axis=0, concat_axis=0, tiled=True)  46.1 us
    all_to_all x3, blocking collectives, swap(): return lax.all_to_all(value, axis, split_axis=0, concat_axis=0, tiled=True)  42.9 us
    all_to_all x3, starting transfers between devices, swap(): return lax.all_to_all(value, axis, split_axis=0, concat_axis=0, tiled=True)  26 us
    pallas_call x11, Pallas kernels, call(): pl.pallas_call(kernel, out_shape=tuple((jax.ShapeDtypeStruct(s, d) for s,...  26 us
    unnamed x56, local copies, waits for them, and re-layouts  18.7 us
    ppermute x4, starting transfers between devices, neighbour(): return lax.ppermute(value, 'ctx', pairs)  13.5 us
    ppermute x4, waiting for transfers between devices, neighbour(): return lax.ppermute(value, 'ctx', pairs)  4.06 us
  transfers between devices with their start and end apart: 7, of which 4 were waited for; matrix products, arithmetic and copies ran while one was open for 0% of the time, Pallas kernels for 8%

commit v1 on v0

v1 whole, which is shorter than its diff:
```python
import jax
import jax.numpy as jnp
from jax import lax
from jax.experimental import pallas as pl
from jax.experimental.pallas import tpu as pltpu
from jax.sharding import PartitionSpec as P

BF = jnp.bfloat16
F32 = jnp.float32
I32 = jnp.int32


def whole(kernel, outs, scratch=(), flops=0, nbytes=0):
    def call(*args):
        return pl.pallas_call(
            kernel,
            out_shape=tuple(jax.ShapeDtypeStruct(s, d) for s, d in outs),
            in_specs=[pl.BlockSpec(memory_space=pltpu.VMEM)] * len(args),
            out_specs=tuple(pl.BlockSpec(memory_space=pltpu.VMEM) for _ in outs),
            scratch_shapes=list(scratch),
            compiler_params=pltpu.CompilerParams(vmem_limit_bytes=20 << 20),
            cost_estimate=pl.CostEstimate(flops=flops, bytes_accessed=nbytes, transcendentals=0),
        )(*args)

    return call


def tiled(kernel, grid, in_specs, outs, scratch, flops, nbytes, limit):
    def call(*args):
        return pl.pallas_call(
            kernel,
            grid=(grid,),
            out_shape=tuple(jax.ShapeDtypeStruct(s, d) for s, d, _, _ in outs),
            in_specs=[pl.BlockSpec(b, m) for b, m in in_specs],
            out_specs=tuple(pl.BlockSpec(b, m) for _, _, b, m in outs),
            scratch_shapes=list(scratch),
            compiler_params=pltpu.CompilerParams(
                vmem_limit_bytes=limit, dimension_semantics=("arbitrary",)
            ),
            cost_estimate=pl.CostEstimate(flops=flops, bytes_accessed=nbytes, transcendentals=0),
        )(*args)

    return call


def at2(i):
    return (0, i)


def at3(i):
    return (0, 0, i)


def fixed2(i):
    return (0, 0)


def dot(a, b, ca=1, cb=0):
    return lax.dot_general(a, b, (((ca,), (cb,)), ((), ())), preferred_element_type=F32)


def iota(shape, dim):
    return lax.broadcasted_iota(I32, shape, dim)


def send_kernel(
    pos_ref, frozen_ref, tok_ref, down_ref, out_ref, sel_ref,
    in_buf, tok_buf, out_buf, extra_buf, in_sem, out_sem,
):
    rows = pos_ref.shape[1]
    slots = sel_ref.shape[0]
    parts, shards, cap, chans = out_buf.shape
    rank_dim = down_ref.shape[0]
    loads = [pltpu.make_async_copy(tok_ref, tok_buf, in_sem.at[parts])]
    for a in range(parts):
        loads.append(pltpu.make_async_copy(frozen_ref.at[a], in_buf.at[a], in_sem.at[a]))
    for load in loads:
        load.start()
    pos = pos_ref[...]
    dest = (pos // rows).astype(F32)
    within = (pos % rows).astype(F32)
    dest_row = jnp.broadcast_to(dest, (rows, rows))
    dest_col = dest_row.T
    earlier = (dest_row == dest_col) & (iota((rows, rows), 0) < iota((rows, rows), 1))
    rank = jnp.sum(jnp.where(earlier, 1.0, 0.0), axis=0, keepdims=True)
    slot = dest * float(cap) + rank
    sel = jnp.where(
        iota((slots, rows), 0).astype(F32) == jnp.broadcast_to(slot, (slots, rows)), 1.0, 0.0
    ).astype(BF)
    sel_ref[...] = sel
    mark = jnp.where(iota((8, rows), 0) == 0, jnp.broadcast_to(within, (8, rows)), 1.0)
    loads[0].wait()
    low = dot(down_ref[...], tok_buf[...], 1, 1)
    high = low.astype(BF).astype(F32)
    rest = low - high
    mid = rest.astype(BF).astype(F32)
    extra = jnp.concatenate(
        [high, mid, rest - mid, mark, jnp.zeros((128 - 8 - 3 * rank_dim, rows), F32)]
    )
    extra_buf[...] = dot(sel, extra.T.astype(BF)).astype(BF).reshape(shards, cap, 128)
    stores = [
        pltpu.make_async_copy(
            extra_buf, out_ref.at[:, :, pl.ds(parts * chans, 128)], out_sem.at[parts]
        )
    ]
    stores[0].start()
    for a in range(parts):
        loads[1 + a].wait()
        for c in range(0, chans, 256):
            out_buf[a, :, :, c : c + 256] = (
                dot(sel, in_buf[a, :, c : c + 256]).astype(BF).reshape(shards, cap, 256)
            )
        store = pltpu.make_async_copy(
            out_buf.at[a], out_ref.at[:, :, pl.ds(a * chans, chans)], out_sem.at[a]
        )
        store.start()
        stores.append(store)
    for store in stores:
        store.wait()


def send_tokens_kernel(sel_ref, tok_ref, out_ref):
    shards, cap, chans = out_ref.shape
    for c in range(0, chans, 256):
        out_ref[:, :, c : c + 256] = (
            dot(sel_ref[...], tok_ref[:, c : c + 256]).astype(BF).reshape(shards, cap, 256)
        )


def place_kernel(extra_ref, place_ref, low_ref):
    copies, rank_dim, rows = low_ref.shape
    shards, cap, _ = extra_ref.shape
    slots = shards * cap
    extra = extra_ref[...].reshape(slots, 128)
    mark = extra[:, 3 * rank_dim : 3 * rank_dim + 2].astype(F32)
    target = jnp.where(mark[:, 1:2] > 0.5, mark[:, 0:1], -1.0)
    place_t = jnp.where(
        jnp.broadcast_to(target, (slots, rows)) == iota((slots, rows), 1).astype(F32), 1.0, 0.0
    )
    place = place_t.T.astype(BF)
    place_ref[...] = place
    split = dot(place, extra).T
    low = split[:rank_dim] + split[rank_dim : 2 * rank_dim] + split[2 * rank_dim : 3 * rank_dim]
    for t in range(copies):
        low_ref[t] = low


def shifted_down(value, edge0, edge1):
    row = iota(value.shape, 0)
    one = jnp.where(row == 0, edge1, pltpu.roll(value, 1, 0))
    two = jnp.where(row == 0, edge0, jnp.where(row == 1, edge1, pltpu.roll(value, 2, 0)))
    return one, two


def post_kernel(
    got0_ref, got1_ref, got2_ref, place_ref, lows_ref, up_ref, taps_ref, off_ref, cot_ref,
    pre_ref, post_ref, x_ref, b_ref, ahead_ref, behind_ref, low_ref,
    ahead_edge, behind_edge, low_t_ref,
):
    parts, rows, width = pre_ref.shape
    slots = place_ref.shape[1]

    @pl.when(pl.program_id(0) == 0)
    def _():
        total = lows_ref[0]
        for t in range(1, lows_ref.shape[0]):
            total = total + lows_ref[t]
        low_ref[...] = total.astype(BF)
        low_t_ref[...] = total.T.astype(BF)

    off = jnp.concatenate([off_ref[:rows]] * (width // 128), 1)
    mask1 = jnp.where(off >= 1.0, 1.0, 0.0)
    mask2 = jnp.where(off >= 2.0, 1.0, 0.0)
    ahead_edge[...] = jnp.zeros_like(ahead_edge)
    behind_edge[...] = jnp.zeros_like(behind_edge)
    nothing = jnp.zeros((1, width), F32)
    made = []
    for a, got_ref in enumerate((got0_ref, got1_ref, got2_ref)):
        value = dot(place_ref[...], got_ref[...].reshape(slots, width)) + dot(low_t_ref[...], up_ref[a])
        value = value.astype(BF)
        pre_ref[a] = value
        value = value.astype(F32)
        ahead_edge[2 * a : 2 * a + 2] = value[rows - 2 :]
        behind_edge[2 * a : 2 * a + 2] = value[:2]
        one, two = shifted_down(value, nothing, nothing)
        total = (
            taps_ref[a : a + 1] * value
            + taps_ref[parts + a : parts + a + 1] * one * mask1
            + taps_ref[2 * parts + a : 2 * parts + a + 1] * two * mask2
        ).astype(BF)
        post_ref[a] = total
        made.append(total.astype(F32))
    product = (made[1] * made[2]).astype(BF)
    grad = cot_ref[...].astype(F32)
    back = (grad * made[0]).astype(BF)
    x_ref[...] = product
    b_ref[...] = back
    ahead_ref[:128] = product[rows - 128 :]
    behind_ref[:128] = back[:128]
    behind_edge[6:8] = grad[:2]
    behind_edge[8:9] = back[128:144].astype(F32)[:1]
    ahead_ref[128:] = ahead_edge[...].astype(BF)
    behind_ref[128:] = behind_edge[...].astype(BF)


def main_kernel(
    pre_ref, post_ref, x_ref, b_ref, prev_ref, next_ref, cot_ref, taps_ref, skip_ref, filt_ref,
    offc_ref, offr_ref, low_ref, up_ref,
    mixer_ref, piece_ref, backlow_ref,
    mfwd_ref, madj_ref, mpair_ref, frow_ref, grow_ref, fwd_ref, adj_ref, lhs_ref, rf_ref, ra_ref, rp_ref, bp_ref, total_ref,
):
    parts, rows, _ = pre_ref.shape
    step = pl.program_id(0)
    rank_dim = low_ref.shape[0]
    blocks = rows // 128
    sub, lane = iota((128, 128), 0), iota((128, 128), 1)
    turn = jnp.where(sub + lane == 127, 1.0, 0.0).astype(BF)
    @pl.when(step == 0)
    def _():
        total_ref[...] = jnp.zeros_like(total_ref)
        for b in range(blocks + 1):
            first = 128 * b
            tall = 128 if b < blocks else 16
            begin_col = (first + sub).astype(F32) - offc_ref[first : first + 128]
            own = (lane <= sub) & ((first + lane).astype(F32) >= begin_col)
            prev = (lane > sub) & ((first - 128 + lane).astype(F32) >= begin_col)
            prev, own = jnp.where(prev, 1.0, 0.0).astype(BF), jnp.where(own, 1.0, 0.0).astype(BF)
            mfwd_ref[first : first + tall, :128] = prev[:tall]
            mfwd_ref[first : first + tall, 128:] = own[:tall]
            if b < blocks:
                mpair_ref[b, :, :128] = dot(turn, prev)
                mpair_ref[b, :, 128:] = dot(turn, own)
            row0 = jnp.broadcast_to(offr_ref[:, first : first + 128], (128, 128))
            row1 = jnp.broadcast_to(offr_ref[:, first + 128 : first + 256], (128, 128))
            begin0 = (first + lane).astype(F32) - row0
            begin1 = (first + 128 + lane).astype(F32) - row1
            at = (first + sub).astype(F32)
            same = jnp.where((sub <= lane) & (at >= begin0), 1.0, 0.0).astype(BF)
            after = jnp.where((lane < sub) & (at >= begin1), 1.0, 0.0).astype(BF)
            madj_ref[first : first + tall, :128] = same[:tall]
            madj_ref[first : first + tall, 128:] = after[:tall]

    filt = filt_ref[...]
    flip = jnp.where((sub + lane) % 128 == 0, 1.0, 0.0).astype(BF)
    frow_ref[...] = filt.astype(F32)
    grow_ref[...] = dot(filt, flip)
    mask1 = jnp.where(offc_ref[:rows] >= 1.0, 1.0, 0.0)
    mask2 = jnp.where(offc_ref[:rows] >= 2.0, 1.0, 0.0)
    next1 = jnp.where(offc_ref[rows : rows + 16] >= 1.0, 1.0, 0.0)
    next2 = jnp.where(offc_ref[rows : rows + 16] >= 2.0, 1.0, 0.0)
    low = low_ref[...]
    row = iota((rows, 128), 0)
    top = iota((16, 128), 0) < 2
    lane_group = lane // 16
    piece_ref[...] = jnp.zeros_like(piece_ref)

    def tap(s, a):
        return taps_ref[s * parts + a : s * parts + a + 1]

    for g in range(8):
        f_row = jnp.broadcast_to(frow_ref[g : g + 1, :], (128, 128))
        g_row = jnp.broadcast_to(grow_ref[g : g + 1, :], (128, 128))
        circ = pltpu.roll(f_row, 0, 1, stride=1, stride_axis=0).astype(BF)
        circ_t = pltpu.roll(g_row, 0, 1, stride=1, stride_axis=0).astype(BF)
        two, two_t = jnp.concatenate([circ, circ], 1), jnp.concatenate([circ_t, circ_t], 1)
        for b in range(blocks + 1):
            tall = 128 if b < blocks else 16
            at = 1024 * b + tall * g
            fwd_ref[at : at + tall] = two_t[:tall] * mfwd_ref[128 * b : 128 * b + tall]
            adj_ref[at : at + tall] = two[:tall] * madj_ref[128 * b : 128 * b + tall]
    pedge = prev_ref[128:].astype(F32)
    nedge = next_ref[128:].astype(F32)
    heads, after = [], []
    for a in range(parts):
        head = pre_ref[a, :16].astype(F32)
        one, two = shifted_down(head, pedge[2 * a : 2 * a + 1], pedge[2 * a + 1 : 2 * a + 2])
        heads.append(
            (tap(0, a) * head + tap(1, a) * one * mask1[:16] + tap(2, a) * two * mask2[:16]).astype(BF)
        )
        tail = pre_ref[a, rows - 16 :].astype(F32)
        head = nedge if a == 0 else pltpu.roll(nedge, 16 - 2 * a, 0)
        one, two = shifted_down(head, tail[14:15], tail[15:16])
        after.append(
            (tap(0, a) * head + tap(1, a) * one * next1 + tap(2, a) * two * next2)
            .astype(BF)
            .astype(F32)
        )
    posts = [jnp.concatenate([heads[a], post_ref[a, 16:]]) for a in range(parts)]
    x_head = (heads[1].astype(F32) * heads[2].astype(F32)).astype(BF)
    b_head = (cot_ref[:16].astype(F32) * heads[0].astype(F32)).astype(BF)
    x_next = jnp.where(top, after[1] * after[2], 0.0).astype(BF)
    cot_next = pltpu.roll(nedge, 10, 0)
    b_next = jnp.where(top, cot_next * after[0], next_ref[:16].astype(F32)).astype(BF)
    b_last = jnp.where(iota((16, 128), 0) == 0, pltpu.roll(nedge, 8, 0), 0.0).astype(BF)
    blank = jnp.zeros((112, 128), BF)
    x_own = jnp.concatenate([x_head, x_ref[16:]])
    x_win = jnp.concatenate([prev_ref[:128], x_own, x_next, blank])
    b_win = jnp.concatenate(
        [b_head, b_ref[16:], b_next, next_ref[16:128], b_last, blank]
    )
    for b in range(blocks + 1):
        at = slice(1024 * b, 1024 * b + (1024 if b < blocks else 128))
        xw = x_win[128 * b : 128 * b + 256]
        rf_ref[at] = dot(fwd_ref[at], xw)
        ra_ref[at] = dot(adj_ref[at], b_win[128 * b : 128 * b + 256])
        if b < blocks:
            back = dot(turn, b_win[128 * b : 128 * b + 128])
            for g in range(8):
                lhs_ref[128 * g : 128 * g + 128] = jnp.where(lane_group == g, back, 0.0).astype(BF)
            rp_ref[b] = dot(lhs_ref[...], xw, 1, 1)
    for g in range(8):
        part = jnp.zeros((128, 128), F32)
        for b in range(blocks):
            pair = rp_ref[b, 128 * g : 128 * g + 128] * mpair_ref[b]
            part = part + pair[:, :128] + pair[:, 128:]
        part = pltpu.roll(part, 0, 1, stride=1, stride_axis=0)
        piece_ref[3, 0, 8 + g : 9 + g] = jnp.sum(part, axis=0, keepdims=True)
    skip = skip_ref[:]
    gsum = jnp.zeros((1, 128), F32)
    edges = None
    for b in range(blocks + 1):
        tall = 128 if b < blocks else 16
        conv = jnp.zeros((tall, 128), F32)
        adj = jnp.zeros((tall, 128), F32)
        for g in range(8):
            at = 1024 * b + tall * g
            conv = jnp.where(lane_group[:tall] == g, rf_ref[at : at + tall], conv)
            adj = jnp.where(lane_group[:tall] == g, ra_ref[at : at + tall], adj)
        at = slice(128 * b, 128 * b + 128)
        if b < blocks:
            query, key, value = (post[at].astype(F32) for post in posts)
            product = x_own[at].astype(F32)
            grad = cot_ref[at].astype(F32)
        else:
            query, key, value = after
            product = x_next.astype(F32)
            grad = cot_next
        direct = conv + skip * product
        gated = grad * query
        back = adj + skip * gated
        made = [(grad * direct).astype(BF), (back * value).astype(BF), (back * key).astype(BF)]
        if b < blocks:
            mixer_ref[at] = (query * direct).astype(BF)
            gsum = gsum + jnp.sum(gated * product, axis=0, keepdims=True)
            for a in range(parts):
                bp_ref[a, at] = made[a].astype(F32)
        else:
            edges = [m.astype(F32) for m in made]
    piece_ref[3, 0, 1:2] = gsum
    total = total_ref[...]
    for a in range(parts):
        post = bp_ref[a]
        edge0, edge1 = edges[a][0:1], edges[a][1:2]
        post1, post2 = post * mask1, post * mask2
        up1 = jnp.where(row == rows - 1, edge0 * next1[0:1], pltpu.roll(post1, rows - 1, 0))
        up2 = jnp.where(
            row == rows - 2,
            edge0 * next2[0:1],
            jnp.where(row == rows - 1, edge1 * next2[1:2], pltpu.roll(post2, rows - 2, 0)),
        )
        back_pre = (tap(0, a) * post + tap(1, a) * up1 + tap(2, a) * up2).astype(BF)
        pre = pre_ref[a, :].astype(F32)
        one, two = shifted_down(pre, pedge[2 * a : 2 * a + 1], pedge[2 * a + 1 : 2 * a + 2])
        sums = (
            jnp.sum(post * pre, axis=0, keepdims=True),
            jnp.sum(post1 * one, axis=0, keepdims=True),
            jnp.sum(post2 * two, axis=0, keepdims=True),
        )
        for t, value in enumerate(sums):
            k = t * parts + a
            if k < 8:
                piece_ref[2, 0, 16 + k : 17 + k] = value
            else:
                piece_ref[3, 0, 0:1] = value
        up_grad = dot(low, back_pre)
        if a == 0:
            piece_ref[0, 0, 16:24] = up_grad[:8]
            piece_ref[1, 0, :8] = up_grad[8:]
        elif a == 1:
            piece_ref[1, 0, 8:24] = up_grad
        else:
            piece_ref[2, 0, :16] = up_grad
        total = total + dot(up_ref[a, :], back_pre, 1, 1)
    total_ref[...] = total


    @pl.when(step == pl.num_programs(0) - 1)
    def _():
        for t in range(backlow_ref.shape[0]):
            backlow_ref[t] = total


def gather_kernel(lows_ref, got_ref, place_ref, sums_ref, out_ref):
    shards, cap, chans = got_ref.shape
    total = lows_ref[0]
    for t in range(1, lows_ref.shape[0]):
        total = total + lows_ref[t]
    placed = dot(total.astype(BF), place_ref[...]).astype(BF)
    down = jnp.concatenate(
        [
            dot(placed, got_ref[:, :, c : c + 256].reshape(shards * cap, 256))
            for c in range(0, chans, 256)
        ],
        1,
    )
    tiles = chans // 128
    for i in range(tiles):
        first = jnp.concatenate([down[:, 128 * i : 128 * i + 128], sums_ref[0, i, 16:]])
        out_ref[i] = first.astype(BF)
        for k in range(1, 4):
            out_ref[k * tiles + i] = sums_ref[k, i].astype(BF)


def sum_kernel(in_ref, out_ref):
    total = in_ref[0].astype(F32)
    for t in range(1, in_ref.shape[0]):
        total = total + in_ref[t].astype(F32)
    total = total.astype(BF)
    for t in range(out_ref.shape[0]):
        out_ref[t] = total


def spread_kernel(in_ref, down_ref, up_ref, short_ref, long_ref, gskip_ref):
    tiles = down_ref.shape[1] // 128
    flip = jnp.where(iota((128, 128), 0) + iota((128, 128), 1) == 127, 1.0, 0.0).astype(BF)
    for i in range(tiles):
        cols = slice(128 * i, 128 * i + 128)
        part = [in_ref[k * tiles + i].astype(F32) for k in range(4)]
        down_ref[:, cols] = part[0][:16]
        up_ref[0, :8, cols] = part[0][16:]
        up_ref[0, 8:, cols] = part[1][:8]
        up_ref[1, :, cols] = part[1][8:]
        up_ref[2, :, cols] = part[2][:16]
        short_ref[:8, cols] = part[2][16:]
        short_ref[8:9, cols] = part[3][0:1]
        gskip_ref[i : i + 1] = part[3][1:2]
        long_ref[8 * i : 8 * i + 8] = dot(part[3][8:16].astype(BF), flip)


def swap(value, axis):
    return lax.all_to_all(value, axis, split_axis=0, concat_axis=0, tiled=True)


def neighbour(value, steps):
    count = lax.axis_size("ctx")
    pairs = [(i, i + steps) for i in range(count) if 0 <= i + steps < count]
    return lax.ppermute(value, "ctx", pairs)


def doc_offsets(positions, lengths):
    index = jnp.arange(lengths.shape[0], dtype=I32)
    starts = jnp.sum(jnp.where(index[None, :] < index[:, None], lengths[None, :], 0), axis=1)
    begins = jnp.max(jnp.where(starts[None, :] <= positions[:, None], starts[None, :], 0), axis=1)
    return positions - begins


def on_device(
    tokens,
    frozen,
    cotangent,
    adapter_down_weight,
    adapter_up_weight,
    short_depthwise_filter,
    long_group_filter,
    skip_direct_scale,
    document_lengths,
    window_row_position,
):
    rows, chans = tokens.shape
    parts = frozen.shape[1]
    rank_dim = adapter_down_weight.shape[0]
    taps = short_depthwise_filter.shape[0]
    groups = long_group_filter.shape[0]
    shards = lax.axis_size("ctx")
    columns = lax.axis_size("tp")
    cap = 2 * rows // shards
    slots = shards * cap
    frozen = frozen.transpose(1, 0, 2)
    up = adapter_up_weight.transpose(1, 0, 2)
    pos_row = window_row_position.reshape(1, rows)
    vmem, far = pl.BlockSpec(memory_space=pltpu.VMEM), pl.BlockSpec(memory_space=pltpu.HBM)
    send, sel = pl.pallas_call(
        send_kernel,
        out_shape=(
            jax.ShapeDtypeStruct((shards, cap, parts * chans + 128), BF),
            jax.ShapeDtypeStruct((slots, rows), BF),
        ),
        in_specs=[vmem, far, far, vmem],
        out_specs=(far, vmem),
        scratch_shapes=[
            pltpu.VMEM((parts, rows, chans), BF),
            pltpu.VMEM((rows, chans), BF),
            pltpu.VMEM((parts, shards, cap, chans), BF),
            pltpu.VMEM((shards, cap, 128), BF),
            pltpu.SemaphoreType.DMA((parts + 1,)),
            pltpu.SemaphoreType.DMA((parts + 1,)),
        ],
        compiler_params=pltpu.CompilerParams(vmem_limit_bytes=66_000_000),
        cost_estimate=pl.CostEstimate(flops=1 << 30, bytes_accessed=5 << 20, transcendentals=0),
    )(pos_row, frozen, tokens, adapter_down_weight)
    got = swap(send, "ctx")

    send, sel, document_lengths, short_depthwise_filter = lax.optimization_barrier(
        (send, sel, document_lengths, short_depthwise_filter)
    )
    (send_tok,) = whole(
        send_tokens_kernel, [((shards, cap, chans), BF)], flops=2 * slots * rows * chans, nbytes=2 << 20
    )(sel, tokens)
    first = lax.axis_index("ctx") * rows
    offsets = doc_offsets(first + jnp.arange(rows + 256, dtype=I32), document_lengths).astype(F32)
    off_row = offsets.reshape(1, rows + 256)
    off_col = jnp.broadcast_to(offsets[:, None], (rows + 256, 128))
    tap_rows = short_depthwise_filter.reshape(taps * parts, chans).astype(F32)
    tap_rows = jnp.pad(tap_rows, ((0, 16 - taps * parts), (0, 0)))
    skip_row = skip_direct_scale.reshape(1, chans)
    got, send_tok, off_row, off_col, tap_rows = lax.optimization_barrier(
        (got, send_tok, off_row, off_col, tap_rows)
    )

    place, low_parts = tiled(
        place_kernel,
        1,
        [((shards, cap, 128), lambda i: (0, 0, parts * chans // 128))],
        [
            ((rows, slots), BF, (rows, slots), fixed2),
            ((columns, rank_dim, rows), F32, (columns, rank_dim, rows), lambda i: (0, 0, 0)),
        ],
        [],
        1 << 26,
        1 << 19,
        60_000_000,
    )(got)
    lows = swap(low_parts, "tp")
    got, lows = lax.optimization_barrier((got, lows))
    wide = 256
    steps = chans // wide
    pre, post, x, back, ahead, behind, low = tiled(
        post_kernel,
        steps,
        [((shards, cap, wide), lambda i, a=a: (0, 0, a * steps + i)) for a in range(parts)]
        + [
            ((rows, slots), fixed2),
            ((columns, rank_dim, rows), lambda i: (0, 0, 0)),
            ((parts, rank_dim, wide), at3),
            ((16, wide), at2),
            ((rows + 256, 128), fixed2),
            ((rows, wide), at2),
        ],
        [
            ((parts, rows, chans), BF, (parts, rows, wide), at3),
            ((parts, rows, chans), BF, (parts, rows, wide), at3),
            ((rows, chans), BF, (rows, wide), at2),
            ((rows, chans), BF, (rows, wide), at2),
            ((144, chans), BF, (144, wide), at2),
            ((144, chans), BF, (144, wide), at2),
            ((rank_dim, rows), BF, (rank_dim, rows), fixed2),
        ],
        [
            pltpu.VMEM((16, wide), F32),
            pltpu.VMEM((16, wide), F32),
            pltpu.VMEM((rows, rank_dim), BF),
        ],
        1 << 30,
        8 << 20,
        60_000_000,
    )(got, got, got, place, lows, up, tap_rows, off_col, cotangent)
    send_tok, ahead, behind = lax.optimization_barrier((send_tok, ahead, behind))
    from_prev = neighbour(ahead, 1)
    from_next = neighbour(behind, -1)
    got_tok = swap(send_tok, "ctx")
    blocks = rows // 128
    tall = 1024 * blocks + 128
    mixer, sums, back_low_part = tiled(
        main_kernel,
        chans // 128,
        [
            ((parts, rows, 128), at3),
            ((parts, rows, 128), at3),
            ((rows, 128), at2),
            ((rows, 128), at2),
            ((144, 128), at2),
            ((144, 128), at2),
            ((rows, 128), at2),
            ((16, 128), at2),
            ((1, 128), at2),
            ((8, 128), lambda i: (i, 0)),
            ((rows + 256, 128), fixed2),
            ((1, rows + 256), fixed2),
            ((rank_dim, rows), fixed2),
            ((parts, rank_dim, 128), at3),
        ],
        [
            ((rows, chans), BF, (rows, 128), at2),
            ((4, chans // 128, 24, 128), F32, (4, 1, 24, 128), lambda i: (0, i, 0, 0)),
            ((columns, rank_dim, rows), F32, (columns, rank_dim, rows), lambda i: (0, 0, 0)),
        ],
        [
            pltpu.VMEM((128 * blocks + 16, 256), BF),
            pltpu.VMEM((128 * blocks + 16, 256), BF),
            pltpu.VMEM((blocks, 128, 256), F32),
            pltpu.VMEM((8, 128), F32),
            pltpu.VMEM((8, 128), F32),
            pltpu.VMEM((tall, 256), BF),
            pltpu.VMEM((tall, 256), BF),
            pltpu.VMEM((1024, 128), BF),
            pltpu.VMEM((tall, 128), F32),
            pltpu.VMEM((tall, 128), F32),
            pltpu.VMEM((blocks, 1024, 256), F32),
            pltpu.VMEM((parts, rows, 128), F32),
            pltpu.VMEM((rank_dim, rows), F32),
        ],
        10 << 30,
        8 << 20,
        60_000_000,
    )(pre, post, x, back, from_prev, from_next, cotangent, tap_rows, skip_row, long_group_filter,
      off_col, off_row, low, up)
    got_tok, back_low_part = lax.optimization_barrier((got_tok, back_low_part))
    back_lows = swap(back_low_part, "tp")
    (pieces,) = whole(
        gather_kernel, [((shards, 24, 128), BF)], flops=1 << 26, nbytes=2 << 20
    )(back_lows, got_tok, place, sums)
    pieces = swap(pieces, "ctx")
    (pieces,) = whole(sum_kernel, [((shards, 24, 128), BF)], flops=1 << 20, nbytes=1 << 20)(pieces)
    pieces = swap(pieces, "ctx")
    grad_down, up_gradient, grad_short, grad_long, grad_skip = whole(
        spread_kernel,
        [
            ((rank_dim, chans), F32),
            ((parts, rank_dim, chans), F32),
            ((taps * parts, chans), F32),
            ((groups, 128), F32),
            ((chans // 128, 128), F32),
        ],
        flops=1 << 20,
        nbytes=1 << 20,
    )(pieces)
    return (
        mixer,
        grad_down,
        up_gradient.transpose(1, 0, 2),
        grad_short.reshape(taps, parts, chans),
        grad_long,
        grad_skip.reshape(chans),
    )


def solution(mesh):
    placed = (
        P("ctx", "tp"),
        P("ctx", None, "tp"),
        P("ctx", "tp"),
        P(None, "tp"),
        P(None, None, "tp"),
        P(None, None, "tp"),
        P("tp", None),
        P("tp"),
        P(),
        P("ctx"),
    )
    return jax.shard_map(
        on_device,
        mesh=mesh,
        in_specs=placed,
        out_specs=(
            P("ctx", "tp"),
            P(None, "tp"),
            P(None, None, "tp"),
            P(None, None, "tp"),
            P("tp", None),
            P("tp"),
        ),
        check_vma=False,
    )
```

time: 181 us -> 157 us (0.87)
  local copies, waits for them, and re-layouts: 20.1 us -> 3.31 us
  starting transfers between devices: 39.5 us -> 23 us
  blocking collectives: 42.9 us -> 56.7 us
  waiting for transfers between devices: 50.2 us -> 38 us
  Pallas kernels: 26 us -> 33.4 us
    pallas_call x0 -> x4, Pallas kernels: none -> 30.7 us  [the longest x3 25.1 us: call(): pl.pallas_call(kernel, grid=(grid,), out_shape=tuple((jax.ShapeDtypeStruc...]
    pallas_call x11 -> x4, Pallas kernels: 26 us -> 2.61 us  [call(): pl.pallas_call(kernel, out_shape=tuple((jax.ShapeDtypeStruct(s, d) for s,...]
    unnamed x56 -> x16, local copies, waits for them, and re-layouts: 18.7 us -> 1.81 us
    all_to_all x3 -> x4, blocking collectives: 42.9 us -> 56.7 us  [swap(): return lax.all_to_all(value, axis, split_axis=0, concat_axis=0, tiled=True)]
    all_to_all x3 -> x2, starting transfers between devices: 26 us -> 15.6 us  [swap(): return lax.all_to_all(value, axis, split_axis=0, concat_axis=0, tiled=True)]
    all_to_all x3 -> x2, waiting for transfers between devices: 46.1 us -> 37.9 us  [swap(): return lax.all_to_all(value, axis, split_axis=0, concat_axis=0, tiled=True)]
    ppermute x4 -> x2, starting transfers between devices: 13.5 us -> 7.42 us  [neighbour(): return lax.ppermute(value, 'ctx', pairs)]
    ppermute x4 -> x2, waiting for transfers between devices: 4.06 us -> 0.01 us  [neighbour(): return lax.ppermute(value, 'ctx', pairs)]
  transfers between devices with their start and end apart: 7 -> 4, of which waited for: 4 -> 1; matrix products, arithmetic and copies ran while one was open for 0% -> 1% of each run, Pallas kernels for 8% -> 11%
where the time goes in v1:
time: 157 us
  blocking collectives  56.7 us (36%)
  waiting for transfers between devices  38 us (24%)
  Pallas kernels  33.4 us (21%)
  starting transfers between devices  23 us (15%)
  local copies, waits for them, and re-layouts  3.31 us (2%)
    all_to_all x4, blocking collectives, swap(): return lax.all_to_all(value, axis, split_axis=0, concat_axis=0, tiled=True)  56.7 us
    all_to_all x2, waiting for transfers between devices, swap(): return lax.all_to_all(value, axis, split_axis=0, concat_axis=0, tiled=True)  37.9 us
    pallas_call x3, Pallas kernels, call(): pl.pallas_call(kernel, grid=(grid,), out_shape=tuple((jax.ShapeDtypeStruc...  25.1 us
    all_to_all x2, starting transfers between devices, swap(): return lax.all_to_all(value, axis, split_axis=0, concat_axis=0, tiled=True)  15.6 us
    ppermute x2, starting transfers between devices, neighbour(): return lax.ppermute(value, 'ctx', pairs)  7.42 us
    pallas_call x1, Pallas kernels, on_device(): pl.pallas_call(send_kernel, out_shape=(jax.ShapeDtypeStruct((shards, cap,...  5.67 us
  transfers between devices with their start and end apart: 4, of which 1 were waited for; matrix products, arithmetic and copies ran while one was open for 1% of the time, Pallas kernels for 11%

profile of v1, /device:TPU:1, one launch (start us, length us, event | category | flops | bytes accessed | tf_op | source)
XLA Modules:
  0.0 156.6 jit_solution(15004433697508374066)
XLA Ops:
  0.6 5.7 %shard_map.145 = (bf16[32,16,3200]{2,1,0:T(8,128)(2,1)}, bf16[512,256]{1,0:T(8,128)(2,1)}) custom-call(s32[1,256]{1,0:T(1,128)} %bitcast.14, bf16[3,256,1024]{2,1,0:T(8,128)(2,1)} %bitcast.10, bf16[256,1024]{1,0:T(8,128)(2,1)} %tok_ref.3, bf16[16,1024]{1,0:T(8,128)(2,1)} %down_ref.1), custom_call_target="tpu_custom_call" | custom-call | flops 1073741824 | bytes 5242880 | tf_op jit(solution)/shard_map/pallas_call | solution.py:482
  6.3 0.0 copy-start.4
  6.3 0.0 copy-start.1
  6.3 0.0 copy-start.3
  6.4 8.8 %all-to-all-start = ((bf16[32,16,3200]{2,1,0:T(8,128)(2,1)}), bf16[32,16,3200]{2,1,0:T(8,128)(2,1)}, u32[]{:S(2)}, u32[]{:S(2)}) async-start(bf16[32,16,3200]{2,1,0:T(8,128)(2,1)} %get-tuple-element.40), calls=%async_computation | async-start | bytes 6553600 | tf_op jit(solution)/shard_map/all_to_all | solution.py:441
  15.1 0.0 copy-start.7
  15.1 0.0 copy-done.4
  15.2 0.0 copy-done.1
  15.2 0.0 copy-done.3
  15.2 1.4 shard_map.146
  16.6 0.0 copy-done.7
  16.6 0.1 select_reduce_fusion.1
  16.7 0.6 pad_convert_fusion.taps_ref
  17.4 0.1 select_reduce_fusion
  17.5 0.6 subtract_convert_fusion.1.offr_ref
  18.1 37.9 %all-to-all-done.extra_ref.got0_ref.got1_ref.got2_ref = bf16[32,16,3200]{2,1,0:T(8,128)(2,1)} async-done(((bf16[32,16,3200]{2,1,0:T(8,128)(2,1)}), bf16[32,16,3200]{2,1,0:T(8,128)(2,1)}, u32[]{:S(2)}, u32[]{:S(2)}) %all-to-all-start) | async-done | bytes 3276832 | tf_op jit(solution)/shard_map/all_to_all | solution.py:441
  56.0 0.8 broadcast_in_dim.37.off_ref.offc_ref
  56.9 2.1 %shard_map.147 = (bf16[256,512]{1,0:T(8,128)(2,1)}, f32[8,16,256]{2,1,0:T(8,128)}) custom-call(bf16[32,16,3200]{2,1,0:T(8,128)(2,1)} %all-to-all-done.extra_ref.got0_ref.got1_ref.got2_ref), custom_call_target="tpu_custom_call" | custom-call | flops 67108864 | bytes 524288 | tf_op jit(solution)/shard_map/pallas_call | solution.py:30
  58.9 16.3 %all_to_all.30.lows_ref = f32[8,16,256]{2,1,0:T(8,128)} all-to-all(f32[8,16,256]{2,1,0:T(8,128)} %get-tuple-element.46), channel_id=1, replica_groups=mesh['ctx'=32,'tp'=8] {'tp'}, dimensions={0} | all-to-all | bytes 262144 | tf_op jit(solution)/shard_map/all_to_all | solution.py:441
  75.3 6.4 %shard_map.148 = (bf16[3,256,1024]{2,1,0:T(8,128)(2,1)}, bf16[3,256,1024]{2,1,0:T(8,128)(2,1)}, bf16[256,1024]{1,0:T(8,128)(2,1)}, bf16[256,1024]{1,0:T(8,128)(2...) custom-call(bf16[32,16,3200]{2,1,0:T(8,128)(2,1)} %all-to-all-done.extra_ref.got0_ref.got1_ref.go, ...), custom_call_target="tpu_custom_call" | custom-call | flops 1073741824 | bytes 8388608 | tf_op jit(solution)/shard_map/pallas_call | solution.py:30
  81.7 5.3 %collective-permute-start = (bf16[144,1024]{1,0:T(8,128)(2,1)}, bf16[144,1024]{1,0:T(8,128)(2,1)S(1)}, u32[]{:S(2)}, u32[]{:S(2)}) collective-permute-start(bf16[144,1024]{1,0:T(8,128)(2,1)} %get-tuple-element.59), channel_id=1, source_target_pairs={{0,8},{8,16},{16,24},{24,32},{32,40},{40,48},{48,56},{56,64},{64,7... | collective-permute-start | bytes 884744 | tf_op jit(solution)/shard_map/ppermute | solution.py:447
  87.0 2.1 %collective-permute-start.1 = (bf16[144,1024]{1,0:T(8,128)(2,1)}, bf16[144,1024]{1,0:T(8,128)(2,1)S(1)}, u32[]{:S(2)}, u32[]{:S(2)}) collective-permute-start(bf16[144,1024]{1,0:T(8,128)(2,1)} %get-tuple-element.60), channel_id=1, source_target_pairs={{8,0},{16,8},{24,16},{32,24},{40,32},{48,40},{56,48},{64,56},{72,6... | collective-permute-start | bytes 884744 | tf_op jit(solution)/shard_map/ppermute | solution.py:447
  89.1 6.8 %all-to-all-start.2 = ((bf16[32,16,1024]{2,1,0:T(8,128)(2,1)}), bf16[32,16,1024]{2,1,0:T(8,128)(2,1)S(1)}, u32[]{:S(2)}, u32[]{:S(2)}) async-start(bf16[32,16,1024]{2,1,0:T(8,128)(2,1)} %shard_map.146), calls=%async_computation.2 | async-start | bytes 2097152 | tf_op jit(solution)/shard_map/all_to_all | solution.py:441
  95.9 0.0 collective-permute-done.prev_ref
  96.0 0.0 copy-start.5
  96.0 0.0 collective-permute-done.1.next_ref
  96.0 0.0 copy-start.6
  96.0 0.7 copy-done.5
  96.7 0.1 copy-done.6
  96.8 0.0 copy-start
  96.8 16.6 %shard_map.149 = (bf16[256,1024]{1,0:T(8,128)(2,1)}, f32[4,8,24,128]{3,2,1,0:T(8,128)}, f32[8,16,256]{2,1,0:T(8,128)}) custom-call(bf16[3,256,1024]{2,1,0:T(8,128)(2,1)} %get-tuple-element.52.pre_ref, bf16[3,256,1024]{2,1,0:T(8,128)(2,1)} %get-tuple-element.53.post_ref, bf16[256,1024]{1,0:T(8,128)(2,1)} %get-tuple-element.54.x_ref, ...), custom_call_target="tpu_custom_call" | custom-call | flops 10737418240 | bytes 8388608 | tf_op jit(solution)/shard_map/pallas_call | solution.py:30
  113.3 0.0 all-to-all-done.2.got_ref
  113.3 11.8 %all_to_all.31.lows_ref = f32[8,16,256]{2,1,0:T(8,128)S(1)} all-to-all(f32[8,16,256]{2,1,0:T(8,128)} %get-tuple-element.66), channel_id=1, replica_groups=mesh['ctx'=32,'tp'=8] {'tp'}, dimensions={0} | all-to-all | bytes 262144 | tf_op jit(solution)/shard_map/all_to_all | solution.py:441
  125.2 0.0 copy-done
  125.2 0.0 copy-start.2
  125.2 1.0 copy-done.2
  126.2 0.4 shard_map.150
  126.5 16.7 %all_to_all.32.in_ref = bf16[32,24,128]{2,1,0:T(8,128)(2,1)S(1)} all-to-all(bf16[32,24,128]{2,1,0:T(8,128)(2,1)S(1)} %shard_map.150), channel_id=1, replica_groups=mesh['ctx'=32,'tp'=8] {'ctx'}, dimensions={0} | all-to-all | bytes 393216 | tf_op jit(solution)/shard_map/all_to_all | solution.py:441
  143.3 11.8 %all_to_all.33.in_ref = bf16[32,24,128]{2,1,0:T(8,128)(2,1)S(1)} all-to-all(bf16[32,24,128]{2,1,0:T(8,128)(2,1)S(1)} %shard_map.151), channel_id=1, replica_groups=mesh['ctx'=32,'tp'=8] {'ctx'}, dimensions={0} | all-to-all | bytes 393216 | tf_op jit(solution)/shard_map/all_to_all | solution.py:441
  155.1 0.8 shard_map.152
  155.9 0.6 reshape.59
  (4 shorter events, 0.1 us)
Async XLA Ops:
  6.3 8.8 %copy-start.4 = (bf16[3,3,1024]{2,1,0:T(4,128)(2,1)S(1)}, bf16[3,3,1024]{2,1,0:T(4,128)(2,1)}, u32[]{:S(2)}) copy-start(bf16[3,3,1024]{2,1,0:T(4,128)(2,1)} %param.15) | copy-start | bytes 55300
  6.3 8.9 %copy-start.1 = (bf16[256,1024]{1,0:T(8,128)(2,1)S(1)}, bf16[256,1024]{1,0:T(8,128)(2,1)}, u32[]{:S(2)}) copy-start(bf16[256,1024]{1,0:T(8,128)(2,1)} %tok_ref.3) | copy-start | bytes 1572868
  6.3 8.9 %copy-start.3 = (bf16[512,256]{1,0:T(8,128)(2,1)S(1)}, bf16[512,256]{1,0:T(8,128)(2,1)}, u32[]{:S(2)}) copy-start(bf16[512,256]{1,0:T(8,128)(2,1)} %get-tuple-element.42.sel_ref) | copy-start | bytes 786436
  6.4 49.7 %all-to-all-start = ((bf16[32,16,3200]{2,1,0:T(8,128)(2,1)}), bf16[32,16,3200]{2,1,0:T(8,128)(2,1)}, u32[]{:S(2)}, u32[]{:S(2)}) async-start(bf16[32,16,3200]{2,1,0:T(8,128)(2,1)} %get-tuple-element.40), calls=%async_computation | async-start | bytes 6553600 | tf_op jit(solution)/shard_map/all_to_all | solution.py:441
  15.1 1.5 copy-start.7
  81.7 14.3 %collective-permute-start = (bf16[144,1024]{1,0:T(8,128)(2,1)}, bf16[144,1024]{1,0:T(8,128)(2,1)S(1)}, u32[]{:S(2)}, u32[]{:S(2)}) collective-permute-start(bf16[144,1024]{1,0:T(8,128)(2,1)} %get-tuple-element.59), channel_id=1, source_target_pairs={{0,8},{8,16},{16,24},{24,32},{32,40},{40,48},{48,56},{56,64},{64,7... | collective-permute-start | bytes 884744 | tf_op jit(solution)/shard_map/ppermute | solution.py:447
  87.0 8.9 %collective-permute-start.1 = (bf16[144,1024]{1,0:T(8,128)(2,1)}, bf16[144,1024]{1,0:T(8,128)(2,1)S(1)}, u32[]{:S(2)}, u32[]{:S(2)}) collective-permute-start(bf16[144,1024]{1,0:T(8,128)(2,1)} %get-tuple-element.60), channel_id=1, source_target_pairs={{8,0},{16,8},{24,16},{32,24},{40,32},{48,40},{56,48},{64,56},{72,6... | collective-permute-start | bytes 884744 | tf_op jit(solution)/shard_map/ppermute | solution.py:447
  89.1 24.2 %all-to-all-start.2 = ((bf16[32,16,1024]{2,1,0:T(8,128)(2,1)}), bf16[32,16,1024]{2,1,0:T(8,128)(2,1)S(1)}, u32[]{:S(2)}, u32[]{:S(2)}) async-start(bf16[32,16,1024]{2,1,0:T(8,128)(2,1)} %shard_map.146), calls=%async_computation.2 | async-start | bytes 2097152 | tf_op jit(solution)/shard_map/all_to_all | solution.py:441
  96.0 0.7 copy-start.5
  96.0 0.8 copy-start.6
  96.8 28.4 %copy-start = (bf16[256,512]{1,0:T(8,128)(2,1)S(1)}, bf16[256,512]{1,0:T(8,128)(2,1)}, u32[]{:S(2)}) copy-start(bf16[256,512]{1,0:T(8,128)(2,1)} %get-tuple-element.48.place_ref) | copy-start | bytes 786436
  125.2 1.0 copy-start.2

commit v2 on v1

--- a/solution.py
+++ b/solution.py
@@ -1,3 +1,5 @@
+import functools
+
 import jax
 import jax.numpy as jnp
 from jax import lax
@@ -63,22 +65,16 @@
     return lax.broadcasted_iota(I32, shape, dim)
 
 
-def send_kernel(
-    pos_ref, frozen_ref, tok_ref, down_ref, out_ref, sel_ref,
-    in_buf, tok_buf, out_buf, extra_buf, in_sem, out_sem,
-):
+def send_kernel(pos_ref, frozen_ref, out_ref, sel_ref, in_buf, out_buf, in_sem, out_sem):
     rows = pos_ref.shape[1]
     slots = sel_ref.shape[0]
     parts, shards, cap, chans = out_buf.shape
-    rank_dim = down_ref.shape[0]
-    loads = [pltpu.make_async_copy(tok_ref, tok_buf, in_sem.at[parts])]
-    for a in range(parts):
-        loads.append(pltpu.make_async_copy(frozen_ref.at[a], in_buf.at[a], in_sem.at[a]))
+    loads = [
+        pltpu.make_async_copy(frozen_ref.at[a], in_buf.at[a], in_sem.at[a]) for a in range(parts)
+    ]
     for load in loads:
         load.start()
-    pos = pos_ref[...]
-    dest = (pos // rows).astype(F32)
-    within = (pos % rows).astype(F32)
+    dest = (pos_ref[...] // rows).astype(F32)
     dest_row = jnp.broadcast_to(dest, (rows, rows))
     dest_col = dest_row.T
     earlier = (dest_row == dest_col) & (iota((rows, rows), 0) < iota((rows, rows), 1))
@@ -88,24 +84,9 @@
         iota((slots, rows), 0).astype(F32) == jnp.broadcast_to(slot, (slots, rows)), 1.0, 0.0
     ).astype(BF)
     sel_ref[...] = sel
-    mark = jnp.where(iota((8, rows), 0) == 0, jnp.broadcast_to(within, (8, rows)), 1.0)
-    loads[0].wait()
-    low = dot(down_ref[...], tok_buf[...], 1, 1)
-    high = low.astype(BF).astype(F32)
-    rest = low - high
-    mid = rest.astype(BF).astype(F32)
-    extra = jnp.concatenate(
-        [high, mid, rest - mid, mark, jnp.zeros((128 - 8 - 3 * rank_dim, rows), F32)]
-    )
-    extra_buf[...] = dot(sel, extra.T.astype(BF)).astype(BF).reshape(shards, cap, 128)
-    stores = [
-        pltpu.make_async_copy(
-            extra_buf, out_ref.at[:, :, pl.ds(parts * chans, 128)], out_sem.at[parts]
-        )
-    ]
-    stores[0].start()
+    stores = []
     for a in range(parts):
-        loads[1 + a].wait()
+        loads[a].wait()
         for c in range(0, chans, 256):
             out_buf[a, :, :, c : c + 256] = (
                 dot(sel, in_buf[a, :, c : c + 256]).astype(BF).reshape(shards, cap, 256)
@@ -119,6 +100,10 @@
         store.wait()
 
 
+def low_kernel(tok_ref, down_ref, out_ref):
+    out_ref[...] = dot(down_ref[...], tok_ref[...], 1, 1)
+
+
 def send_tokens_kernel(sel_ref, tok_ref, out_ref):
     shards, cap, chans = out_ref.shape
     for c in range(0, chans, 256):
@@ -127,22 +112,33 @@
         )
 
 
-def place_kernel(extra_ref, place_ref, low_ref):
-    copies, rank_dim, rows = low_ref.shape
-    shards, cap, _ = extra_ref.shape
-    slots = shards * cap
-    extra = extra_ref[...].reshape(slots, 128)
-    mark = extra[:, 3 * rank_dim : 3 * rank_dim + 2].astype(F32)
-    target = jnp.where(mark[:, 1:2] > 0.5, mark[:, 0:1], -1.0)
-    place_t = jnp.where(
-        jnp.broadcast_to(target, (slots, rows)) == iota((slots, rows), 1).astype(F32), 1.0, 0.0
-    )
-    place = place_t.T.astype(BF)
-    place_ref[...] = place
-    split = dot(place, extra).T
-    low = split[:rank_dim] + split[rank_dim : 2 * rank_dim] + split[2 * rank_dim : 3 * rank_dim]
-    for t in range(copies):
-        low_ref[t] = low
+def place_kernel(cap, all_ref, shard_ref, place_ref, low_ref):
+    rows, slots = place_ref.shape
+    rank_dim = low_ref.shape[0]
+    group = 128 // cap
+    row, col = iota((rows, rows), 0), iota((rows, rows), 1)
+    before = jnp.where(row < col, 1.0, 0.0).astype(BF)
+    shard = shard_ref[0:1, 0:1]
+    low = jnp.zeros((rank_dim, rows), F32)
+    for j in range(slots // 128):
+        total = jnp.zeros((rows, 128), F32)
+        for k in range(group):
+            at = (j * group + k) * rows
+            block = all_ref[:, at : at + rows]
+            where = block[rank_dim : rank_dim + 8].astype(F32)
+            hit = jnp.where(where == shard, 1.0, 0.0)[0:1]
+            rank = dot(jnp.broadcast_to(hit, (16, rows)).astype(BF), before)[0:1]
+            target = where[1:2] * hit - (1.0 - hit)
+            sel = jnp.where(jnp.broadcast_to(target, (rows, rows)) == row.astype(F32), 1.0, 0.0)
+            sel = sel.astype(BF)
+            slot = rank + float(cap * k)
+            into = jnp.where(
+                jnp.broadcast_to(slot, (128, rows)) == iota((128, rows), 0).astype(F32), hit, 0.0
+            )
+            total = total + dot(sel, into.astype(BF), 1, 1)
+            low = low + dot(block[:rank_dim], sel, 1, 1)
+        place_ref[:, 128 * j : 128 * j + 128] = total.astype(BF)
+    low_ref[...] = low.astype(BF)
 
 
 def shifted_down(value, edge0, edge1):
@@ -153,24 +149,23 @@
 
 
 def post_kernel(
-    got0_ref, got1_ref, got2_ref, place_ref, lows_ref, up_ref, taps_ref, off_ref, cot_ref,
-    pre_ref, post_ref, x_ref, b_ref, ahead_ref, behind_ref, low_ref,
-    ahead_edge, behind_edge, low_t_ref,
+    got0_ref, got1_ref, got2_ref, place_ref, low_ref, up_ref, taps_ref, offr_ref, cot_ref,
+    pre_ref, post_ref, x_ref, b_ref, ahead_ref, behind_ref,
+    ahead_edge, behind_edge, low_t_ref, mask_ref,
 ):
     parts, rows, width = pre_ref.shape
     slots = place_ref.shape[1]
 
     @pl.when(pl.program_id(0) == 0)
     def _():
-        total = lows_ref[0]
-        for t in range(1, lows_ref.shape[0]):
-            total = total + lows_ref[t]
-        low_ref[...] = total.astype(BF)
-        low_t_ref[...] = total.T.astype(BF)
-
-    off = jnp.concatenate([off_ref[:rows]] * (width // 128), 1)
-    mask1 = jnp.where(off >= 1.0, 1.0, 0.0)
-    mask2 = jnp.where(off >= 2.0, 1.0, 0.0)
+        low_t_ref[...] = low_ref[...].astype(F32).T.astype(BF)
+        for b in range(rows // 128):
+            off = columns_of(offr_ref[:, 128 * b : 128 * b + 128])
+            mask_ref[0, 128 * b : 128 * b + 128] = jnp.where(off >= 1.0, 1.0, 0.0)
+            mask_ref[1, 128 * b : 128 * b + 128] = jnp.where(off >= 2.0, 1.0, 0.0)
+
+    mask1 = jnp.concatenate([mask_ref[0]] * (width // 128), 1)
+    mask2 = jnp.concatenate([mask_ref[1]] * (width // 128), 1)
     ahead_edge[...] = jnp.zeros_like(ahead_edge)
     behind_edge[...] = jnp.zeros_like(behind_edge)
     nothing = jnp.zeros((1, width), F32)
@@ -203,37 +198,24 @@
     behind_ref[128:] = behind_edge[...].astype(BF)
 
 
-def main_kernel(
-    pre_ref, post_ref, x_ref, b_ref, prev_ref, next_ref, cot_ref, taps_ref, skip_ref, filt_ref,
-    offc_ref, offr_ref, low_ref, up_ref,
-    mixer_ref, piece_ref, backlow_ref,
-    mfwd_ref, madj_ref, mpair_ref, frow_ref, grow_ref, fwd_ref, adj_ref, lhs_ref, rf_ref, ra_ref, rp_ref, bp_ref, total_ref,
-):
-    parts, rows, _ = pre_ref.shape
-    step = pl.program_id(0)
-    rank_dim = low_ref.shape[0]
-    blocks = rows // 128
+def columns_of(row):
+    return jnp.broadcast_to(row, (128, row.shape[1])).T
+
+
+def bank_kernel(filt_ref, offr_ref, fwd_ref, adj_ref, mfwd_ref, madj_ref, frow_ref, grow_ref):
+    blocks = offr_ref.shape[1] // 128 - 2
     sub, lane = iota((128, 128), 0), iota((128, 128), 1)
-    turn = jnp.where(sub + lane == 127, 1.0, 0.0).astype(BF)
-    @pl.when(step == 0)
+
+    @pl.when(pl.program_id(0) == 0)
     def _():
-        total_ref[...] = jnp.zeros_like(total_ref)
         for b in range(blocks + 1):
             first = 128 * b
             tall = 128 if b < blocks else 16
-            begin_col = (first + sub).astype(F32) - offc_ref[first : first + 128]
-            own = (lane <= sub) & ((first + lane).astype(F32) >= begin_col)
-            prev = (lane > sub) & ((first - 128 + lane).astype(F32) >= begin_col)
-            prev, own = jnp.where(prev, 1.0, 0.0).astype(BF), jnp.where(own, 1.0, 0.0).astype(BF)
-            mfwd_ref[first : first + tall, :128] = prev[:tall]
-            mfwd_ref[first : first + tall, 128:] = own[:tall]
-            if b < blocks:
-                mpair_ref[b, :, :128] = dot(turn, prev)
-                mpair_ref[b, :, 128:] = dot(turn, own)
-            row0 = jnp.broadcast_to(offr_ref[:, first : first + 128], (128, 128))
-            row1 = jnp.broadcast_to(offr_ref[:, first + 128 : first + 256], (128, 128))
-            begin0 = (first + lane).astype(F32) - row0
-            begin1 = (first + 128 + lane).astype(F32) - row1
+            prev, own = forward_masks(offr_ref, first)
+            mfwd_ref[first : first + tall, :128] = prev.astype(BF)[:tall]
+            mfwd_ref[first : first + tall, 128:] = own.astype(BF)[:tall]
+            begin0 = (first + lane).astype(F32) - offr_ref[:, first : first + 128]
+            begin1 = (first + 128 + lane).astype(F32) - offr_ref[:, first + 128 : first + 256]
             at = (first + sub).astype(F32)
             same = jnp.where((sub <= lane) & (at >= begin0), 1.0, 0.0).astype(BF)
             after = jnp.where((lane < sub) & (at >= begin1), 1.0, 0.0).astype(BF)
@@ -244,19 +226,6 @@
     flip = jnp.where((sub + lane) % 128 == 0, 1.0, 0.0).astype(BF)
     frow_ref[...] = filt.astype(F32)
     grow_ref[...] = dot(filt, flip)
-    mask1 = jnp.where(offc_ref[:rows] >= 1.0, 1.0, 0.0)
-    mask2 = jnp.where(offc_ref[:rows] >= 2.0, 1.0, 0.0)
-    next1 = jnp.where(offc_ref[rows : rows + 16] >= 1.0, 1.0, 0.0)
-    next2 = jnp.where(offc_ref[rows : rows + 16] >= 2.0, 1.0, 0.0)
-    low = low_ref[...]
-    row = iota((rows, 128), 0)
-    top = iota((16, 128), 0) < 2
-    lane_group = lane // 16
-    piece_ref[...] = jnp.zeros_like(piece_ref)
-
-    def tap(s, a):
-        return taps_ref[s * parts + a : s * parts + a + 1]
-
     for g in range(8):
         f_row = jnp.broadcast_to(frow_ref[g : g + 1, :], (128, 128))
         g_row = jnp.broadcast_to(grow_ref[g : g + 1, :], (128, 128))
@@ -266,8 +235,54 @@
         for b in range(blocks + 1):
             tall = 128 if b < blocks else 16
             at = 1024 * b + tall * g
-            fwd_ref[at : at + tall] = two_t[:tall] * mfwd_ref[128 * b : 128 * b + tall]
-            adj_ref[at : at + tall] = two[:tall] * madj_ref[128 * b : 128 * b + tall]
+            fwd_ref[0, at : at + tall] = two_t[:tall] * mfwd_ref[128 * b : 128 * b + tall]
+            adj_ref[0, at : at + tall] = two[:tall] * madj_ref[128 * b : 128 * b + tall]
+
+
+def forward_masks(offr_ref, first):
+    sub, lane = iota((128, 128), 0), iota((128, 128), 1)
+    begin = (first + sub).astype(F32) - columns_of(offr_ref[:, first : first + 128])
+    own = (lane <= sub) & ((first + lane).astype(F32) >= begin)
+    prev = (lane > sub) & ((first - 128 + lane).astype(F32) >= begin)
+    return jnp.where(prev, 1.0, 0.0), jnp.where(own, 1.0, 0.0)
+
+
+def main_kernel(
+    pre_ref, post_ref, x_ref, b_ref, prev_ref, next_ref, cot_ref, taps_ref, skip_ref, fwd_ref, adj_ref,
+    offr_ref, low_ref, up_ref,
+    mixer_ref, piece_ref, backlow_ref,
+    mpair_ref, mask_ref, lhs_ref, rf_ref, ra_ref, rp_ref, bp_ref, total_ref,
+):
+    parts, rows, _ = pre_ref.shape
+    step = pl.program_id(0)
+    rank_dim = low_ref.shape[0]
+    blocks = rows // 128
+    sub, lane = iota((128, 128), 0), iota((128, 128), 1)
+    turn = jnp.where(sub + lane == 127, 1.0, 0.0).astype(BF)
+
+    @pl.when(step == 0)
+    def _():
+        total_ref[...] = jnp.zeros_like(total_ref)
+        for b in range(blocks):
+            prev, own = forward_masks(offr_ref, 128 * b)
+            mpair_ref[b, :, :128] = dot(turn, prev.astype(BF))
+            mpair_ref[b, :, 128:] = dot(turn, own.astype(BF))
+        for b in range(blocks + 1):
+            off = columns_of(offr_ref[:, 128 * b : 128 * b + 128])
+            mask_ref[0, 128 * b : 128 * b + 128] = jnp.where(off >= 1.0, 1.0, 0.0)
+            mask_ref[1, 128 * b : 128 * b + 128] = jnp.where(off >= 2.0, 1.0, 0.0)
+
+    mask1, mask2 = mask_ref[0, :rows], mask_ref[1, :rows]
+    next1, next2 = mask_ref[0, rows : rows + 16], mask_ref[1, rows : rows + 16]
+    low = low_ref[...]
+    row = iota((rows, 128), 0)
+    top = iota((16, 128), 0) < 2
+    lane_group = lane // 16
+    piece_ref[...] = jnp.zeros_like(piece_ref)
+
+    def tap(s, a):
+        return taps_ref[s * parts + a : s * parts + a + 1]
+
     pedge = prev_ref[128:].astype(F32)
     nedge = next_ref[128:].astype(F32)
     heads, after = [], []
@@ -301,17 +316,14 @@
     for b in range(blocks + 1):
         at = slice(1024 * b, 1024 * b + (1024 if b < blocks else 128))
         xw = x_win[128 * b : 128 * b + 256]
-        rf_ref[at] = dot(fwd_ref[at], xw)
-        ra_ref[at] = dot(adj_ref[at], b_win[128 * b : 128 * b + 256])
-        if b < blocks:
-            back = dot(turn, b_win[128 * b : 128 * b + 128])
-            for g in range(8):
-                lhs_ref[128 * g : 128 * g + 128] = jnp.where(lane_group == g, back, 0.0).astype(BF)
-            rp_ref[b] = dot(lhs_ref[...], xw, 1, 1)
+        rf_ref[at] = dot(fwd_ref[0, at], xw)
+        ra_ref[at] = dot(adj_ref[0, at], b_win[128 * b : 128 * b + 256])
+    backs = [dot(turn, b_win[128 * b : 128 * b + 128]) for b in range(blocks)]
     for g in range(8):
         part = jnp.zeros((128, 128), F32)
         for b in range(blocks):
-            pair = rp_ref[b, 128 * g : 128 * g + 128] * mpair_ref[b]
+            lhs = jnp.where(lane_group == g, backs[b], 0.0).astype(BF)
+            pair = dot(lhs, x_win[128 * b : 128 * b + 256], 1, 1) * mpair_ref[b]
             part = part + pair[:, :128] + pair[:, 128:]
         part = pltpu.roll(part, 0, 1, stride=1, stride_axis=0)
         piece_ref[3, 0, 8 + g : 9 + g] = jnp.sum(part, axis=0, keepdims=True)
@@ -431,8 +443,9 @@
         up_ref[0, 8:, cols] = part[1][:8]
         up_ref[1, :, cols] = part[1][8:]
         up_ref[2, :, cols] = part[2][:16]
-        short_ref[:8, cols] = part[2][16:]
-        short_ref[8:9, cols] = part[3][0:1]
+        for k in range(9):
+            row = part[2][16 + k : 17 + k] if k < 8 else part[3][0:1]
+            short_ref[k // 3, k % 3 : k % 3 + 1, cols] = row
         gskip_ref[i : i + 1] = part[3][1:2]
         long_ref[8 * i : 8 * i + 8] = dot(part[3][8:16].astype(BF), flip)
 
@@ -445,6 +458,10 @@
     count = lax.axis_size("ctx")
     pairs = [(i, i + steps) for i in range(count) if 0 <= i + steps < count]
     return lax.ppermute(value, "ctx", pairs)
+
+
+def partner(value, axis, bit):
+    return lax.ppermute(value, axis, [(i, i ^ bit) for i in range(lax.axis_size(axis))])
 
 
 def doc_offsets(positions, lengths):
@@ -482,68 +499,83 @@
     send, sel = pl.pallas_call(
         send_kernel,
         out_shape=(
-            jax.ShapeDtypeStruct((shards, cap, parts * chans + 128), BF),
+            jax.ShapeDtypeStruct((shards, cap, parts * chans), BF),
             jax.ShapeDtypeStruct((slots, rows), BF),
         ),
-        in_specs=[vmem, far, far, vmem],
+        in_specs=[vmem, far],
         out_specs=(far, vmem),
         scratch_shapes=[
             pltpu.VMEM((parts, rows, chans), BF),
-            pltpu.VMEM((rows, chans), BF),
             pltpu.VMEM((parts, shards, cap, chans), BF),
-            pltpu.VMEM((shards, cap, 128), BF),
-            pltpu.SemaphoreType.DMA((parts + 1,)),
-            pltpu.SemaphoreType.DMA((parts + 1,)),
+            pltpu.SemaphoreType.DMA((parts,)),
+            pltpu.SemaphoreType.DMA((parts,)),
         ],
         compiler_params=pltpu.CompilerParams(vmem_limit_bytes=66_000_000),
         cost_estimate=pl.CostEstimate(flops=1 << 30, bytes_accessed=5 << 20, transcendentals=0),
-    )(pos_row, frozen, tokens, adapter_down_weight)
+    )(pos_row, frozen)
     got = swap(send, "ctx")
 
-    send, sel, document_lengths, short_depthwise_filter = lax.optimization_barrier(
-        (send, sel, document_lengths, short_depthwise_filter)
-    )
+    send, sel, document_lengths, short_depthwise_filter, adapter_down_weight = lax.optimization_barrier(
+        (send, sel, document_lengths, short_depthwise_filter, adapter_down_weight)
+    )
+    (low_sum,) = whole(low_kernel, [((rank_dim, rows), F32)], flops=1 << 23, nbytes=1 << 19)(
+        tokens, adapter_down_weight
+    )
+    for bit in range(3):
+        low_sum = low_sum + partner(low_sum, "tp", 1 << bit)
+    where = jnp.concatenate([pos_row // rows, pos_row % rows]).astype(BF)
+    packet = jnp.concatenate([low_sum.astype(BF), where, jnp.zeros((6, rows), BF)])
+    packets = lax.all_gather(packet, "ctx", axis=1, tiled=True)
+    shard = jnp.full((1, 128), lax.axis_index("ctx"), F32)
+    place, low = whole(
+        functools.partial(place_kernel, cap),
+        [((rows, slots), BF), ((rank_dim, rows), BF)],
+        flops=1 << 30,
+        nbytes=1 << 20,
+    )(packets, shard)
     (send_tok,) = whole(
         send_tokens_kernel, [((shards, cap, chans), BF)], flops=2 * slots * rows * chans, nbytes=2 << 20
     )(sel, tokens)
     first = lax.axis_index("ctx") * rows
     offsets = doc_offsets(first + jnp.arange(rows + 256, dtype=I32), document_lengths).astype(F32)
     off_row = offsets.reshape(1, rows + 256)
-    off_col = jnp.broadcast_to(offsets[:, None], (rows + 256, 128))
     tap_rows = short_depthwise_filter.reshape(taps * parts, chans).astype(F32)
     tap_rows = jnp.pad(tap_rows, ((0, 16 - taps * parts), (0, 0)))
     skip_row = skip_direct_scale.reshape(1, chans)
-    got, send_tok, off_row, off_col, tap_rows = lax.optimization_barrier(
-        (got, send_tok, off_row, off_col, tap_rows)
-    )
-
-    place, low_parts = tiled(
-        place_kernel,
-        1,
-        [((shards, cap, 128), lambda i: (0, 0, parts * chans // 128))],
-        [
-            ((rows, slots), BF, (rows, slots), fixed2),
-            ((columns, rank_dim, rows), F32, (columns, rank_dim, rows), lambda i: (0, 0, 0)),
-        ],
-        [],
-        1 << 26,
-        1 << 19,
+    blocks = rows // 128
+    tall = 1024 * blocks + 128
+    tiles = chans // 128
+    fwd_bank, adj_bank = tiled(
+        bank_kernel,
+        tiles,
+        [((8, 128), lambda i: (i, 0)), ((1, rows + 256), fixed2)],
+        [((tiles, tall, 256), BF, (1, tall, 256), lambda i: (i, 0, 0))] * 2,
+        [
+            pltpu.VMEM((128 * blocks + 16, 256), BF),
+            pltpu.VMEM((128 * blocks + 16, 256), BF),
+            pltpu.VMEM((8, 128), F32),
+            pltpu.VMEM((8, 128), F32),
+        ],
+        1 << 30,
+        18 << 20,
         60_000_000,
-    )(got)
-    lows = swap(low_parts, "tp")
-    got, lows = lax.optimization_barrier((got, lows))
+    )(long_group_filter, off_row)
+    got, send_tok, off_row, fwd_bank, adj_bank, tap_rows, place, low = lax.optimization_barrier(
+        (got, send_tok, off_row, fwd_bank, adj_bank, tap_rows, place, low)
+    )
+
     wide = 256
     steps = chans // wide
-    pre, post, x, back, ahead, behind, low = tiled(
+    pre, post, x, back, ahead, behind = tiled(
         post_kernel,
         steps,
         [((shards, cap, wide), lambda i, a=a: (0, 0, a * steps + i)) for a in range(parts)]
         + [
             ((rows, slots), fixed2),
-            ((columns, rank_dim, rows), lambda i: (0, 0, 0)),
+            ((rank_dim, rows), fixed2),
             ((parts, rank_dim, wide), at3),
             ((16, wide), at2),
-            ((rows + 256, 128), fixed2),
+            ((1, rows + 256), fixed2),
             ((rows, wide), at2),
         ],
         [
@@ -553,23 +585,21 @@
             ((rows, chans), BF, (rows, wide), at2),
             ((144, chans), BF, (144, wide), at2),
             ((144, chans), BF, (144, wide), at2),
-            ((rank_dim, rows), BF, (rank_dim, rows), fixed2),
         ],
         [
             pltpu.VMEM((16, wide), F32),
             pltpu.VMEM((16, wide), F32),
             pltpu.VMEM((rows, rank_dim), BF),
+            pltpu.VMEM((2, rows, 128), F32),
         ],
         1 << 30,
         8 << 20,
         60_000_000,
-    )(got, got, got, place, lows, up, tap_rows, off_col, cotangent)
+    )(got, got, got, place, low, up, tap_rows, off_row, cotangent)
     send_tok, ahead, behind = lax.optimization_barrier((send_tok, ahead, behind))
     from_prev = neighbour(ahead, 1)
     from_next = neighbour(behind, -1)
     got_tok = swap(send_tok, "ctx")
-    blocks = rows // 128
-    tall = 1024 * blocks + 128
     mixer, sums, back_low_part = tiled(
         main_kernel,
         chans // 128,
@@ -583,8 +613,8 @@
             ((rows, 128), at2),
             ((16, 128), at2),
             ((1, 128), at2),
-            ((8, 128), lambda i: (i, 0)),
-            ((rows + 256, 128), fixed2),
+            ((1, tall, 256), lambda i: (i, 0, 0)),
+            ((1, tall, 256), lambda i: (i, 0, 0)),
             ((1, rows + 256), fixed2),
             ((rank_dim, rows), fixed2),
             ((parts, rank_dim, 128), at3),
@@ -595,13 +625,8 @@
             ((columns, rank_dim, rows), F32, (columns, rank_dim, rows), lambda i: (0, 0, 0)),
         ],
         [
-            pltpu.VMEM((128 * blocks + 16, 256), BF),
-            pltpu.VMEM((128 * blocks + 16, 256), BF),
             pltpu.VMEM((blocks, 128, 256), F32),
-            pltpu.VMEM((8, 128), F32),
-            pltpu.VMEM((8, 128), F32),
-            pltpu.VMEM((tall, 256), BF),
-            pltpu.VMEM((tall, 256), BF),
+            pltpu.VMEM((2, rows + 128, 128), F32),
             pltpu.VMEM((1024, 128), BF),
             pltpu.VMEM((tall, 128), F32),
             pltpu.VMEM((tall, 128), F32),
@@ -612,8 +637,8 @@
         10 << 30,
         8 << 20,
         60_000_000,
-    )(pre, post, x, back, from_prev, from_next, cotangent, tap_rows, skip_row, long_group_filter,
-      off_col, off_row, low, up)
+    )(pre, post, x, back, from_prev, from_next, cotangent, tap_rows, skip_row, fwd_bank, adj_bank,
+      off_row, low, up)
     got_tok, back_low_part = lax.optimization_barrier((got_tok, back_low_part))
     back_lows = swap(back_low_part, "tp")
     (pieces,) = whole(
@@ -627,7 +652,7 @@
         [
             ((rank_dim, chans), F32),
             ((parts, rank_dim, chans), F32),
-            ((taps * parts, chans), F32),
+            ((taps, parts, chans), F32),
             ((groups, 128), F32),
             ((chans // 128, 128), F32),
         ],
@@ -638,7 +663,7 @@
         mixer,
         grad_down,
         up_gradient.transpose(1, 0, 2),
-        grad_short.reshape(taps, parts, chans),
+        grad_short,
         grad_long,
         grad_skip.reshape(chans),
     )

time: 157 us -> 159 us (1.013)
  waiting for transfers between devices: 38 us -> 0.81 us
  blocking collectives: 56.7 us -> 78.4 us
  Pallas kernels: 33.4 us -> 42.8 us
  starting transfers between devices: 23 us -> 30.7 us
    all_to_all x2, waiting for transfers between devices: 37.9 us -> 0.54 us  [swap(): return lax.all_to_all(value, axis, split_axis=0, concat_axis=0, tiled=True)]
    all_gather x0 -> x1, blocking collectives: none -> 33.2 us  [on_device(): packets = lax.all_gather(packet, 'ctx', axis=1, tiled=True)]
    all_to_all x4 -> x3, blocking collectives: 56.7 us -> 45.1 us  [swap(): return lax.all_to_all(value, axis, split_axis=0, concat_axis=0, tiled=True)]
    ppermute x0 -> x3, starting transfers between devices: none -> 9.64 us  [partner(): lax.ppermute(value, axis, [(i, i ^ bit) for i in range(lax.axis_size(axis...]
    pallas_call x3, Pallas kernels: 25.1 us -> 30.7 us  [call(): pl.pallas_call(kernel, grid=(grid,), out_shape=tuple((jax.ShapeDtypeStruc...]
    pallas_call x4 -> x6, Pallas kernels: 2.61 us -> 7.36 us  [call(): pl.pallas_call(kernel, out_shape=tuple((jax.ShapeDtypeStruct(s, d) for s,...]
    ppermute x2, starting transfers between devices: 7.42 us -> 4.34 us  [neighbour(): return lax.ppermute(value, 'ctx', pairs)]
  transfers between devices with their start and end apart: 4 -> 7, of which waited for: 1 -> 2; matrix products, arithmetic and copies ran while one was open for 1% -> 1% of each run, Pallas kernels for 11% -> 19%
where the time goes in v2:
time: 159 us; the launch traced here: 158 us
  blocking collectives  78.4 us (49%)
  Pallas kernels  42.8 us (27%)
  starting transfers between devices  30.7 us (19%)
  local copies, waits for them, and re-layouts  3.24 us (2%)
    all_to_all x3, blocking collectives, swap(): return lax.all_to_all(value, axis, split_axis=0, concat_axis=0, tiled=True)  45.1 us
    all_gather x1, blocking collectives, on_device(): packets = lax.all_gather(packet, 'ctx', axis=1, tiled=True)  33.2 us
    pallas_call x3, Pallas kernels, call(): pl.pallas_call(kernel, grid=(grid,), out_shape=tuple((jax.ShapeDtypeStruc...  30.7 us
    all_to_all x2, starting transfers between devices, swap(): return lax.all_to_all(value, axis, split_axis=0, concat_axis=0, tiled=True)  16.8 us
    ppermute x3, starting transfers between devices, partner(): lax.ppermute(value, axis, [(i, i ^ bit) for i in range(lax.axis_size(axis...  9.64 us
    pallas_call x6, Pallas kernels, call(): pl.pallas_call(kernel, out_shape=tuple((jax.ShapeDtypeStruct(s, d) for s,...  7.36 us
    pallas_call x1, Pallas kernels, on_device(): pl.pallas_call(send_kernel, out_shape=(jax.ShapeDtypeStruct((shards, cap,...  4.81 us
    ppermute x2, starting transfers between devices, neighbour(): return lax.ppermute(value, 'ctx', pairs)  4.34 us
  transfers between devices with their start and end apart: 7, of which 2 were waited for; matrix products, arithmetic and copies ran while one was open for 1% of the time, Pallas kernels for 19%

profile of v2, /device:TPU:1, one launch (start us, length us, event | category | flops | bytes accessed | tf_op | source)
XLA Modules:
  0.0 158.4 jit_solution(8015365909843550946)
XLA Ops:
  0.6 4.8 %shard_map.145 = (bf16[32,16,3072]{2,1,0:T(8,128)(2,1)}, bf16[512,256]{1,0:T(8,128)(2,1)}) custom-call(s32[1,256]{1,0:T(1,128)} %bitcast.10, bf16[3,256,1024]{2,1,0:T(8,128)(2,1)} %bitcast.11), custom_call_target="tpu_custom_call" | custom-call | flops 1073741824 | bytes 5242880 | tf_op jit(solution)/shard_map/pallas_call | solution.py:499
  5.5 0.0 copy-start
  5.5 0.0 copy-start.5
  5.5 0.0 copy-start.7
  5.5 0.0 copy-start.11
  5.5 0.0 copy-start.8
  5.5 8.8 %all-to-all-start = ((bf16[32,16,3072]{2,1,0:T(8,128)(2,1)}), bf16[32,16,3072]{2,1,0:T(8,128)(2,1)}, u32[]{:S(2)}, u32[]{:S(2)}) async-start(bf16[32,16,3072]{2,1,0:T(8,128)(2,1)} %get-tuple-element.43), calls=%async_computation | async-start | bytes 6291456 | tf_op jit(solution)/shard_map/all_to_all | solution.py:454
  14.3 0.0 copy-start.4
  14.3 0.0 copy-done
  14.4 0.0 copy-done.5
  14.4 0.2 shard_map.148
  14.6 1.6 %collective-permute-start = (f32[16,256]{1,0:T(8,128)S(1)}, f32[16,256]{1,0:T(8,128)S(1)}, u32[]{:S(2)}, u32[]{:S(2)}) collective-permute-start(f32[16,256]{1,0:T(8,128)S(1)} %shard_map.148), channel_id=1, source_target_pairs={{0,1},{1,0},{2,3},{3,2},{4,5},{5,4},{6,7},{7,6},{8,9},{9,8},{10,11... | collective-permute-start | bytes 49160 | tf_op jit(solution)/shard_map/ppermute | solution.py:464
  16.2 0.0 copy-done.7
  16.3 0.1 select_reduce_fusion.1
  16.4 0.1 select_reduce_fusion
  16.5 0.6 subtract_convert_fusion.offr_ref
  17.1 0.6 pad_convert_fusion.taps_ref
  17.7 0.0 collective-permute-done
  17.7 3.1 %collective-permute-start.1 = (f32[16,256]{1,0:T(8,128)S(1)}, f32[16,256]{1,0:T(8,128)S(1)}, u32[]{:S(2)}, u32[]{:S(2)}) collective-permute-start(f32[16,256]{1,0:T(8,128)S(1)} %add.45), channel_id=1, source_target_pairs={{0,2},{1,3},{2,0},{3,1},{4,6},{5,7},{6,4},{7,5},{8,10},{9,11},{10,... | collective-permute-start | bytes 49160 | tf_op jit(solution)/shard_map/ppermute | solution.py:464
  20.8 8.7 %shard_map.147 = (bf16[8,2176,256]{2,1,0:T(8,128)(2,1)}, bf16[8,2176,256]{2,1,0:T(8,128)(2,1)}) custom-call(bf16[64,128]{1,0:T(8,128)(2,1)} %filt_ref.1, f32[1,512]{1,0:T(1,128)} %subtract_convert_fusion.offr_ref), custom_call_target="tpu_custom_call" | custom-call | flops 1073741824 | bytes 18874368 | tf_op jit(solution)/shard_map/pallas_call | solution.py:32
  29.5 0.1 pad.12.clone
  29.6 0.0 collective-permute-done.1
  29.6 4.9 %collective-permute-start.2 = (f32[16,256]{1,0:T(8,128)S(1)}, f32[16,256]{1,0:T(8,128)S(1)}, u32[]{:S(2)}, u32[]{:S(2)}) collective-permute-start(f32[16,256]{1,0:T(8,128)S(1)} %add.46), channel_id=1, source_target_pairs={{0,4},{1,5},{2,6},{3,7},{4,0},{5,1},{6,2},{7,3},{8,12},{9,13},{10,... | collective-permute-start | bytes 49160 | tf_op jit(solution)/shard_map/ppermute | solution.py:464
  34.5 1.5 shard_map.146
  36.0 0.3 collective-permute-done.2
  36.3 0.1 maximum_maximum_fusion
  36.4 33.2 %all_gather.3.all_ref = bf16[24,8192]{1,0:T(8,128)(2,1)S(1)} all-gather(bf16[24,256]{1,0:T(8,128)(2,1)S(1)} %maximum_maximum_fusion), channel_id=1, replica_groups=mesh['ctx'=32,'tp'=8] {'ctx'}, dimensions={1}, use_global_device_ids=true | all-gather | bytes 405504 | tf_op jit(solution)/shard_map/all_gather | solution.py:528
  69.6 4.4 %shard_map.149 = (bf16[256,512]{1,0:T(8,128)(2,1)S(1)}, bf16[16,256]{1,0:T(8,128)(2,1)S(1)}) custom-call(bf16[24,8192]{1,0:T(8,128)(2,1)S(1)} %all_gather.3.all_ref, f32[1,128]{1,0:T(1,128)S(1)} %broadcast_in_dim.38.shard_ref), custom_call_target="tpu_custom_call" | custom-call | flops 1073741824 | bytes 1048576 | tf_op jit(solution)/shard_map/pallas_call | solution.py:17
  74.1 0.0 copy-start.1
  74.1 0.7 copy-done.1
  74.8 0.6 copy-done.6
  75.4 0.0 all-to-all-done.got0_ref.got1_ref.got2_ref
  75.4 6.3 %shard_map.150 = (bf16[3,256,1024]{2,1,0:T(8,128)(2,1)}, bf16[3,256,1024]{2,1,0:T(8,128)(2,1)}, bf16[256,1024]{1,0:T(8,128)(2,1)}, bf16[256,1024]{1,0:T(8,128)(2...) custom-call(bf16[32,16,3072]{2,1,0:T(8,128)(2,1)} %all-to-all-done.got0_ref.got1_ref.got2_ref, ...), custom_call_target="tpu_custom_call" | custom-call | flops 1073741824 | bytes 8388608 | tf_op jit(solution)/shard_map/pallas_call | solution.py:32
  81.7 1.9 %collective-permute-start.3 = (bf16[144,1024]{1,0:T(8,128)(2,1)}, bf16[144,1024]{1,0:T(8,128)(2,1)S(1)}, u32[]{:S(2)}, u32[]{:S(2)}) collective-permute-start(bf16[144,1024]{1,0:T(8,128)(2,1)} %get-tuple-element.65), channel_id=1, source_target_pairs={{0,8},{8,16},{16,24},{24,32},{32,40},{40,48},{48,56},{56,64},{64,7... | collective-permute-start | bytes 884744 | tf_op jit(solution)/shard_map/ppermute | solution.py:460
  83.6 2.4 %collective-permute-start.4 = (bf16[144,1024]{1,0:T(8,128)(2,1)}, bf16[144,1024]{1,0:T(8,128)(2,1)S(1)}, u32[]{:S(2)}, u32[]{:S(2)}) collective-permute-start(bf16[144,1024]{1,0:T(8,128)(2,1)} %get-tuple-element.66), channel_id=1, source_target_pairs={{8,0},{16,8},{24,16},{32,24},{40,32},{48,40},{56,48},{64,56},{72,6... | collective-permute-start | bytes 884744 | tf_op jit(solution)/shard_map/ppermute | solution.py:460
  86.0 7.9 %all-to-all-start.1 = ((bf16[32,16,1024]{2,1,0:T(8,128)(2,1)}), bf16[32,16,1024]{2,1,0:T(8,128)(2,1)S(1)}, u32[]{:S(2)}, u32[]{:S(2)}) async-start(bf16[32,16,1024]{2,1,0:T(8,128)(2,1)} %shard_map.146), calls=%async_computation.1 | async-start | bytes 2097152 | tf_op jit(solution)/shard_map/all_to_all | solution.py:454
  94.0 0.0 collective-permute-done.3.prev_ref
  94.0 0.0 collective-permute-done.4.next_ref
  94.0 0.7 copy-done.9
  94.7 0.1 copy-done.10
  94.8 15.7 %shard_map.151 = (bf16[256,1024]{1,0:T(8,128)(2,1)}, f32[4,8,24,128]{3,2,1,0:T(8,128)}, f32[8,16,256]{2,1,0:T(8,128)}) custom-call(bf16[3,256,1024]{2,1,0:T(8,128)(2,1)} %get-tuple-element.58.pre_ref, bf16[3,256,1024]{2,1,0:T(8,128)(2,1)} %get-tuple-element.59.post_ref, bf16[256,1024]{1,0:T(8,128)(2,1)} %get-tuple-element.60.x_ref, ...), custom_call_target="tpu_custom_call" | custom-call | flops 10737418240 | bytes 8388608 | tf_op jit(solution)/shard_map/pallas_call | solution.py:32
  110.5 0.5 all-to-all-done.1.got_ref
  111.0 16.0 %all_to_all.25.lows_ref = f32[8,16,256]{2,1,0:T(8,128)S(1)} all-to-all(f32[8,16,256]{2,1,0:T(8,128)} %get-tuple-element.72), channel_id=1, replica_groups=mesh['ctx'=32,'tp'=8] {'tp'}, dimensions={0} | all-to-all | bytes 262144 | tf_op jit(solution)/shard_map/all_to_all | solution.py:454
  127.0 1.0 copy-done.3
  128.0 0.4 shard_map.152
  128.3 17.3 %all_to_all.26.in_ref = bf16[32,24,128]{2,1,0:T(8,128)(2,1)S(1)} all-to-all(bf16[32,24,128]{2,1,0:T(8,128)(2,1)S(1)} %shard_map.152), channel_id=1, replica_groups=mesh['ctx'=32,'tp'=8] {'ctx'}, dimensions={0} | all-to-all | bytes 393216 | tf_op jit(solution)/shard_map/all_to_all | solution.py:454
  145.7 11.8 %all_to_all.27.in_ref = bf16[32,24,128]{2,1,0:T(8,128)(2,1)S(1)} all-to-all(bf16[32,24,128]{2,1,0:T(8,128)(2,1)S(1)} %shard_map.153), channel_id=1, replica_groups=mesh['ctx'=32,'tp'=8] {'ctx'}, dimensions={0} | all-to-all | bytes 393216 | tf_op jit(solution)/shard_map/all_to_all | solution.py:454
  157.6 0.8 shard_map.154
  (20 shorter events, 0.1 us)
Async XLA Ops:
  5.5 8.9 %copy-start = (bf16[256,1024]{1,0:T(8,128)(2,1)S(1)}, bf16[256,1024]{1,0:T(8,128)(2,1)}, u32[]{:S(2)}) copy-start(bf16[256,1024]{1,0:T(8,128)(2,1)} %tok_ref.3) | copy-start | bytes 1572868
  5.5 8.9 %copy-start.5 = (bf16[16,1024]{1,0:T(8,128)(2,1)S(1)}, bf16[16,1024]{1,0:T(8,128)(2,1)}, u32[]{:S(2)}) copy-start(bf16[16,1024]{1,0:T(8,128)(2,1)} %down_ref) | copy-start | bytes 98308
  5.5 10.7 %copy-start.7 = (bf16[3,3,1024]{2,1,0:T(4,128)(2,1)S(1)}, bf16[3,3,1024]{2,1,0:T(4,128)(2,1)}, u32[]{:S(2)}) copy-start(bf16[3,3,1024]{2,1,0:T(4,128)(2,1)} %param.15) | copy-start | bytes 55300
  5.5 10.8 %copy-start.11 = (s32[64]{0:T(128)S(1)}, s32[64]{0:T(128)}, u32[]{:S(2)}) copy-start(s32[64]{0:T(128)} %param.18) | copy-start | bytes 772
  5.5 11.0 %copy-start.8 = (s32[256]{0:T(256)S(1)}, s32[256]{0:T(256)}, u32[]{:S(2)}) copy-start(s32[256]{0:T(256)} %param.19) | copy-start | bytes 3076
  5.5 69.9 %all-to-all-start = ((bf16[32,16,3072]{2,1,0:T(8,128)(2,1)}), bf16[32,16,3072]{2,1,0:T(8,128)(2,1)}, u32[]{:S(2)}, u32[]{:S(2)}) async-start(bf16[32,16,3072]{2,1,0:T(8,128)(2,1)} %get-tuple-element.43), calls=%async_computation | async-start | bytes 6291456 | tf_op jit(solution)/shard_map/all_to_all | solution.py:454
  14.3 20.2 %copy-start.4 = (bf16[512,256]{1,0:T(8,128)(2,1)S(1)}, bf16[512,256]{1,0:T(8,128)(2,1)}, u32[]{:S(2)}) copy-start(bf16[512,256]{1,0:T(8,128)(2,1)} %get-tuple-element.45.sel_ref) | copy-start | bytes 786436
  14.6 3.2 %collective-permute-start = (f32[16,256]{1,0:T(8,128)S(1)}, f32[16,256]{1,0:T(8,128)S(1)}, u32[]{:S(2)}, u32[]{:S(2)}) collective-permute-start(f32[16,256]{1,0:T(8,128)S(1)} %shard_map.148), channel_id=1, source_target_pairs={{0,1},{1,0},{2,3},{3,2},{4,5},{5,4},{6,7},{7,6},{8,9},{9,8},{10,11... | collective-permute-start | bytes 49160 | tf_op jit(solution)/shard_map/ppermute | solution.py:464
  17.7 11.9 %collective-permute-start.1 = (f32[16,256]{1,0:T(8,128)S(1)}, f32[16,256]{1,0:T(8,128)S(1)}, u32[]{:S(2)}, u32[]{:S(2)}) collective-permute-start(f32[16,256]{1,0:T(8,128)S(1)} %add.45), channel_id=1, source_target_pairs={{0,2},{1,3},{2,0},{3,1},{4,6},{5,7},{6,4},{7,5},{8,10},{9,11},{10,... | collective-permute-start | bytes 49160 | tf_op jit(solution)/shard_map/ppermute | solution.py:464
  29.6 6.7 %collective-permute-start.2 = (f32[16,256]{1,0:T(8,128)S(1)}, f32[16,256]{1,0:T(8,128)S(1)}, u32[]{:S(2)}, u32[]{:S(2)}) collective-permute-start(f32[16,256]{1,0:T(8,128)S(1)} %add.46), channel_id=1, source_target_pairs={{0,4},{1,5},{2,6},{3,7},{4,0},{5,1},{6,2},{7,3},{8,12},{9,13},{10,... | collective-permute-start | bytes 49160 | tf_op jit(solution)/shard_map/ppermute | solution.py:464
  74.1 0.7 copy-start.1
  74.8 0.6 copy-start.6
  81.7 12.3 %collective-permute-start.3 = (bf16[144,1024]{1,0:T(8,128)(2,1)}, bf16[144,1024]{1,0:T(8,128)(2,1)S(1)}, u32[]{:S(2)}, u32[]{:S(2)}) collective-permute-start(bf16[144,1024]{1,0:T(8,128)(2,1)} %get-tuple-element.65), channel_id=1, source_target_pairs={{0,8},{8,16},{16,24},{24,32},{32,40},{40,48},{48,56},{56,64},{64,7... | collective-permute-start | bytes 884744 | tf_op jit(solution)/shard_map/ppermute | solution.py:460
  83.6 10.4 %collective-permute-start.4 = (bf16[144,1024]{1,0:T(8,128)(2,1)}, bf16[144,1024]{1,0:T(8,128)(2,1)S(1)}, u32[]{:S(2)}, u32[]{:S(2)}) collective-permute-start(bf16[144,1024]{1,0:T(8,128)(2,1)} %get-tuple-element.66), channel_id=1, source_target_pairs={{8,0},{16,8},{24,16},{32,24},{40,32},{48,40},{56,48},{64,56},{72,6... | collective-permute-start | bytes 884744 | tf_op jit(solution)/shard_map/ppermute | solution.py:460
  86.0 25.0 %all-to-all-start.1 = ((bf16[32,16,1024]{2,1,0:T(8,128)(2,1)}), bf16[32,16,1024]{2,1,0:T(8,128)(2,1)S(1)}, u32[]{:S(2)}, u32[]{:S(2)}) async-start(bf16[32,16,1024]{2,1,0:T(8,128)(2,1)} %shard_map.146), calls=%async_computation.1 | async-start | bytes 2097152 | tf_op jit(solution)/shard_map/all_to_all | solution.py:454
  94.0 0.7 copy-start.9
  94.0 0.8 copy-start.10
  94.8 32.2 %copy-start.2 = (bf16[256,512]{1,0:T(8,128)(2,1)S(1)}, bf16[256,512]{1,0:T(8,128)(2,1)}, u32[]{:S(2)}) copy-start(bf16[256,512]{1,0:T(8,128)(2,1)} %copy-done.1) | copy-start | bytes 786436
  127.0 1.0 copy-start.3

commit v3 on v2

--- a/solution.py
+++ b/solution.py
@@ -1,5 +1,3 @@
-import functools
-
 import jax
 import jax.numpy as jnp
 from jax import lax
@@ -104,6 +102,15 @@
     out_ref[...] = dot(down_ref[...], tok_ref[...], 1, 1)
 
 
+def send_low_kernel(sel_ref, pos_ref, low_ref, out_ref):
+    shards, cap, _ = out_ref.shape
+    rank_dim, rows = low_ref.shape
+    within = jnp.broadcast_to((pos_ref[...] % rows).astype(F32), (8, rows))
+    mark = jnp.where(iota((8, rows), 0) == 0, within, 1.0)
+    extra = jnp.concatenate([low_ref[...], mark, jnp.zeros((128 - 8 - rank_dim, rows), F32)])
+    out_ref[...] = dot(sel_ref[...], extra.T.astype(BF)).astype(BF).reshape(shards, cap, 128)
+
+
 def send_tokens_kernel(sel_ref, tok_ref, out_ref):
     shards, cap, chans = out_ref.shape
     for c in range(0, chans, 256):
@@ -112,35 +119,6 @@
         )
 
 
-def place_kernel(cap, all_ref, shard_ref, place_ref, low_ref):
-    rows, slots = place_ref.shape
-    rank_dim = low_ref.shape[0]
-    group = 128 // cap
-    row, col = iota((rows, rows), 0), iota((rows, rows), 1)
-    before = jnp.where(row < col, 1.0, 0.0).astype(BF)
-    shard = shard_ref[0:1, 0:1]
-    low = jnp.zeros((rank_dim, rows), F32)
-    for j in range(slots // 128):
-        total = jnp.zeros((rows, 128), F32)
-        for k in range(group):
-            at = (j * group + k) * rows
-            block = all_ref[:, at : at + rows]
-            where = block[rank_dim : rank_dim + 8].astype(F32)
-            hit = jnp.where(where == shard, 1.0, 0.0)[0:1]
-            rank = dot(jnp.broadcast_to(hit, (16, rows)).astype(BF), before)[0:1]
-            target = where[1:2] * hit - (1.0 - hit)
-            sel = jnp.where(jnp.broadcast_to(target, (rows, rows)) == row.astype(F32), 1.0, 0.0)
-            sel = sel.astype(BF)
-            slot = rank + float(cap * k)
-            into = jnp.where(
-                jnp.broadcast_to(slot, (128, rows)) == iota((128, rows), 0).astype(F32), hit, 0.0
-            )
-            total = total + dot(sel, into.astype(BF), 1, 1)
-            low = low + dot(block[:rank_dim], sel, 1, 1)
-        place_ref[:, 128 * j : 128 * j + 128] = total.astype(BF)
-    low_ref[...] = low.astype(BF)
-
-
 def shifted_down(value, edge0, edge1):
     row = iota(value.shape, 0)
     one = jnp.where(row == 0, edge1, pltpu.roll(value, 1, 0))
@@ -149,16 +127,27 @@
 
 
 def post_kernel(
-    got0_ref, got1_ref, got2_ref, place_ref, low_ref, up_ref, taps_ref, offr_ref, cot_ref,
-    pre_ref, post_ref, x_ref, b_ref, ahead_ref, behind_ref,
+    got0_ref, got1_ref, got2_ref, extra_ref, up_ref, taps_ref, offr_ref, cot_ref,
+    pre_ref, post_ref, x_ref, b_ref, ahead_ref, behind_ref, place_ref, low_ref,
     ahead_edge, behind_edge, low_t_ref, mask_ref,
 ):
     parts, rows, width = pre_ref.shape
     slots = place_ref.shape[1]
+    rank_dim = low_ref.shape[0]
 
     @pl.when(pl.program_id(0) == 0)
     def _():
-        low_t_ref[...] = low_ref[...].astype(F32).T.astype(BF)
+        extra = extra_ref[...].reshape(slots, 128)
+        mark = extra[:, rank_dim : rank_dim + 2].astype(F32)
+        target = jnp.where(mark[:, 1:2] > 0.5, mark[:, 0:1], -1.0)
+        place_t = jnp.where(
+            jnp.broadcast_to(target, (slots, rows)) == iota((slots, rows), 1).astype(F32), 1.0, 0.0
+        )
+        place = place_t.T.astype(BF)
+        place_ref[...] = place
+        picked = dot(place, extra)
+        low_t_ref[...] = picked[:, :rank_dim].astype(BF)
+        low_ref[...] = picked.T[:rank_dim].astype(BF)
         for b in range(rows // 128):
             off = columns_of(offr_ref[:, 128 * b : 128 * b + 128])
             mask_ref[0, 128 * b : 128 * b + 128] = jnp.where(off >= 1.0, 1.0, 0.0)
@@ -523,16 +512,9 @@
     )
     for bit in range(3):
         low_sum = low_sum + partner(low_sum, "tp", 1 << bit)
-    where = jnp.concatenate([pos_row // rows, pos_row % rows]).astype(BF)
-    packet = jnp.concatenate([low_sum.astype(BF), where, jnp.zeros((6, rows), BF)])
-    packets = lax.all_gather(packet, "ctx", axis=1, tiled=True)
-    shard = jnp.full((1, 128), lax.axis_index("ctx"), F32)
-    place, low = whole(
-        functools.partial(place_kernel, cap),
-        [((rows, slots), BF), ((rank_dim, rows), BF)],
-        flops=1 << 30,
-        nbytes=1 << 20,
-    )(packets, shard)
+    (send_low,) = whole(
+        send_low_kernel, [((shards, cap, 128), BF)], flops=1 << 25, nbytes=1 << 19
+    )(sel, pos_row, low_sum)
     (send_tok,) = whole(
         send_tokens_kernel, [((shards, cap, chans), BF)], flops=2 * slots * rows * chans, nbytes=2 << 20
     )(sel, tokens)
@@ -560,19 +542,19 @@
         18 << 20,
         60_000_000,
     )(long_group_filter, off_row)
-    got, send_tok, off_row, fwd_bank, adj_bank, tap_rows, place, low = lax.optimization_barrier(
-        (got, send_tok, off_row, fwd_bank, adj_bank, tap_rows, place, low)
-    )
+    got, send_low, send_tok, off_row, fwd_bank, adj_bank, tap_rows = lax.optimization_barrier(
+        (got, send_low, send_tok, off_row, fwd_bank, adj_bank, tap_rows)
+    )
+    got_low = swap(send_low, "ctx")
 
     wide = 256
     steps = chans // wide
-    pre, post, x, back, ahead, behind = tiled(
+    pre, post, x, back, ahead, behind, place, low = tiled(
         post_kernel,
         steps,
         [((shards, cap, wide), lambda i, a=a: (0, 0, a * steps + i)) for a in range(parts)]
         + [
-            ((rows, slots), fixed2),
-            ((rank_dim, rows), fixed2),
+            ((shards, cap, 128), lambda i: (0, 0, 0)),
             ((parts, rank_dim, wide), at3),
             ((16, wide), at2),
             ((1, rows + 256), fixed2),
@@ -585,6 +567,8 @@
             ((rows, chans), BF, (rows, wide), at2),
             ((144, chans), BF, (144, wide), at2),
             ((144, chans), BF, (144, wide), at2),
+            ((rows, slots), BF, (rows, slots), fixed2),
+            ((rank_dim, rows), BF, (rank_dim, rows), fixed2),
         ],
         [
             pltpu.VMEM((16, wide), F32),
@@ -595,7 +579,7 @@
         1 << 30,
         8 << 20,
         60_000_000,
-    )(got, got, got, place, low, up, tap_rows, off_row, cotangent)
+    )(got, got, got, got_low, up, tap_rows, off_row, cotangent)
     send_tok, ahead, behind = lax.optimization_barrier((send_tok, ahead, behind))
     from_prev = neighbour(ahead, 1)
     from_next = neighbour(behind, -1)

time: 159 us -> 150 us (0.943)
  blocking collectives: 78.4 us -> 58.5 us
  waiting for transfers between devices: 0.81 us -> 18.4 us
  Pallas kernels: 42.8 us -> 39.1 us
    all_gather x1 -> x0, blocking collectives: 33.2 us -> none  [on_device(): packets = lax.all_gather(packet, 'ctx', axis=1, tiled=True)]
    all_to_all x2, waiting for transfers between devices: 0.54 us -> 18.1 us  [swap(): return lax.all_to_all(value, axis, split_axis=0, concat_axis=0, tiled=True)]
    all_to_all x3 -> x4, blocking collectives: 45.1 us -> 58.5 us  [swap(): return lax.all_to_all(value, axis, split_axis=0, concat_axis=0, tiled=True)]
    pallas_call x6, Pallas kernels: 7.36 us -> 3.22 us  [call(): pl.pallas_call(kernel, out_shape=tuple((jax.ShapeDtypeStruct(s, d) for s,...]
    all_to_all x2, starting transfers between devices: 16.8 us -> 15.1 us  [swap(): return lax.all_to_all(value, axis, split_axis=0, concat_axis=0, tiled=True)]
  transfers between devices with their start and end apart: 7 -> 7, of which waited for: 2 -> 3; matrix products, arithmetic and copies ran while one was open for 1% -> 1% of each run, Pallas kernels for 19% -> 18%
where the time goes in v3:
time: 150 us; the launch traced here: 149 us
  blocking collectives  58.5 us (39%)
  Pallas kernels  39.1 us (26%)
  starting transfers between devices  29.2 us (19%)
  waiting for transfers between devices  18.4 us (12%)
  local copies, waits for them, and re-layouts  1.85 us (1%)
    all_to_all x4, blocking collectives, swap(): return lax.all_to_all(value, axis, split_axis=0, concat_axis=0, tiled=True)  58.5 us
    pallas_call x3, Pallas kernels, call(): pl.pallas_call(kernel, grid=(grid,), out_shape=tuple((jax.ShapeDtypeStruc...  31.1 us
    all_to_all x2, waiting for transfers between devices, swap(): return lax.all_to_all(value, axis, split_axis=0, concat_axis=0, tiled=True)  18.1 us
    all_to_all x2, starting transfers between devices, swap(): return lax.all_to_all(value, axis, split_axis=0, concat_axis=0, tiled=True)  15.1 us
    ppermute x3, starting transfers between devices, partner(): lax.ppermute(value, axis, [(i, i ^ bit) for i in range(lax.axis_size(axis...  9.65 us
    pallas_call x1, Pallas kernels, on_device(): pl.pallas_call(send_kernel, out_shape=(jax.ShapeDtypeStruct((shards, cap,...  4.84 us
    ppermute x2, starting transfers between devices, neighbour(): return lax.ppermute(value, 'ctx', pairs)  4.45 us
    pallas_call x6, Pallas kernels, call(): pl.pallas_call(kernel, out_shape=tuple((jax.ShapeDtypeStruct(s, d) for s,...  3.22 us
  transfers between devices with their start and end apart: 7, of which 3 were waited for; matrix products, arithmetic and copies ran while one was open for 1% of the time, Pallas kernels for 18%

profile of v3, /device:TPU:1, one launch (start us, length us, event | category | flops | bytes accessed | tf_op | source)
XLA Modules:
  0.0 149.4 jit_solution(362829758789724143)
XLA Ops:
  0.6 4.8 %shard_map.145 = (bf16[32,16,3072]{2,1,0:T(8,128)(2,1)}, bf16[512,256]{1,0:T(8,128)(2,1)}) custom-call(s32[1,256]{1,0:T(1,128)} %bitcast.7, bf16[3,256,1024]{2,1,0:T(8,128)(2,1)} %bitcast.12), custom_call_target="tpu_custom_call" | custom-call | flops 1073741824 | bytes 5242880 | tf_op jit(solution)/shard_map/pallas_call | solution.py:488
  5.5 0.0 copy-start
  5.5 0.0 copy-start.4
  5.5 0.0 copy-start.6
  5.5 0.0 copy-start.9
  5.5 8.8 %all-to-all-start = ((bf16[32,16,3072]{2,1,0:T(8,128)(2,1)}), bf16[32,16,3072]{2,1,0:T(8,128)(2,1)}, u32[]{:S(2)}, u32[]{:S(2)}) async-start(bf16[32,16,3072]{2,1,0:T(8,128)(2,1)} %get-tuple-element.42), calls=%async_computation | async-start | bytes 6291456 | tf_op jit(solution)/shard_map/all_to_all | solution.py:443
  14.3 0.0 copy-start.1
  14.4 0.0 copy-done
  14.4 0.0 copy-done.4
  14.4 0.2 shard_map.146
  14.6 1.6 %collective-permute-start = (f32[16,256]{1,0:T(8,128)S(1)}, f32[16,256]{1,0:T(8,128)S(1)}, u32[]{:S(2)}, u32[]{:S(2)}) collective-permute-start(f32[16,256]{1,0:T(8,128)S(1)} %shard_map.146), channel_id=1, source_target_pairs={{0,1},{1,0},{2,3},{3,2},{4,5},{5,4},{6,7},{7,6},{8,9},{9,8},{10,11... | collective-permute-start | bytes 49160 | tf_op jit(solution)/shard_map/ppermute | solution.py:453
  16.2 0.0 copy-done.6
  16.3 0.0 copy-done.9
  16.3 0.1 select_reduce_fusion.1
  16.4 0.1 select_reduce_fusion
  16.5 0.6 subtract_convert_fusion.offr_ref
  17.1 0.6 pad_convert_fusion.taps_ref
  17.7 0.0 collective-permute-done
  17.8 3.1 %collective-permute-start.1 = (f32[16,256]{1,0:T(8,128)S(1)}, f32[16,256]{1,0:T(8,128)S(1)}, u32[]{:S(2)}, u32[]{:S(2)}) collective-permute-start(f32[16,256]{1,0:T(8,128)S(1)} %add.32), channel_id=1, source_target_pairs={{0,2},{1,3},{2,0},{3,1},{4,6},{5,7},{6,4},{7,5},{8,10},{9,11},{10,... | collective-permute-start | bytes 49160 | tf_op jit(solution)/shard_map/ppermute | solution.py:453
  20.8 8.7 %shard_map.149 = (bf16[8,2176,256]{2,1,0:T(8,128)(2,1)}, bf16[8,2176,256]{2,1,0:T(8,128)(2,1)}) custom-call(bf16[64,128]{1,0:T(8,128)(2,1)} %filt_ref.1, f32[1,512]{1,0:T(1,128)} %subtract_convert_fusion.offr_ref), custom_call_target="tpu_custom_call" | custom-call | flops 1073741824 | bytes 18874368 | tf_op jit(solution)/shard_map/pallas_call | solution.py:30
  29.5 0.0 collective-permute-done.1
  29.6 5.0 %collective-permute-start.2 = (f32[16,256]{1,0:T(8,128)S(1)}, f32[16,256]{1,0:T(8,128)S(1)}, u32[]{:S(2)}, u32[]{:S(2)}) collective-permute-start(f32[16,256]{1,0:T(8,128)S(1)} %add.33), channel_id=1, source_target_pairs={{0,4},{1,5},{2,6},{3,7},{4,0},{5,1},{6,2},{7,3},{8,12},{9,13},{10,... | collective-permute-start | bytes 49160 | tf_op jit(solution)/shard_map/ppermute | solution.py:453
  34.5 0.0 copy-done.1
  34.5 1.5 shard_map.148
  36.0 0.3 collective-permute-done.2
  36.2 0.0 copy-done.5
  36.3 0.3 shard_map.147
  36.6 17.6 %all-to-all-done.got0_ref.got1_ref.got2_ref = bf16[32,16,3072]{2,1,0:T(8,128)(2,1)} async-done(((bf16[32,16,3072]{2,1,0:T(8,128)(2,1)}), bf16[32,16,3072]{2,1,0:T(8,128)(2,1)}, u32[]{:S(2)}, u32[]{:S(2)}) %all-to-all-start) | async-done | bytes 3145760 | tf_op jit(solution)/shard_map/all_to_all | solution.py:443
  54.2 13.5 %all_to_all.30.extra_ref = bf16[32,16,128]{2,1,0:T(8,128)(2,1)} all-to-all(bf16[32,16,128]{2,1,0:T(8,128)(2,1)S(1)} %shard_map.147), channel_id=1, replica_groups=mesh['ctx'=32,'tp'=8] {'ctx'}, dimensions={0} | all-to-all | bytes 262144 | tf_op jit(solution)/shard_map/all_to_all | solution.py:443
  67.7 6.7 %shard_map.150 = (bf16[3,256,1024]{2,1,0:T(8,128)(2,1)}, bf16[3,256,1024]{2,1,0:T(8,128)(2,1)}, bf16[256,1024]{1,0:T(8,128)(2,1)}, bf16[256,1024]{1,0:T(8,128)(2...) custom-call(bf16[32,16,3072]{2,1,0:T(8,128)(2,1)} %all-to-all-done.g, ...), custom_call_target="tpu_custom_call" | custom-call | flops 1073741824 | bytes 8388608 | tf_op jit(solution)/shard_map/pallas_call | solution.py:30
  74.3 2.5 %collective-permute-start.3 = (bf16[144,1024]{1,0:T(8,128)(2,1)}, bf16[144,1024]{1,0:T(8,128)(2,1)S(1)}, u32[]{:S(2)}, u32[]{:S(2)}) collective-permute-start(bf16[144,1024]{1,0:T(8,128)(2,1)} %get-tuple-element.61), channel_id=1, source_target_pairs={{0,8},{8,16},{16,24},{24,32},{32,40},{40,48},{48,56},{56,64},{64,7... | collective-permute-start | bytes 884744 | tf_op jit(solution)/shard_map/ppermute | solution.py:449
  76.9 1.9 %collective-permute-start.4 = (bf16[144,1024]{1,0:T(8,128)(2,1)}, bf16[144,1024]{1,0:T(8,128)(2,1)S(1)}, u32[]{:S(2)}, u32[]{:S(2)}) collective-permute-start(bf16[144,1024]{1,0:T(8,128)(2,1)} %get-tuple-element.62), channel_id=1, source_target_pairs={{8,0},{16,8},{24,16},{32,24},{40,32},{48,40},{56,48},{64,56},{72,6... | collective-permute-start | bytes 884744 | tf_op jit(solution)/shard_map/ppermute | solution.py:449
  78.8 6.3 %all-to-all-start.2 = ((bf16[32,16,1024]{2,1,0:T(8,128)(2,1)}), bf16[32,16,1024]{2,1,0:T(8,128)(2,1)S(1)}, u32[]{:S(2)}, u32[]{:S(2)}) async-start(bf16[32,16,1024]{2,1,0:T(8,128)(2,1)} %shard_map.148), calls=%async_computation.2 | async-start | bytes 2097152 | tf_op jit(solution)/shard_map/all_to_all | solution.py:443
  85.1 0.0 collective-permute-done.3.prev_ref
  85.1 0.0 copy-start.7
  85.1 0.0 collective-permute-done.4.next_ref
  85.1 0.0 copy-start.8
  85.1 0.7 copy-done.7
  85.8 0.1 copy-done.8
  85.9 15.7 %shard_map.151 = (bf16[256,1024]{1,0:T(8,128)(2,1)}, f32[4,8,24,128]{3,2,1,0:T(8,128)}, f32[8,16,256]{2,1,0:T(8,128)}) custom-call(bf16[3,256,1024]{2,1,0:T(8,128)(2,1)} %get-tuple-element.54.pre_ref, bf16[3,256,1024]{2,1,0:T(8,128)(2,1)} %get-tuple-element.55.post_ref, bf16[256,1024]{1,0:T(8,128)(2,1)} %get-tuple-element.56.x_ref, ...), custom_call_target="tpu_custom_call" | custom-call | flops 10737418240 | bytes 8388608 | tf_op jit(solution)/shard_map/pallas_call | solution.py:30
  101.6 0.5 all-to-all-done.2.got_ref
  102.2 16.0 %all_to_all.31.lows_ref = f32[8,16,256]{2,1,0:T(8,128)S(1)} all-to-all(f32[8,16,256]{2,1,0:T(8,128)} %get-tuple-element.69), channel_id=1, replica_groups=mesh['ctx'=32,'tp'=8] {'tp'}, dimensions={0} | all-to-all | bytes 262144 | tf_op jit(solution)/shard_map/all_to_all | solution.py:443
  118.2 0.0 copy-done.3
  118.2 1.0 copy-done.2
  119.2 0.4 shard_map.152
  119.5 17.2 %all_to_all.32.in_ref = bf16[32,24,128]{2,1,0:T(8,128)(2,1)S(1)} all-to-all(bf16[32,24,128]{2,1,0:T(8,128)(2,1)S(1)} %shard_map.152), channel_id=1, replica_groups=mesh['ctx'=32,'tp'=8] {'ctx'}, dimensions={0} | all-to-all | bytes 393216 | tf_op jit(solution)/shard_map/all_to_all | solution.py:443
  136.7 11.8 %all_to_all.33.in_ref = bf16[32,24,128]{2,1,0:T(8,128)(2,1)S(1)} all-to-all(bf16[32,24,128]{2,1,0:T(8,128)(2,1)S(1)} %shard_map.153), channel_id=1, replica_groups=mesh['ctx'=32,'tp'=8] {'ctx'}, dimensions={0} | all-to-all | bytes 393216 | tf_op jit(solution)/shard_map/all_to_all | solution.py:443
  148.6 0.8 shard_map.154
  (9 shorter events, 0.1 us)
Async XLA Ops:
  5.5 8.9 %copy-start = (bf16[256,1024]{1,0:T(8,128)(2,1)S(1)}, bf16[256,1024]{1,0:T(8,128)(2,1)}, u32[]{:S(2)}) copy-start(bf16[256,1024]{1,0:T(8,128)(2,1)} %tok_ref.3) | copy-start | bytes 1572868
  5.5 8.9 %copy-start.4 = (bf16[16,1024]{1,0:T(8,128)(2,1)S(1)}, bf16[16,1024]{1,0:T(8,128)(2,1)}, u32[]{:S(2)}) copy-start(bf16[16,1024]{1,0:T(8,128)(2,1)} %down_ref) | copy-start | bytes 98308
  5.5 10.7 %copy-start.6 = (bf16[3,3,1024]{2,1,0:T(4,128)(2,1)S(1)}, bf16[3,3,1024]{2,1,0:T(4,128)(2,1)}, u32[]{:S(2)}) copy-start(bf16[3,3,1024]{2,1,0:T(4,128)(2,1)} %param.15) | copy-start | bytes 55300
  5.5 10.8 %copy-start.9 = (s32[64]{0:T(128)S(1)}, s32[64]{0:T(128)}, u32[]{:S(2)}) copy-start(s32[64]{0:T(128)} %param.18) | copy-start | bytes 772
  5.5 48.6 %all-to-all-start = ((bf16[32,16,3072]{2,1,0:T(8,128)(2,1)}), bf16[32,16,3072]{2,1,0:T(8,128)(2,1)}, u32[]{:S(2)}, u32[]{:S(2)}) async-start(bf16[32,16,3072]{2,1,0:T(8,128)(2,1)} %get-tuple-element.42), calls=%async_computation | async-start | bytes 6291456 | tf_op jit(solution)/shard_map/all_to_all | solution.py:443
  14.3 20.2 %copy-start.1 = (bf16[512,256]{1,0:T(8,128)(2,1)S(1)}, bf16[512,256]{1,0:T(8,128)(2,1)}, u32[]{:S(2)}) copy-start(bf16[512,256]{1,0:T(8,128)(2,1)} %get-tuple-element.44.sel_ref) | copy-start | bytes 786436
  14.6 21.7 %copy-start.5 = (s32[256]{0:T(256)S(1)}, s32[256]{0:T(256)}, u32[]{:S(2)}) copy-start(s32[256]{0:T(256)} %param.19) | copy-start | bytes 3076
  14.6 3.2 %collective-permute-start = (f32[16,256]{1,0:T(8,128)S(1)}, f32[16,256]{1,0:T(8,128)S(1)}, u32[]{:S(2)}, u32[]{:S(2)}) collective-permute-start(f32[16,256]{1,0:T(8,128)S(1)} %shard_map.146), channel_id=1, source_target_pairs={{0,1},{1,0},{2,3},{3,2},{4,5},{5,4},{6,7},{7,6},{8,9},{9,8},{10,11... | collective-permute-start | bytes 49160 | tf_op jit(solution)/shard_map/ppermute | solution.py:453
  17.8 11.8 %collective-permute-start.1 = (f32[16,256]{1,0:T(8,128)S(1)}, f32[16,256]{1,0:T(8,128)S(1)}, u32[]{:S(2)}, u32[]{:S(2)}) collective-permute-start(f32[16,256]{1,0:T(8,128)S(1)} %add.32), channel_id=1, source_target_pairs={{0,2},{1,3},{2,0},{3,1},{4,6},{5,7},{6,4},{7,5},{8,10},{9,11},{10,... | collective-permute-start | bytes 49160 | tf_op jit(solution)/shard_map/ppermute | solution.py:453
  29.6 6.7 %collective-permute-start.2 = (f32[16,256]{1,0:T(8,128)S(1)}, f32[16,256]{1,0:T(8,128)S(1)}, u32[]{:S(2)}, u32[]{:S(2)}) collective-permute-start(f32[16,256]{1,0:T(8,128)S(1)} %add.33), channel_id=1, source_target_pairs={{0,4},{1,5},{2,6},{3,7},{4,0},{5,1},{6,2},{7,3},{8,12},{9,13},{10,... | collective-permute-start | bytes 49160 | tf_op jit(solution)/shard_map/ppermute | solution.py:453
  74.3 10.8 %collective-permute-start.3 = (bf16[144,1024]{1,0:T(8,128)(2,1)}, bf16[144,1024]{1,0:T(8,128)(2,1)S(1)}, u32[]{:S(2)}, u32[]{:S(2)}) collective-permute-start(bf16[144,1024]{1,0:T(8,128)(2,1)} %get-tuple-element.61), channel_id=1, source_target_pairs={{0,8},{8,16},{16,24},{24,32},{32,40},{40,48},{48,56},{56,64},{64,7... | collective-permute-start | bytes 884744 | tf_op jit(solution)/shard_map/ppermute | solution.py:449
  76.9 8.3 %collective-permute-start.4 = (bf16[144,1024]{1,0:T(8,128)(2,1)}, bf16[144,1024]{1,0:T(8,128)(2,1)S(1)}, u32[]{:S(2)}, u32[]{:S(2)}) collective-permute-start(bf16[144,1024]{1,0:T(8,128)(2,1)} %get-tuple-element.62), channel_id=1, source_target_pairs={{8,0},{16,8},{24,16},{32,24},{40,32},{48,40},{56,48},{64,56},{72,6... | collective-permute-start | bytes 884744 | tf_op jit(solution)/shard_map/ppermute | solution.py:449
  78.8 23.4 %all-to-all-start.2 = ((bf16[32,16,1024]{2,1,0:T(8,128)(2,1)}), bf16[32,16,1024]{2,1,0:T(8,128)(2,1)S(1)}, u32[]{:S(2)}, u32[]{:S(2)}) async-start(bf16[32,16,1024]{2,1,0:T(8,128)(2,1)} %shard_map.148), calls=%async_computation.2 | async-start | bytes 2097152 | tf_op jit(solution)/shard_map/all_to_all | solution.py:443
  85.1 0.7 copy-start.7
  85.1 0.8 copy-start.8
  85.9 32.2 %copy-start.3 = (bf16[256,512]{1,0:T(8,128)(2,1)S(1)}, bf16[256,512]{1,0:T(8,128)(2,1)}, u32[]{:S(2)}) copy-start(bf16[256,512]{1,0:T(8,128)(2,1)} %get-tuple-element.71.place_ref) | copy-start | bytes 786436
  118.2 1.0 copy-start.2

commit v4 on v3

--- a/solution.py
+++ b/solution.py
@@ -67,8 +67,13 @@
     rows = pos_ref.shape[1]
     slots = sel_ref.shape[0]
     parts, shards, cap, chans = out_buf.shape
+    half = chans // 2
+    spans = [(a, c) for a in range(parts) for c in range(0, chans, half)]
     loads = [
-        pltpu.make_async_copy(frozen_ref.at[a], in_buf.at[a], in_sem.at[a]) for a in range(parts)
+        pltpu.make_async_copy(
+            frozen_ref.at[a, :, pl.ds(c, half)], in_buf.at[a, :, pl.ds(c, half)], in_sem.at[k]
+        )
+        for k, (a, c) in enumerate(spans)
     ]
     for load in loads:
         load.start()
@@ -83,14 +88,16 @@
     ).astype(BF)
     sel_ref[...] = sel
     stores = []
-    for a in range(parts):
-        loads[a].wait()
-        for c in range(0, chans, 256):
+    for k, (a, first) in enumerate(spans):
+        loads[k].wait()
+        for c in range(first, first + half, 256):
             out_buf[a, :, :, c : c + 256] = (
                 dot(sel, in_buf[a, :, c : c + 256]).astype(BF).reshape(shards, cap, 256)
             )
         store = pltpu.make_async_copy(
-            out_buf.at[a], out_ref.at[:, :, pl.ds(a * chans, chans)], out_sem.at[a]
+            out_buf.at[a, :, :, pl.ds(first, half)],
+            out_ref.at[:, :, pl.ds(a * chans + first, half)],
+            out_sem.at[k],
         )
         store.start()
         stores.append(store)
@@ -387,15 +394,12 @@
 
     @pl.when(step == pl.num_programs(0) - 1)
     def _():
-        for t in range(backlow_ref.shape[0]):
-            backlow_ref[t] = total
-
-
-def gather_kernel(lows_ref, got_ref, place_ref, sums_ref, out_ref):
+        backlow_ref[...] = total
+
+
+def gather_kernel(low_ref, rest_ref, got_ref, place_ref, sums_ref, out_ref):
     shards, cap, chans = got_ref.shape
-    total = lows_ref[0]
-    for t in range(1, lows_ref.shape[0]):
-        total = total + lows_ref[t]
+    total = low_ref[...] + rest_ref[...]
     placed = dot(total.astype(BF), place_ref[...]).astype(BF)
     down = jnp.concatenate(
         [
@@ -478,7 +482,6 @@
     taps = short_depthwise_filter.shape[0]
     groups = long_group_filter.shape[0]
     shards = lax.axis_size("ctx")
-    columns = lax.axis_size("tp")
     cap = 2 * rows // shards
     slots = shards * cap
     frozen = frozen.transpose(1, 0, 2)
@@ -496,8 +499,8 @@
         scratch_shapes=[
             pltpu.VMEM((parts, rows, chans), BF),
             pltpu.VMEM((parts, shards, cap, chans), BF),
-            pltpu.SemaphoreType.DMA((parts,)),
-            pltpu.SemaphoreType.DMA((parts,)),
+            pltpu.SemaphoreType.DMA((2 * parts,)),
+            pltpu.SemaphoreType.DMA((2 * parts,)),
         ],
         compiler_params=pltpu.CompilerParams(vmem_limit_bytes=66_000_000),
         cost_estimate=pl.CostEstimate(flops=1 << 30, bytes_accessed=5 << 20, transcendentals=0),
@@ -547,7 +550,7 @@
     )
     got_low = swap(send_low, "ctx")
 
-    wide = 256
+    wide = 512
     steps = chans // wide
     pre, post, x, back, ahead, behind, place, low = tiled(
         post_kernel,
@@ -606,7 +609,7 @@
         [
             ((rows, chans), BF, (rows, 128), at2),
             ((4, chans // 128, 24, 128), F32, (4, 1, 24, 128), lambda i: (0, i, 0, 0)),
-            ((columns, rank_dim, rows), F32, (columns, rank_dim, rows), lambda i: (0, 0, 0)),
+            ((rank_dim, rows), F32, (rank_dim, rows), fixed2),
         ],
         [
             pltpu.VMEM((blocks, 128, 256), F32),
@@ -624,10 +627,13 @@
     )(pre, post, x, back, from_prev, from_next, cotangent, tap_rows, skip_row, fwd_bank, adj_bank,
       off_row, low, up)
     got_tok, back_low_part = lax.optimization_barrier((got_tok, back_low_part))
-    back_lows = swap(back_low_part, "tp")
+    back_low = back_low_part
+    for bit in range(2):
+        back_low = back_low + partner(back_low, "tp", 1 << bit)
+    back_low_rest = partner(back_low, "tp", 4)
     (pieces,) = whole(
         gather_kernel, [((shards, 24, 128), BF)], flops=1 << 26, nbytes=2 << 20
-    )(back_lows, got_tok, place, sums)
+    )(back_low, back_low_rest, got_tok, place, sums)
     pieces = swap(pieces, "ctx")
     (pieces,) = whole(sum_kernel, [((shards, 24, 128), BF)], flops=1 << 20, nbytes=1 << 20)(pieces)
     pieces = swap(pieces, "ctx")

time: 150 us -> 150 us (level)
  blocking collectives: 58.5 us -> 43.4 us
  starting transfers between devices: 29.2 us -> 40 us
  waiting for transfers between devices: 18.4 us -> 22 us
    all_to_all x4 -> x3, blocking collectives: 58.5 us -> 43.4 us  [swap(): return lax.all_to_all(value, axis, split_axis=0, concat_axis=0, tiled=True)]
    ppermute x3 -> x6, starting transfers between devices: 9.65 us -> 20.5 us  [partner(): lax.ppermute(value, axis, [(i, i ^ bit) for i in range(lax.axis_size(axis...]
    ppermute x3 -> x6, waiting for transfers between devices: 0.28 us -> 3.84 us  [partner(): lax.ppermute(value, axis, [(i, i ^ bit) for i in range(lax.axis_size(axis...]
  transfers between devices with their start and end apart: 7 -> 10, of which waited for: 3 -> 6; matrix products, arithmetic and copies ran while one was open for 1% -> 1% of each run, Pallas kernels for 18% -> 18%
where the time goes in v4:
time: 150 us; the launch traced here: 149 us
  blocking collectives  43.4 us (29%)
  starting transfers between devices  40 us (27%)
  Pallas kernels  38.9 us (26%)
  waiting for transfers between devices  22 us (15%)
  other arithmetic  2.18 us (1%)
  local copies, waits for them, and re-layouts  1.86 us (1%)
    all_to_all x3, blocking collectives, swap(): return lax.all_to_all(value, axis, split_axis=0, concat_axis=0, tiled=True)  43.4 us
    pallas_call x3, Pallas kernels, call(): pl.pallas_call(kernel, grid=(grid,), out_shape=tuple((jax.ShapeDtypeStruc...  30.6 us
    ppermute x6, starting transfers between devices, partner(): lax.ppermute(value, axis, [(i, i ^ bit) for i in range(lax.axis_size(axis...  20.5 us
    all_to_all x2, waiting for transfers between devices, swap(): return lax.all_to_all(value, axis, split_axis=0, concat_axis=0, tiled=True)  18.2 us
    all_to_all x2, starting transfers between devices, swap(): return lax.all_to_all(value, axis, split_axis=0, concat_axis=0, tiled=True)  15.1 us
    pallas_call x1, Pallas kernels, on_device(): pl.pallas_call(send_kernel, out_shape=(jax.ShapeDtypeStruct((shards, cap,...  5.07 us
    ppermute x2, starting transfers between devices, neighbour(): return lax.ppermute(value, 'ctx', pairs)  4.44 us
    ppermute x6, waiting for transfers between devices, partner(): lax.ppermute(value, axis, [(i, i ^ bit) for i in range(lax.axis_size(axis...  3.84 us
  transfers between devices with their start and end apart: 10, of which 6 were waited for; matrix products, arithmetic and copies ran while one was open for 1% of the time, Pallas kernels for 18%

profile of v4, /device:TPU:1, one launch (start us, length us, event | category | flops | bytes accessed | tf_op | source)
XLA Modules:
  0.0 149.2 jit_solution(2076424823933333282)
XLA Ops:
  0.6 5.1 %shard_map.145 = (bf16[32,16,3072]{2,1,0:T(8,128)(2,1)}, bf16[512,256]{1,0:T(8,128)(2,1)}) custom-call(s32[1,256]{1,0:T(1,128)} %bitcast.7, bf16[3,256,1024]{2,1,0:T(8,128)(2,1)} %bitcast.12), custom_call_target="tpu_custom_call" | custom-call | flops 1073741824 | bytes 5242880 | tf_op jit(solution)/shard_map/pallas_call | solution.py:491
  5.7 0.0 copy-start
  5.7 0.0 copy-start.4
  5.7 0.0 copy-start.6
  5.7 0.0 copy-start.9
  5.8 8.7 %all-to-all-start = ((bf16[32,16,3072]{2,1,0:T(8,128)(2,1)}), bf16[32,16,3072]{2,1,0:T(8,128)(2,1)}, u32[]{:S(2)}, u32[]{:S(2)}) async-start(bf16[32,16,3072]{2,1,0:T(8,128)(2,1)} %get-tuple-element.42), calls=%async_computation | async-start | bytes 6291456 | tf_op jit(solution)/shard_map/all_to_all | solution.py:447
  14.5 0.0 copy-start.1
  14.5 0.0 copy-done
  14.5 0.0 copy-done.4
  14.5 0.2 shard_map.146
  14.8 1.7 %collective-permute-start = (f32[16,256]{1,0:T(8,128)S(1)}, f32[16,256]{1,0:T(8,128)S(1)}, u32[]{:S(2)}, u32[]{:S(2)}) collective-permute-start(f32[16,256]{1,0:T(8,128)S(1)} %shard_map.146), channel_id=1, source_target_pairs={{0,1},{1,0},{2,3},{3,2},{4,5},{5,4},{6,7},{7,6},{8,9},{9,8},{10,11... | collective-permute-start | bytes 49160 | tf_op jit(solution)/shard_map/ppermute | solution.py:457
  16.5 0.0 copy-done.6
  16.5 0.1 select_reduce_fusion.1
  16.6 0.1 select_reduce_fusion
  16.7 0.6 subtract_convert_fusion.offr_ref
  17.3 0.6 pad_convert_fusion.taps_ref
  18.0 0.0 collective-permute-done
  18.0 3.0 %collective-permute-start.1 = (f32[16,256]{1,0:T(8,128)S(1)}, f32[16,256]{1,0:T(8,128)S(1)}, u32[]{:S(2)}, u32[]{:S(2)}) collective-permute-start(f32[16,256]{1,0:T(8,128)S(1)} %add.38), channel_id=1, source_target_pairs={{0,2},{1,3},{2,0},{3,1},{4,6},{5,7},{6,4},{7,5},{8,10},{9,11},{10,... | collective-permute-start | bytes 49160 | tf_op jit(solution)/shard_map/ppermute | solution.py:457
  21.0 8.7 %shard_map.149 = (bf16[8,2176,256]{2,1,0:T(8,128)(2,1)}, bf16[8,2176,256]{2,1,0:T(8,128)(2,1)}) custom-call(bf16[64,128]{1,0:T(8,128)(2,1)} %filt_ref.1, f32[1,512]{1,0:T(1,128)} %subtract_convert_fusion.offr_ref), custom_call_target="tpu_custom_call" | custom-call | flops 1073741824 | bytes 18874368 | tf_op jit(solution)/shard_map/pallas_call | solution.py:30
  29.7 0.0 collective-permute-done.1
  29.7 5.0 %collective-permute-start.2 = (f32[16,256]{1,0:T(8,128)S(1)}, f32[16,256]{1,0:T(8,128)S(1)}, u32[]{:S(2)}, u32[]{:S(2)}) collective-permute-start(f32[16,256]{1,0:T(8,128)S(1)} %add.39), channel_id=1, source_target_pairs={{0,4},{1,5},{2,6},{3,7},{4,0},{5,1},{6,2},{7,3},{8,12},{9,13},{10,... | collective-permute-start | bytes 49160 | tf_op jit(solution)/shard_map/ppermute | solution.py:457
  34.7 1.5 %shard_map.148 = bf16[32,16,1024]{2,1,0:T(8,128)(2,1)} custom-call(bf16[512,256]{1,0:T(8,128)(2,1)S(1)} %copy-done.1, bf16[256,1024]{1,0:T(8,128)(2,1)S(1)} %copy-done), custom_call_target="tpu_custom_call" | custom-call | flops 268435456 | bytes 2097152 | tf_op jit(solution)/shard_map/pallas_call | solution.py:15
  36.2 0.2 collective-permute-done.2
  36.4 0.3 shard_map.147
  36.7 17.6 %all-to-all-done.got0_ref.got1_ref.got2_ref = bf16[32,16,3072]{2,1,0:T(8,128)(2,1)} async-done(((bf16[32,16,3072]{2,1,0:T(8,128)(2,1)}), bf16[32,16,3072]{2,1,0:T(8,128)(2,1)}, u32[]{:S(2)}, u32[]{:S(2)}) %all-to-all-start) | async-done | bytes 3145760 | tf_op jit(solution)/shard_map/all_to_all | solution.py:447
  54.3 13.5 %all_to_all.25.extra_ref = bf16[32,16,128]{2,1,0:T(8,128)(2,1)} all-to-all(bf16[32,16,128]{2,1,0:T(8,128)(2,1)S(1)} %shard_map.147), channel_id=1, replica_groups=mesh['ctx'=32,'tp'=8] {'ctx'}, dimensions={0} | all-to-all | bytes 262144 | tf_op jit(solution)/shard_map/all_to_all | solution.py:447
  67.8 6.3 %shard_map.150 = (bf16[3,256,1024]{2,1,0:T(8,128)(2,1)}, bf16[3,256,1024]{2,1,0:T(8,128)(2,1)}, bf16[256,1024]{1,0:T(8,128)(2,1)}, bf16[256,1024]{1,0:T(8,128)(2...) custom-call(bf16[32,16,3072]{2,1,0:T(8,128)(2,1)} %all-to-all-done.g, ...), custom_call_target="tpu_custom_call" | custom-call | flops 1073741824 | bytes 8388608 | tf_op jit(solution)/shard_map/pallas_call | solution.py:30
  74.1 2.5 %collective-permute-start.3 = (bf16[144,1024]{1,0:T(8,128)(2,1)}, bf16[144,1024]{1,0:T(8,128)(2,1)S(1)}, u32[]{:S(2)}, u32[]{:S(2)}) collective-permute-start(bf16[144,1024]{1,0:T(8,128)(2,1)} %get-tuple-element.61), channel_id=1, source_target_pairs={{0,8},{8,16},{16,24},{24,32},{32,40},{40,48},{48,56},{56,64},{64,7... | collective-permute-start | bytes 884744 | tf_op jit(solution)/shard_map/ppermute | solution.py:453
  76.6 1.9 %collective-permute-start.4 = (bf16[144,1024]{1,0:T(8,128)(2,1)}, bf16[144,1024]{1,0:T(8,128)(2,1)S(1)}, u32[]{:S(2)}, u32[]{:S(2)}) collective-permute-start(bf16[144,1024]{1,0:T(8,128)(2,1)} %get-tuple-element.62), channel_id=1, source_target_pairs={{8,0},{16,8},{24,16},{32,24},{40,32},{48,40},{56,48},{64,56},{72,6... | collective-permute-start | bytes 884744 | tf_op jit(solution)/shard_map/ppermute | solution.py:453
  78.6 6.3 %all-to-all-start.2 = ((bf16[32,16,1024]{2,1,0:T(8,128)(2,1)}), bf16[32,16,1024]{2,1,0:T(8,128)(2,1)S(1)}, u32[]{:S(2)}, u32[]{:S(2)}) async-start(bf16[32,16,1024]{2,1,0:T(8,128)(2,1)} %shard_map.148), calls=%async_computation.2 | async-start | bytes 2097152 | tf_op jit(solution)/shard_map/all_to_all | solution.py:447
  84.9 0.0 collective-permute-done.3.prev_ref
  84.9 0.0 collective-permute-done.4.next_ref
  84.9 0.7 copy-done.7
  85.6 0.1 copy-done.8
  85.7 15.6 %shard_map.151 = (bf16[256,1024]{1,0:T(8,128)(2,1)}, f32[4,8,24,128]{3,2,1,0:T(8,128)}, f32[16,256]{1,0:T(8,128)}) custom-call(bf16[3,256,1024]{2,1,0:T(8,128)(2,1)} %get-tuple-element.54.pre_ref, bf16[3,256,1024]{2,1,0:T(8,128)(2,1)} %get-tuple-element.55.post_ref, bf16[256,1024]{1,0:T(8,128)(2,1)} %get-tuple-element.56.x_ref, ...), custom_call_target="tpu_custom_call" | custom-call | flops 10737418240 | bytes 8388608 | tf_op jit(solution)/shard_map/pallas_call | solution.py:30
  101.4 0.6 all-to-all-done.2.got_ref
  101.9 1.7 %collective-permute-start.5 = (f32[16,256]{1,0:T(8,128)}, f32[16,256]{1,0:T(8,128)S(1)}, u32[]{:S(2)}, u32[]{:S(2)}) collective-permute-start(f32[16,256]{1,0:T(8,128)} %get-tuple-element.69), channel_id=1, source_target_pairs={{0,1},{1,0},{2,3},{3,2},{4,5},{5,4},{6,7},{7,6},{8,9},{9,8},{10,11... | collective-permute-start | bytes 49160 | tf_op jit(solution)/shard_map/ppermute | solution.py:457
  103.6 1.3 collective-permute-done.5
  105.0 0.7 add.45
  105.7 3.0 %collective-permute-start.6 = (f32[16,256]{1,0:T(8,128)S(1)}, f32[16,256]{1,0:T(8,128)S(1)}, u32[]{:S(2)}, u32[]{:S(2)}) collective-permute-start(f32[16,256]{1,0:T(8,128)S(1)} %add.45), channel_id=1, source_target_pairs={{0,2},{1,3},{2,0},{3,1},{4,6},{5,7},{6,4},{7,5},{8,10},{9,11},{10,... | collective-permute-start | bytes 49160 | tf_op jit(solution)/shard_map/ppermute | solution.py:457
  108.6 1.1 collective-permute-done.6
  109.8 6.1 %collective-permute-start.7 = (f32[16,256]{1,0:T(8,128)S(1)}, f32[16,256]{1,0:T(8,128)S(1)}, u32[]{:S(2)}, u32[]{:S(2)}) collective-permute-start(f32[16,256]{1,0:T(8,128)S(1)} %add.46.low_ref), channel_id=1, source_target_pairs={{0,4},{1,5},{2,6},{3,7},{4,0},{5,1},{6,2},{7,3},{8,12},{9,13},{10,... | collective-permute-start | bytes 49160 | tf_op jit(solution)/shard_map/ppermute | solution.py:457
  115.9 1.1 collective-permute-done.7.rest_ref
  117.0 1.0 copy-done.2
  118.0 0.4 shard_map.152
  118.4 18.1 %all_to_all.26.in_ref = bf16[32,24,128]{2,1,0:T(8,128)(2,1)S(1)} all-to-all(bf16[32,24,128]{2,1,0:T(8,128)(2,1)S(1)} %shard_map.152), channel_id=1, replica_groups=mesh['ctx'=32,'tp'=8] {'ctx'}, dimensions={0} | all-to-all | bytes 393216 | tf_op jit(solution)/shard_map/all_to_all | solution.py:447
  136.6 11.8 %all_to_all.27.in_ref = bf16[32,24,128]{2,1,0:T(8,128)(2,1)S(1)} all-to-all(bf16[32,24,128]{2,1,0:T(8,128)(2,1)S(1)} %shard_map.153), channel_id=1, replica_groups=mesh['ctx'=32,'tp'=8] {'ctx'}, dimensions={0} | all-to-all | bytes 393216 | tf_op jit(solution)/shard_map/all_to_all | solution.py:447
  148.4 0.8 shard_map.154
  (16 shorter events, 0.1 us)
Async XLA Ops:
  5.7 8.8 %copy-start = (bf16[256,1024]{1,0:T(8,128)(2,1)S(1)}, bf16[256,1024]{1,0:T(8,128)(2,1)}, u32[]{:S(2)}) copy-start(bf16[256,1024]{1,0:T(8,128)(2,1)} %tok_ref.3) | copy-start | bytes 1572868
  5.7 8.8 %copy-start.4 = (bf16[16,1024]{1,0:T(8,128)(2,1)S(1)}, bf16[16,1024]{1,0:T(8,128)(2,1)}, u32[]{:S(2)}) copy-start(bf16[16,1024]{1,0:T(8,128)(2,1)} %down_ref) | copy-start | bytes 98308
  5.7 10.7 %copy-start.6 = (bf16[3,3,1024]{2,1,0:T(4,128)(2,1)S(1)}, bf16[3,3,1024]{2,1,0:T(4,128)(2,1)}, u32[]{:S(2)}) copy-start(bf16[3,3,1024]{2,1,0:T(4,128)(2,1)} %param.15) | copy-start | bytes 55300
  5.7 10.8 %copy-start.9 = (s32[64]{0:T(128)S(1)}, s32[64]{0:T(128)}, u32[]{:S(2)}) copy-start(s32[64]{0:T(128)} %param.18) | copy-start | bytes 772
  5.8 48.6 %all-to-all-start = ((bf16[32,16,3072]{2,1,0:T(8,128)(2,1)}), bf16[32,16,3072]{2,1,0:T(8,128)(2,1)}, u32[]{:S(2)}, u32[]{:S(2)}) async-start(bf16[32,16,3072]{2,1,0:T(8,128)(2,1)} %get-tuple-element.42), calls=%async_computation | async-start | bytes 6291456 | tf_op jit(solution)/shard_map/all_to_all | solution.py:447
  14.5 20.2 %copy-start.1 = (bf16[512,256]{1,0:T(8,128)(2,1)S(1)}, bf16[512,256]{1,0:T(8,128)(2,1)}, u32[]{:S(2)}) copy-start(bf16[512,256]{1,0:T(8,128)(2,1)} %get-tuple-element.44.sel_ref) | copy-start | bytes 786436
  14.8 21.7 %copy-start.5 = (s32[256]{0:T(256)S(1)}, s32[256]{0:T(256)}, u32[]{:S(2)}) copy-start(s32[256]{0:T(256)} %param.19) | copy-start | bytes 3076
  14.8 3.2 %collective-permute-start = (f32[16,256]{1,0:T(8,128)S(1)}, f32[16,256]{1,0:T(8,128)S(1)}, u32[]{:S(2)}, u32[]{:S(2)}) collective-permute-start(f32[16,256]{1,0:T(8,128)S(1)} %shard_map.146), channel_id=1, source_target_pairs={{0,1},{1,0},{2,3},{3,2},{4,5},{5,4},{6,7},{7,6},{8,9},{9,8},{10,11... | collective-permute-start | bytes 49160 | tf_op jit(solution)/shard_map/ppermute | solution.py:457
  18.0 11.7 %collective-permute-start.1 = (f32[16,256]{1,0:T(8,128)S(1)}, f32[16,256]{1,0:T(8,128)S(1)}, u32[]{:S(2)}, u32[]{:S(2)}) collective-permute-start(f32[16,256]{1,0:T(8,128)S(1)} %add.38), channel_id=1, source_target_pairs={{0,2},{1,3},{2,0},{3,1},{4,6},{5,7},{6,4},{7,5},{8,10},{9,11},{10,... | collective-permute-start | bytes 49160 | tf_op jit(solution)/shard_map/ppermute | solution.py:457
  29.7 6.7 %collective-permute-start.2 = (f32[16,256]{1,0:T(8,128)S(1)}, f32[16,256]{1,0:T(8,128)S(1)}, u32[]{:S(2)}, u32[]{:S(2)}) collective-permute-start(f32[16,256]{1,0:T(8,128)S(1)} %add.39), channel_id=1, source_target_pairs={{0,4},{1,5},{2,6},{3,7},{4,0},{5,1},{6,2},{7,3},{8,12},{9,13},{10,... | collective-permute-start | bytes 49160 | tf_op jit(solution)/shard_map/ppermute | solution.py:457
  74.1 10.8 %collective-permute-start.3 = (bf16[144,1024]{1,0:T(8,128)(2,1)}, bf16[144,1024]{1,0:T(8,128)(2,1)S(1)}, u32[]{:S(2)}, u32[]{:S(2)}) collective-permute-start(bf16[144,1024]{1,0:T(8,128)(2,1)} %get-tuple-element.61), channel_id=1, source_target_pairs={{0,8},{8,16},{16,24},{24,32},{32,40},{40,48},{48,56},{56,64},{64,7... | collective-permute-start | bytes 884744 | tf_op jit(solution)/shard_map/ppermute | solution.py:453
  76.6 8.3 %collective-permute-start.4 = (bf16[144,1024]{1,0:T(8,128)(2,1)}, bf16[144,1024]{1,0:T(8,128)(2,1)S(1)}, u32[]{:S(2)}, u32[]{:S(2)}) collective-permute-start(bf16[144,1024]{1,0:T(8,128)(2,1)} %get-tuple-element.62), channel_id=1, source_target_pairs={{8,0},{16,8},{24,16},{32,24},{40,32},{48,40},{56,48},{64,56},{72,6... | collective-permute-start | bytes 884744 | tf_op jit(solution)/shard_map/ppermute | solution.py:453
  78.6 23.4 %all-to-all-start.2 = ((bf16[32,16,1024]{2,1,0:T(8,128)(2,1)}), bf16[32,16,1024]{2,1,0:T(8,128)(2,1)S(1)}, u32[]{:S(2)}, u32[]{:S(2)}) async-start(bf16[32,16,1024]{2,1,0:T(8,128)(2,1)} %shard_map.148), calls=%async_computation.2 | async-start | bytes 2097152 | tf_op jit(solution)/shard_map/all_to_all | solution.py:447
  84.9 0.7 copy-start.7
  84.9 0.8 copy-start.8
  85.7 31.3 %copy-start.3 = (bf16[256,512]{1,0:T(8,128)(2,1)S(1)}, bf16[256,512]{1,0:T(8,128)(2,1)}, u32[]{:S(2)}) copy-start(bf16[256,512]{1,0:T(8,128)(2,1)} %get-tuple-element.71.place_ref) | copy-start | bytes 786436
  101.9 3.0 %collective-permute-start.5 = (f32[16,256]{1,0:T(8,128)}, f32[16,256]{1,0:T(8,128)S(1)}, u32[]{:S(2)}, u32[]{:S(2)}) collective-permute-start(f32[16,256]{1,0:T(8,128)} %get-tuple-element.69), channel_id=1, source_target_pairs={{0,1},{1,0},{2,3},{3,2},{4,5},{5,4},{6,7},{7,6},{8,9},{9,8},{10,11... | collective-permute-start | bytes 49160 | tf_op jit(solution)/shard_map/ppermute | solution.py:457
  105.7 4.1 %collective-permute-start.6 = (f32[16,256]{1,0:T(8,128)S(1)}, f32[16,256]{1,0:T(8,128)S(1)}, u32[]{:S(2)}, u32[]{:S(2)}) collective-permute-start(f32[16,256]{1,0:T(8,128)S(1)} %add.45), channel_id=1, source_target_pairs={{0,2},{1,3},{2,0},{3,1},{4,6},{5,7},{6,4},{7,5},{8,10},{9,11},{10,... | collective-permute-start | bytes 49160 | tf_op jit(solution)/shard_map/ppermute | solution.py:457
  109.8 7.3 %collective-permute-start.7 = (f32[16,256]{1,0:T(8,128)S(1)}, f32[16,256]{1,0:T(8,128)S(1)}, u32[]{:S(2)}, u32[]{:S(2)}) collective-permute-start(f32[16,256]{1,0:T(8,128)S(1)} %add.46.low_ref), channel_id=1, source_target_pairs={{0,4},{1,5},{2,6},{3,7},{4,0},{5,1},{6,2},{7,3},{8,12},{9,13},{10,... | collective-permute-start | bytes 49160 | tf_op jit(solution)/shard_map/ppermute | solution.py:457
  117.0 1.0 copy-start.2

commit v5 on v3

--- a/solution.py
+++ b/solution.py
@@ -547,7 +547,7 @@
     )
     got_low = swap(send_low, "ctx")
 
-    wide = 256
+    wide = 512
     steps = chans // wide
     pre, post, x, back, ahead, behind, place, low = tiled(
         post_kernel,

time: 150 us -> 150 us (level)
  no operation moved by 1% of the time
where the time goes in v5:
time: 150 us; the launch traced here: 149 us
  blocking collectives  58.5 us (39%)
  Pallas kernels  38.8 us (26%)
  starting transfers between devices  29.2 us (19%)
  waiting for transfers between devices  18.4 us (12%)
  local copies, waits for them, and re-layouts  1.85 us (1%)
    all_to_all x4, blocking collectives, swap(): return lax.all_to_all(value, axis, split_axis=0, concat_axis=0, tiled=True)  58.5 us
    pallas_call x3, Pallas kernels, call(): pl.pallas_call(kernel, grid=(grid,), out_shape=tuple((jax.ShapeDtypeStruc...  30.7 us
    all_to_all x2, waiting for transfers between devices, swap(): return lax.all_to_all(value, axis, split_axis=0, concat_axis=0, tiled=True)  18.1 us
    all_to_all x2, starting transfers between devices, swap(): return lax.all_to_all(value, axis, split_axis=0, concat_axis=0, tiled=True)  15.1 us
    ppermute x3, starting transfers between devices, partner(): lax.ppermute(value, axis, [(i, i ^ bit) for i in range(lax.axis_size(axis...  9.65 us
    pallas_call x1, Pallas kernels, on_device(): pl.pallas_call(send_kernel, out_shape=(jax.ShapeDtypeStruct((shards, cap,...  4.84 us
    ppermute x2, starting transfers between devices, neighbour(): return lax.ppermute(value, 'ctx', pairs)  4.45 us
    pallas_call x6, Pallas kernels, call(): pl.pallas_call(kernel, out_shape=tuple((jax.ShapeDtypeStruct(s, d) for s,...  3.22 us
  transfers between devices with their start and end apart: 7, of which 3 were waited for; matrix products, arithmetic and copies ran while one was open for 1% of the time, Pallas kernels for 18%

profile of v5, /device:TPU:1, one launch (start us, length us, event | category | flops | bytes accessed | tf_op | source)
XLA Modules:
  0.0 149.0 jit_solution(15026339928415930655)
XLA Ops:
  0.6 4.8 %shard_map.145 = (bf16[32,16,3072]{2,1,0:T(8,128)(2,1)}, bf16[512,256]{1,0:T(8,128)(2,1)}) custom-call(s32[1,256]{1,0:T(1,128)} %bitcast.7, bf16[3,256,1024]{2,1,0:T(8,128)(2,1)} %bitcast.12), custom_call_target="tpu_custom_call" | custom-call | flops 1073741824 | bytes 5242880 | tf_op jit(solution)/shard_map/pallas_call | solution.py:488
  5.5 0.0 copy-start
  5.5 0.0 copy-start.4
  5.5 0.0 copy-start.6
  5.5 0.0 copy-start.9
  5.5 8.8 %all-to-all-start = ((bf16[32,16,3072]{2,1,0:T(8,128)(2,1)}), bf16[32,16,3072]{2,1,0:T(8,128)(2,1)}, u32[]{:S(2)}, u32[]{:S(2)}) async-start(bf16[32,16,3072]{2,1,0:T(8,128)(2,1)} %get-tuple-element.42), calls=%async_computation | async-start | bytes 6291456 | tf_op jit(solution)/shard_map/all_to_all | solution.py:443
  14.3 0.0 copy-start.1
  14.4 0.0 copy-done
  14.4 0.0 copy-done.4
  14.4 0.2 shard_map.146
  14.6 1.6 %collective-permute-start = (f32[16,256]{1,0:T(8,128)S(1)}, f32[16,256]{1,0:T(8,128)S(1)}, u32[]{:S(2)}, u32[]{:S(2)}) collective-permute-start(f32[16,256]{1,0:T(8,128)S(1)} %shard_map.146), channel_id=1, source_target_pairs={{0,1},{1,0},{2,3},{3,2},{4,5},{5,4},{6,7},{7,6},{8,9},{9,8},{10,11... | collective-permute-start | bytes 49160 | tf_op jit(solution)/shard_map/ppermute | solution.py:453
  16.2 0.0 copy-done.6
  16.3 0.0 copy-done.9
  16.3 0.1 select_reduce_fusion.1
  16.4 0.1 select_reduce_fusion
  16.5 0.6 subtract_convert_fusion.offr_ref
  17.1 0.6 pad_convert_fusion.taps_ref
  17.7 0.0 collective-permute-done
  17.8 3.1 %collective-permute-start.1 = (f32[16,256]{1,0:T(8,128)S(1)}, f32[16,256]{1,0:T(8,128)S(1)}, u32[]{:S(2)}, u32[]{:S(2)}) collective-permute-start(f32[16,256]{1,0:T(8,128)S(1)} %add.32), channel_id=1, source_target_pairs={{0,2},{1,3},{2,0},{3,1},{4,6},{5,7},{6,4},{7,5},{8,10},{9,11},{10,... | collective-permute-start | bytes 49160 | tf_op jit(solution)/shard_map/ppermute | solution.py:453
  20.8 8.7 %shard_map.149 = (bf16[8,2176,256]{2,1,0:T(8,128)(2,1)}, bf16[8,2176,256]{2,1,0:T(8,128)(2,1)}) custom-call(bf16[64,128]{1,0:T(8,128)(2,1)} %filt_ref.1, f32[1,512]{1,0:T(1,128)} %subtract_convert_fusion.offr_ref), custom_call_target="tpu_custom_call" | custom-call | flops 1073741824 | bytes 18874368 | tf_op jit(solution)/shard_map/pallas_call | solution.py:30
  29.5 0.0 collective-permute-done.1
  29.6 5.0 %collective-permute-start.2 = (f32[16,256]{1,0:T(8,128)S(1)}, f32[16,256]{1,0:T(8,128)S(1)}, u32[]{:S(2)}, u32[]{:S(2)}) collective-permute-start(f32[16,256]{1,0:T(8,128)S(1)} %add.33), channel_id=1, source_target_pairs={{0,4},{1,5},{2,6},{3,7},{4,0},{5,1},{6,2},{7,3},{8,12},{9,13},{10,... | collective-permute-start | bytes 49160 | tf_op jit(solution)/shard_map/ppermute | solution.py:453
  34.5 0.0 copy-done.1
  34.5 1.5 shard_map.148
  36.0 0.3 collective-permute-done.2
  36.2 0.0 copy-done.5
  36.3 0.3 shard_map.147
  36.6 17.6 %all-to-all-done.got0_ref.got1_ref.got2_ref = bf16[32,16,3072]{2,1,0:T(8,128)(2,1)} async-done(((bf16[32,16,3072]{2,1,0:T(8,128)(2,1)}), bf16[32,16,3072]{2,1,0:T(8,128)(2,1)}, u32[]{:S(2)}, u32[]{:S(2)}) %all-to-all-start) | async-done | bytes 3145760 | tf_op jit(solution)/shard_map/all_to_all | solution.py:443
  54.2 13.5 %all_to_all.30.extra_ref = bf16[32,16,128]{2,1,0:T(8,128)(2,1)} all-to-all(bf16[32,16,128]{2,1,0:T(8,128)(2,1)S(1)} %shard_map.147), channel_id=1, replica_groups=mesh['ctx'=32,'tp'=8] {'ctx'}, dimensions={0} | all-to-all | bytes 262144 | tf_op jit(solution)/shard_map/all_to_all | solution.py:443
  67.7 6.3 %shard_map.150 = (bf16[3,256,1024]{2,1,0:T(8,128)(2,1)}, bf16[3,256,1024]{2,1,0:T(8,128)(2,1)}, bf16[256,1024]{1,0:T(8,128)(2,1)}, bf16[256,1024]{1,0:T(8,128)(2...) custom-call(bf16[32,16,3072]{2,1,0:T(8,128)(2,1)} %all-to-all-done.g, ...), custom_call_target="tpu_custom_call" | custom-call | flops 1073741824 | bytes 8388608 | tf_op jit(solution)/shard_map/pallas_call | solution.py:30
  74.0 2.5 %collective-permute-start.3 = (bf16[144,1024]{1,0:T(8,128)(2,1)}, bf16[144,1024]{1,0:T(8,128)(2,1)S(1)}, u32[]{:S(2)}, u32[]{:S(2)}) collective-permute-start(bf16[144,1024]{1,0:T(8,128)(2,1)} %get-tuple-element.61), channel_id=1, source_target_pairs={{0,8},{8,16},{16,24},{24,32},{32,40},{40,48},{48,56},{56,64},{64,7... | collective-permute-start | bytes 884744 | tf_op jit(solution)/shard_map/ppermute | solution.py:449
  76.5 1.9 %collective-permute-start.4 = (bf16[144,1024]{1,0:T(8,128)(2,1)}, bf16[144,1024]{1,0:T(8,128)(2,1)S(1)}, u32[]{:S(2)}, u32[]{:S(2)}) collective-permute-start(bf16[144,1024]{1,0:T(8,128)(2,1)} %get-tuple-element.62), channel_id=1, source_target_pairs={{8,0},{16,8},{24,16},{32,24},{40,32},{48,40},{56,48},{64,56},{72,6... | collective-permute-start | bytes 884744 | tf_op jit(solution)/shard_map/ppermute | solution.py:449
  78.4 6.3 %all-to-all-start.2 = ((bf16[32,16,1024]{2,1,0:T(8,128)(2,1)}), bf16[32,16,1024]{2,1,0:T(8,128)(2,1)S(1)}, u32[]{:S(2)}, u32[]{:S(2)}) async-start(bf16[32,16,1024]{2,1,0:T(8,128)(2,1)} %shard_map.148), calls=%async_computation.2 | async-start | bytes 2097152 | tf_op jit(solution)/shard_map/all_to_all | solution.py:443
  84.7 0.0 collective-permute-done.3.prev_ref
  84.7 0.0 copy-start.7
  84.8 0.0 collective-permute-done.4.next_ref
  84.8 0.0 copy-start.8
  84.8 0.7 copy-done.7
  85.5 0.1 copy-done.8
  85.6 15.7 %shard_map.151 = (bf16[256,1024]{1,0:T(8,128)(2,1)}, f32[4,8,24,128]{3,2,1,0:T(8,128)}, f32[8,16,256]{2,1,0:T(8,128)}) custom-call(bf16[3,256,1024]{2,1,0:T(8,128)(2,1)} %get-tuple-element.54.pre_ref, bf16[3,256,1024]{2,1,0:T(8,128)(2,1)} %get-tuple-element.55.post_ref, bf16[256,1024]{1,0:T(8,128)(2,1)} %get-tuple-element.56.x_ref, ...), custom_call_target="tpu_custom_call" | custom-call | flops 10737418240 | bytes 8388608 | tf_op jit(solution)/shard_map/pallas_call | solution.py:30
  101.2 0.5 all-to-all-done.2.got_ref
  101.8 16.0 %all_to_all.31.lows_ref = f32[8,16,256]{2,1,0:T(8,128)S(1)} all-to-all(f32[8,16,256]{2,1,0:T(8,128)} %get-tuple-element.69), channel_id=1, replica_groups=mesh['ctx'=32,'tp'=8] {'tp'}, dimensions={0} | all-to-all | bytes 262144 | tf_op jit(solution)/shard_map/all_to_all | solution.py:443
  117.8 0.0 copy-done.3
  117.8 1.0 copy-done.2
  118.8 0.4 shard_map.152
  119.1 17.2 %all_to_all.32.in_ref = bf16[32,24,128]{2,1,0:T(8,128)(2,1)S(1)} all-to-all(bf16[32,24,128]{2,1,0:T(8,128)(2,1)S(1)} %shard_map.152), channel_id=1, replica_groups=mesh['ctx'=32,'tp'=8] {'ctx'}, dimensions={0} | all-to-all | bytes 393216 | tf_op jit(solution)/shard_map/all_to_all | solution.py:443
  136.4 11.8 %all_to_all.33.in_ref = bf16[32,24,128]{2,1,0:T(8,128)(2,1)S(1)} all-to-all(bf16[32,24,128]{2,1,0:T(8,128)(2,1)S(1)} %shard_map.153), channel_id=1, replica_groups=mesh['ctx'=32,'tp'=8] {'ctx'}, dimensions={0} | all-to-all | bytes 393216 | tf_op jit(solution)/shard_map/all_to_all | solution.py:443
  148.2 0.8 shard_map.154
  (9 shorter events, 0.1 us)
Async XLA Ops:
  5.5 8.9 %copy-start = (bf16[256,1024]{1,0:T(8,128)(2,1)S(1)}, bf16[256,1024]{1,0:T(8,128)(2,1)}, u32[]{:S(2)}) copy-start(bf16[256,1024]{1,0:T(8,128)(2,1)} %tok_ref.3) | copy-start | bytes 1572868
  5.5 8.9 %copy-start.4 = (bf16[16,1024]{1,0:T(8,128)(2,1)S(1)}, bf16[16,1024]{1,0:T(8,128)(2,1)}, u32[]{:S(2)}) copy-start(bf16[16,1024]{1,0:T(8,128)(2,1)} %down_ref) | copy-start | bytes 98308
  5.5 10.7 %copy-start.6 = (bf16[3,3,1024]{2,1,0:T(4,128)(2,1)S(1)}, bf16[3,3,1024]{2,1,0:T(4,128)(2,1)}, u32[]{:S(2)}) copy-start(bf16[3,3,1024]{2,1,0:T(4,128)(2,1)} %param.15) | copy-start | bytes 55300
  5.5 10.8 %copy-start.9 = (s32[64]{0:T(128)S(1)}, s32[64]{0:T(128)}, u32[]{:S(2)}) copy-start(s32[64]{0:T(128)} %param.18) | copy-start | bytes 772
  5.5 48.6 %all-to-all-start = ((bf16[32,16,3072]{2,1,0:T(8,128)(2,1)}), bf16[32,16,3072]{2,1,0:T(8,128)(2,1)}, u32[]{:S(2)}, u32[]{:S(2)}) async-start(bf16[32,16,3072]{2,1,0:T(8,128)(2,1)} %get-tuple-element.42), calls=%async_computation | async-start | bytes 6291456 | tf_op jit(solution)/shard_map/all_to_all | solution.py:443
  14.3 20.2 %copy-start.1 = (bf16[512,256]{1,0:T(8,128)(2,1)S(1)}, bf16[512,256]{1,0:T(8,128)(2,1)}, u32[]{:S(2)}) copy-start(bf16[512,256]{1,0:T(8,128)(2,1)} %get-tuple-element.44.sel_ref) | copy-start | bytes 786436
  14.6 21.7 %copy-start.5 = (s32[256]{0:T(256)S(1)}, s32[256]{0:T(256)}, u32[]{:S(2)}) copy-start(s32[256]{0:T(256)} %param.19) | copy-start | bytes 3076
  14.6 3.2 %collective-permute-start = (f32[16,256]{1,0:T(8,128)S(1)}, f32[16,256]{1,0:T(8,128)S(1)}, u32[]{:S(2)}, u32[]{:S(2)}) collective-permute-start(f32[16,256]{1,0:T(8,128)S(1)} %shard_map.146), channel_id=1, source_target_pairs={{0,1},{1,0},{2,3},{3,2},{4,5},{5,4},{6,7},{7,6},{8,9},{9,8},{10,11... | collective-permute-start | bytes 49160 | tf_op jit(solution)/shard_map/ppermute | solution.py:453
  17.8 11.8 %collective-permute-start.1 = (f32[16,256]{1,0:T(8,128)S(1)}, f32[16,256]{1,0:T(8,128)S(1)}, u32[]{:S(2)}, u32[]{:S(2)}) collective-permute-start(f32[16,256]{1,0:T(8,128)S(1)} %add.32), channel_id=1, source_target_pairs={{0,2},{1,3},{2,0},{3,1},{4,6},{5,7},{6,4},{7,5},{8,10},{9,11},{10,... | collective-permute-start | bytes 49160 | tf_op jit(solution)/shard_map/ppermute | solution.py:453
  29.6 6.7 %collective-permute-start.2 = (f32[16,256]{1,0:T(8,128)S(1)}, f32[16,256]{1,0:T(8,128)S(1)}, u32[]{:S(2)}, u32[]{:S(2)}) collective-permute-start(f32[16,256]{1,0:T(8,128)S(1)} %add.33), channel_id=1, source_target_pairs={{0,4},{1,5},{2,6},{3,7},{4,0},{5,1},{6,2},{7,3},{8,12},{9,13},{10,... | collective-permute-start | bytes 49160 | tf_op jit(solution)/shard_map/ppermute | solution.py:453
  74.0 10.8 %collective-permute-start.3 = (bf16[144,1024]{1,0:T(8,128)(2,1)}, bf16[144,1024]{1,0:T(8,128)(2,1)S(1)}, u32[]{:S(2)}, u32[]{:S(2)}) collective-permute-start(bf16[144,1024]{1,0:T(8,128)(2,1)} %get-tuple-element.61), channel_id=1, source_target_pairs={{0,8},{8,16},{16,24},{24,32},{32,40},{40,48},{48,56},{56,64},{64,7... | collective-permute-start | bytes 884744 | tf_op jit(solution)/shard_map/ppermute | solution.py:449
  76.5 8.3 %collective-permute-start.4 = (bf16[144,1024]{1,0:T(8,128)(2,1)}, bf16[144,1024]{1,0:T(8,128)(2,1)S(1)}, u32[]{:S(2)}, u32[]{:S(2)}) collective-permute-start(bf16[144,1024]{1,0:T(8,128)(2,1)} %get-tuple-element.62), channel_id=1, source_target_pairs={{8,0},{16,8},{24,16},{32,24},{40,32},{48,40},{56,48},{64,56},{72,6... | collective-permute-start | bytes 884744 | tf_op jit(solution)/shard_map/ppermute | solution.py:449
  78.4 23.4 %all-to-all-start.2 = ((bf16[32,16,1024]{2,1,0:T(8,128)(2,1)}), bf16[32,16,1024]{2,1,0:T(8,128)(2,1)S(1)}, u32[]{:S(2)}, u32[]{:S(2)}) async-start(bf16[32,16,1024]{2,1,0:T(8,128)(2,1)} %shard_map.148), calls=%async_computation.2 | async-start | bytes 2097152 | tf_op jit(solution)/shard_map/all_to_all | solution.py:443
  84.7 0.7 copy-start.7
  84.8 0.8 copy-start.8
  85.6 32.2 %copy-start.3 = (bf16[256,512]{1,0:T(8,128)(2,1)S(1)}, bf16[256,512]{1,0:T(8,128)(2,1)}, u32[]{:S(2)}) copy-start(bf16[256,512]{1,0:T(8,128)(2,1)} %get-tuple-element.71.place_ref) | copy-start | bytes 786436
  117.8 1.0 copy-start.2
